TPU v7x, 512 devices: a whole 4x8x8 slice. The times are simulated.
512 devices in a mesh: gx: 16 (over y_hi, z), gy: 4 (over y_lo), gz: 8 (over x, core).
Axes of the slice: x: 4, y: 8 (y_hi: 2, y_lo: 4; y = y_hi * 4 + y_lo), z: 8, core: 2. Of those that a mesh axis runs over, the one named last changes fastest.
Arguments:
- field: float32 [4, 128, 512, 512], P(None, ('gx', 'gz'), 'gy'), may hold values from -6 to 6
- brick_order: int32 [32], replicated, may hold values from 0 to 31, each once
- start_first: float32 [128, 32], replicated, may hold values from -6 to 6
- start_second: float32 [512, 32], replicated, may hold values from -6 to 6
- start_third: float32 [512, 32], replicated, may hold values from -6 to 6
Outputs:
- core: float32 [128, 32, 32], P(('gx', 'gy'), 'gz')
Inputs may be any that keep to these rules, and one draw needn't show every extreme that they name: `brick_order`: each of 0 to 31 appears exactly once.
All inputs are finite; a program needn't handle non-finite values.
Results may differ from a plain program's by a relative error of at most 0.0003.
Values sent between devices are 32-bit elements; how exact they have to be, the bound alone decides.
No kernel may reach another device: no remote copies, remote signals or barrier semaphores. Data moves between devices by JAX's collectives and lax.ppermute only.
A program may use at most 64 MiB of HBM per device.

v0:
```python
import jax
import jax.numpy as jnp
from jax import lax
from jax.sharding import PartitionSpec as P

ITERS = 2


highest = lax.Precision.HIGHEST


def orthonormal(columns):
    inner_gram = jnp.dot(columns.T, columns, precision=highest)
    factor_low = jnp.linalg.cholesky(inner_gram)
    return jax.scipy.linalg.solve_triangular(factor_low, columns.T, lower=True).T


def subspace(gram_mat, initial):
    current = initial
    for repeat in range(ITERS):
        current = orthonormal(jnp.dot(gram_mat, current, precision=highest))
    return current


def shards(field, brick_order, start_first, start_second, start_third):
    species, rows_x, cells_y, cells_z = field.shape
    count_gx = lax.axis_size("gx")
    count_gy = lax.axis_size("gy")
    count_gz = lax.axis_size("gz")
    brick_count = brick_order.shape[0]
    brick_len = cells_z // count_gz
    small_len = cells_z // brick_count
    cut_y = cells_y // count_gx
    onehot = (brick_order[:, None] == lax.iota(jnp.int32, brick_count)[None, :]).astype(jnp.float32)
    stored = field.reshape(species, rows_x, cells_y, brick_count, small_len)
    placed = jnp.einsum("sxybc,bg->sxygc", stored, onehot, precision=highest).reshape(
        species, rows_x, cells_y, cells_z
    )
    taper = 0.5 + 1.5 * lax.iota(jnp.float32, cells_z) / (cells_z - 1)
    placed = placed * taper
    grid_block = lax.all_to_all(placed, "gz", split_axis=3, concat_axis=1, tiled=True)
    spread = lax.all_to_all(grid_block, "gx", split_axis=2, concat_axis=1, tiled=True)
    local_first = jnp.einsum("sxyz,swyz->xw", spread, spread, precision=highest)
    gram_first = lax.psum(local_first, ("gx", "gy", "gz"))
    factor_first = subspace(gram_first, start_first)
    rank_one = factor_first.shape[1]
    after_first = jnp.einsum("sxyz,xr->sryz", spread, factor_first, precision=highest)
    after_first = after_first.reshape(species * rank_one, cut_y, brick_len)
    regrouped = lax.all_to_all(after_first, ("gx", "gy"), split_axis=0, concat_axis=1, tiled=True)
    merged_rows = regrouped.shape[0]
    regrouped = regrouped.reshape(merged_rows, count_gx, count_gy, cut_y, brick_len)
    second_fibres = jnp.transpose(regrouped, (0, 2, 1, 3, 4)).reshape(
        merged_rows, count_gy * count_gx * cut_y, brick_len
    )
    local_second = jnp.einsum("myz,muz->yu", second_fibres, second_fibres, precision=highest)
    gram_second = lax.psum(local_second, ("gx", "gy", "gz"))
    factor_second = subspace(gram_second, start_second)
    after_second = jnp.einsum("myz,yq->mqz", second_fibres, factor_second, precision=highest)
    third_fibres = lax.all_to_all(after_second, "gz", split_axis=1, concat_axis=2, tiled=True)
    local_third = jnp.einsum("mqz,mqw->zw", third_fibres, third_fibres, precision=highest)
    gram_third = lax.psum(local_third, ("gx", "gy", "gz"))
    factor_third = subspace(gram_third, start_third)
    return jnp.einsum("mqz,zt->mqt", third_fibres, factor_third, precision=highest)


def solution(mesh):
    in_specs = (P(None, ("gx", "gz"), "gy", None), P(), P(), P(), P())
    out_specs = P(("gx", "gy"), "gz", None)
    return jax.shard_map(shards, mesh=mesh, in_specs=in_specs, out_specs=out_specs, check_vma=False)
```

profile of v0, /device:TPU:1, one launch (start us, length us, event | category | flops | bytes accessed | tf_op | source)
XLA Modules:
  0.0 976.1 jit_solution(7257902330931354419)
XLA Ops:
  6.6 1.6 copy.35
  10.6 24.4 %all_to_all.69 = f32[4,1,128,512]{2,0,1,3:T(4,128)S(1)} all-to-all(f32[4,1,128,512]{2,0,1,3:T(4,128)S(1)} %copy.38), channel_id=1, replica_groups=mesh['gx'=16,'gy'=4,'gz'=8] {'gz'}, dimensions={3} | all-to-all | bytes 2097152 | tf_op jit(solution)/shard_map/all_to_all | solution.py:41
  35.0 1.8 copy.40
  36.9 1.3 reshape.62
  38.2 34.4 %all_to_all.70 = f32[16,1,16384]{2,1,0:T(1,128)S(1)} all-to-all(f32[16,1,16384]{2,1,0:T(1,128)S(1)} %reshape.62), channel_id=1, replica_groups=mesh['gx'=16,'gy'=4,'gz'=8] {'gx'}, dimensions={0} | all-to-all | bytes 2097152 | tf_op jit(solution)/shard_map/all_to_all | solution.py:42
  73.1 3.1 reduce.4
  77.1 2.6 copy.42
  79.6 2.2 copy.43
  81.8 2.4 convolution_bitcast_fusion.6
  84.4 260.8 %all-reduce.4.cloned.1.call-done = f32[128,128]{1,0:T(8,128)} async-done(((f32[128,128]{1,0:T(8,128)}), f32[128,128]{1,0:T(8,128)}) %all-reduce.4.cloned.1.call-update) | async-done | bytes 65552 | tf_op jit(solution)/shard_map/psum | solution.py:44
  346.4 2.9 cholesky.104
  350.7 2.4 custom-call.12
  354.7 2.9 cholesky.115
  359.1 2.4 custom-call.13
  361.7 2.9 convolution_bitcast_fusion.3
  365.3 19.0 %all_to_all.71 = f32[64,1,1024]{2,1,0:T(1,128)S(1)} all-to-all(f32[64,1,1024]{2,1,0:T(1,128)S(1)} %reshape.64), channel_id=1, replica_groups=mesh['gx'=16,'gy'=4,'gz'=8] {'gx','gy'}, dimensions={0} | all-to-all | bytes 524288 | tf_op jit(solution)/shard_map/all_to_all | solution.py:49
  384.3 1.3 reduce.5
  385.7 2.1 convolution_bitcast_fusion.1
  387.9 264.7 %all-reduce.6.cloned.1.call-done = f32[512,512]{1,0:T(8,128)} async-done(((f32[512,512]{1,0:T(8,128)}), f32[512,512]{1,0:T(8,128)}) %all-reduce.6.cloned.1.call-update) | async-done | bytes 1048592 | tf_op jit(solution)/shard_map/psum | solution.py:56
  652.6 2.4 fusion.41
  655.2 2.9 cholesky.126
  659.6 2.4 custom-call.14
  663.7 2.9 cholesky.137
  668.1 2.4 custom-call.15
  671.3 8.3 all_to_all.72
  680.5 2.1 convolution_bitcast_fusion
  682.6 268.1 %all-reduce.8.cloned.1.call-done = f32[512,512]{1,0:T(8,128)} async-done(((f32[512,512]{1,0:T(8,128)}), f32[512,512]{1,0:T(8,128)}) %all-reduce.8.cloned.1.call-update) | async-done | bytes 1048592 | tf_op jit(solution)/shard_map/psum | solution.py:61
  950.8 2.4 fusion.45
  953.4 2.9 cholesky.148
  957.7 2.4 custom-call.16
  961.8 2.9 cholesky.159
  966.0 2.4 custom-call.17
  (84 shorter events, 22.6 us)
Async XLA Ops:
  6.5 646.0 %copy-start = (f32[512,32]{0,1:T(8,128)S(1)}, f32[512,32]{0,1:T(8,128)}, u32[]{:S(2)}) copy-start(f32[512,32]{0,1:T(8,128)} %param.13) | copy-start | bytes 196612
  6.5 1.6 copy-start.5
  6.5 338.6 %all-reduce.4.cloned.1.call-start = ((), (), s32[]{:S(2)}) async-start(), calls=%async_computation.4 | async-start | bytes 131072 | tf_op jit(solution)/shard_map/psum | solution.py:44
  79.6 265.5 %copy-start.4 = (f32[128,32]{0,1:T(8,128)S(1)}, f32[128,32]{0,1:T(8,128)}, u32[]{:S(2)}) copy-start(f32[128,32]{0,1:T(8,128)} %param.12) | copy-start | bytes 49156
  84.3 568.3 %all-reduce.6.cloned.1.call-start = ((), (), s32[]{:S(2)}) async-start(), calls=%async_computation.5 | async-start | bytes 2097152 | tf_op jit(solution)/shard_map/psum | solution.py:56
  387.8 562.9 %all-reduce.8.cloned.1.call-start = ((), (), s32[]{:S(2)}) async-start(), calls=%async_computation.6 | async-start | bytes 2097152 | tf_op jit(solution)/shard_map/psum | solution.py:61
  652.6 9.8 %copy-start.1 = (f32[512,512]{1,0:T(8,128)S(1)}, f32[512,512]{1,0:T(8,128)}, u32[]{:S(2)}) copy-start(f32[512,512]{1,0:T(8,128)} %all-reduce.6.cloned.1.call-done) | copy-start | bytes 3145732
  662.3 288.4 %copy-start.3 = (f32[512,32]{0,1:T(8,128)S(1)}, f32[512,32]{0,1:T(8,128)}, u32[]{:S(2)}) copy-start(f32[512,32]{0,1:T(8,128)} %param.14) | copy-start | bytes 196612
  950.8 9.6 copy-start.2
Sparse Core Ops, SparseCore 0:
  84.4 260.6 all-reduce.3
  387.9 264.5 all-reduce.5
  682.8 267.9 all-reduce.7
where the time goes:
time: 977 us; the launch traced here: 976 us
  waiting for transfers between devices  794 us (81%)
  blocking collectives  86 us (9%)
  other arithmetic  45.7 us (5%)
  matrix products  23.3 us (2%)
  local copies, waits for them, and re-layouts  13.7 us (1%)
  between operations  13.5 us (1%)
    psum x1, waiting for transfers between devices, shards(): gram_third = lax.psum(local_third, ('gx', 'gy', 'gz'))  268 us
    psum x1, waiting for transfers between devices, shards(): gram_second = lax.psum(local_second, ('gx', 'gy', 'gz'))  265 us
    psum x1, waiting for transfers between devices, shards(): gram_first = lax.psum(local_first, ('gx', 'gy', 'gz'))  261 us
    all_to_all x1, blocking collectives, shards(): lax.all_to_all(grid_block, 'gx', split_axis=2, concat_axis=1, tiled=True)  34.4 us
    all_to_all x1, blocking collectives, shards(): lax.all_to_all(placed, 'gz', split_axis=3, concat_axis=1, tiled=True)  24.4 us
    another operation x18, other arithmetic, orthonormal(): factor_low = jnp.linalg.cholesky(inner_gram)  21.9 us
  transfers between devices with their start and end apart: 3, of which 3 were waited for; matrix products, arithmetic and copies ran while one was open for 0% of the time, Pallas kernels for 0%

commit v1 on v0

v1 whole, which is shorter than its diff:
```python
import functools

import jax
import jax.numpy as jnp
from jax import lax
from jax.experimental import pallas as pl
from jax.experimental.pallas import tpu as pltpu
from jax.sharding import PartitionSpec as P

ITERS = 2
LANES = 128
ORDER = ("gy", "gx", "gz")

highest = lax.Precision.HIGHEST


def mm(a, b, dims):
    return lax.dot_general(a, b, (dims, ((), ())), precision=highest, preferred_element_type=jnp.float32)


def mm_nn(a, b):
    return mm(a, b, ((1,), (0,)))


def mm_nt(a, b):
    return mm(a, b, ((1,), (1,)))


def mm_tn(a, b):
    return mm(a, b, ((0,), (0,)))


def orthonormal_rows(wide):
    rank = wide.shape[0]
    inner = mm_nt(wide, wide)
    row_id = lax.broadcasted_iota(jnp.int32, (rank, rank), 0)
    col_id = lax.broadcasted_iota(jnp.int32, (rank, rank), 1)
    eye = (row_id == col_id).astype(jnp.float32)
    work = jnp.concatenate([inner, eye], axis=1)
    rows = lax.broadcasted_iota(jnp.int32, work.shape, 0)
    for k in range(rank - 1):
        factor = work[:, k : k + 1] / work[k : k + 1, k : k + 1]
        work = jnp.where(rows > k, work - factor * work[k : k + 1, :], work)
    diag = jnp.sum(work[:, :rank] * eye, axis=1, keepdims=True)
    inverse = work[:, rank:] * (1.0 / jnp.sqrt(diag))
    return mm_nn(inverse, wide)


def send_field_kernel(order_ref, field_ref, out_ref, *, brick_len):
    species, cells_y, cells_z = field_ref.shape
    lane = lax.broadcasted_iota(jnp.int32, (1, cells_z), 1)
    brick = lane // brick_len
    place = jnp.zeros((1, cells_z), jnp.int32)
    for b in range(cells_z // brick_len):
        place = jnp.where(brick == b, order_ref[b] * brick_len, place)
    grid_z = (place + lane % brick_len).astype(jnp.float32)
    taper = 0.5 + 1.5 * grid_z / (cells_z - 1)
    for s in range(species):
        for j in range(cells_z // LANES):
            cut = slice(j * LANES, (j + 1) * LANES)
            block = field_ref[s, :, cut] * taper[:, cut]
            out_ref[pl.ds(j * LANES * species + s, LANES, stride=species), :] = block.T


def fibre(ref, s, species, rows_x, parts):
    return jnp.concatenate(
        [ref[pl.ds(yq * rows_x * species + s, rows_x, stride=species), :] for yq in range(parts)], axis=1
    )


def gram_first_kernel(data_ref, out_ref, *, species, rows_x, parts):
    total = jnp.zeros(out_ref.shape, jnp.float32)
    for s in range(species):
        cut = fibre(data_ref, s, species, rows_x, parts)
        total = total + mm_nt(cut, cut)
    out_ref[...] = total


def second_kernel(gram_ref, start_ref, data_ref, merged_ref, out_ref, *, species, rows_x, parts):
    gram = gram_ref[...]
    wide = mm_tn(start_ref[...], gram)
    current = orthonormal_rows(wide)
    for repeat in range(ITERS - 1):
        current = orthonormal_rows(mm_nn(current, gram))
    rank = current.shape[0]
    for s in range(species):
        cut = fibre(data_ref, s, species, rows_x, parts)
        merged_ref[s * rank : (s + 1) * rank, :] = mm_nn(current, cut)
    merged = merged_ref[...]
    flipped = merged.T
    for j in range(parts):
        cut = slice(j * LANES, (j + 1) * LANES)
        out_ref[pl.ds(j, flipped.shape[0], stride=parts), :] = mm_nn(flipped, merged[:, cut])


def third_kernel(gram_ref, start_ref, merged_ref, out_ref, *, parts, copies):
    size = gram_ref.shape[0] // parts
    gram = jnp.concatenate([gram_ref[pl.ds(j, size, stride=parts), :] for j in range(parts)], axis=1)
    current = orthonormal_rows(mm_tn(start_ref[...], gram))
    for repeat in range(ITERS - 1):
        current = orthonormal_rows(mm_nn(current, gram))
    after = mm_nt(current, merged_ref[...])
    rank = after.shape[0]
    for i in range(copies):
        out_ref[i * rank : (i + 1) * rank, :] = after


def columns_of(ref, parts):
    size = ref.shape[0] // parts
    return jnp.concatenate([ref[pl.ds(q, size, stride=parts), :] for q in range(parts)], axis=1)


def spread(out_ref, wide):
    for i in range(out_ref.shape[0]):
        out_ref[i] = wide


def start_third_kernel(order_ref, start_ref, data_ref, out_ref, placed_ref, *, brick_len, parts):
    for b in range(start_ref.shape[0] // brick_len):
        at = pl.multiple_of(order_ref[b] * brick_len, brick_len)
        placed_ref[b * brick_len : (b + 1) * brick_len, :] = start_ref[pl.ds(at, brick_len), :]
    data = columns_of(data_ref, parts)
    spread(out_ref, mm_nt(mm_tn(placed_ref[...], data), data))


def total_of(parts_ref):
    total = parts_ref[0]
    for i in range(1, parts_ref.shape[0]):
        total = total + parts_ref[i]
    return total


def step_third_kernel(parts_ref, data_ref, out_ref, *, parts):
    current = orthonormal_rows(total_of(parts_ref))
    data = columns_of(data_ref, parts)
    spread(out_ref, mm_nt(mm_nn(current, data), data))


def core_kernel(at_ref, parts_ref, data_ref, out_ref, rows_ref, *, parts):
    current = orthonormal_rows(total_of(parts_ref))
    size = data_ref.shape[0] // parts
    count = out_ref.shape[0]
    for q in range(parts):
        data = data_ref[pl.ds(q, size, stride=parts), :]
        rows_ref[...] = mm_nn(current, data).T
        out_ref[:, q, :] = rows_ref[pl.ds(at_ref[0] * count, count), :]


def call(kernel, out_shape, *args, scratch=(), scalars=0):
    vmem = pl.BlockSpec(memory_space=pltpu.VMEM)
    smem = pl.BlockSpec(memory_space=pltpu.SMEM)
    return pl.pallas_call(
        kernel,
        out_shape=out_shape,
        in_specs=[smem] * scalars + [vmem] * (len(args) - scalars),
        out_specs=jax.tree.map(lambda _: vmem, out_shape),
        scratch_shapes=scratch,
    )(*args)


def f32(*shape):
    return jax.ShapeDtypeStruct(shape, jnp.float32)


def swap(pieces, axes):
    return lax.all_to_all(pieces, axes, split_axis=0, concat_axis=0, tiled=True)


def shards(field, brick_order, start_first, start_second, start_third):
    species, rows_here, cells_y, cells_z = field.shape
    count_gx = lax.axis_size("gx")
    count_gy = lax.axis_size("gy")
    count_gz = lax.axis_size("gz")
    devices = count_gx * count_gy * count_gz
    rows_x, rank_one = start_first.shape
    full_y, rank_two = start_second.shape
    rank_three = start_third.shape[1]
    brick_len = cells_z // brick_order.shape[0]
    merged_rows = species * rank_one
    q_here = rank_two // count_gz

    sent = call(
        functools.partial(send_field_kernel, brick_len=brick_len),
        f32(cells_z * species, cells_y),
        brick_order,
        field.reshape(species, cells_y, cells_z),
        scalars=1,
    )
    data = swap(sent.reshape(devices, species, cells_y), ORDER).reshape(devices * species, cells_y)

    gram = call(
        functools.partial(gram_first_kernel, species=species, rows_x=rows_x, parts=count_gy),
        f32(rows_x, rows_x),
        data,
    )
    gram = jnp.sum(swap(gram.reshape(count_gz, rows_x // count_gz, rows_x), "gz"), axis=0)
    others = count_gx * count_gy
    gram = jnp.sum(swap(jnp.broadcast_to(gram, (others,) + gram.shape), ("gx", "gy")), axis=0)
    gram = swap(jnp.broadcast_to(gram, (count_gz,) + gram.shape), "gz").reshape(rows_x, rows_x)

    parts_y = full_y // LANES
    merged, gram = call(
        functools.partial(second_kernel, species=species, rows_x=rows_x, parts=parts_y),
        (f32(merged_rows, full_y), f32(full_y * parts_y, LANES)),
        gram,
        start_first,
        data,
    )
    gram = jnp.sum(swap(gram.reshape(devices, full_y * parts_y // devices, LANES), ORDER), axis=0)
    gram = swap(jnp.broadcast_to(gram, (devices,) + gram.shape), ORDER).reshape(full_y * parts_y, LANES)

    sent = call(
        functools.partial(third_kernel, parts=parts_y, copies=others),
        f32(others * rank_two, merged_rows),
        gram,
        start_second,
        merged,
    )
    data = swap(sent.reshape(devices, q_here, merged_rows), ORDER).reshape(devices * q_here, merged_rows)

    spread_shape = f32(count_gz, rank_three, cells_z)
    pieces = call(
        functools.partial(start_third_kernel, brick_len=brick_len, parts=q_here),
        spread_shape,
        brick_order,
        start_third,
        data,
        scratch=[pltpu.VMEM(start_third.shape, jnp.float32)],
        scalars=1,
    )
    for repeat in range(ITERS - 1):
        pieces = call(functools.partial(step_third_kernel, parts=q_here), spread_shape, swap(pieces, "gz"), data)
    at = (lax.axis_index("gx") * count_gy + lax.axis_index("gy")).astype(jnp.int32).reshape(1)
    return call(
        functools.partial(core_kernel, parts=q_here),
        f32(merged_rows // others, q_here, rank_three),
        at,
        swap(pieces, "gz"),
        data,
        scratch=[pltpu.VMEM((merged_rows, rank_three), jnp.float32)],
        scalars=1,
    )


def solution(mesh):
    in_specs = (P(None, ("gx", "gz"), "gy", None), P(), P(), P(), P())
    out_specs = P(("gx", "gy"), "gz", None)
    return jax.shard_map(shards, mesh=mesh, in_specs=in_specs, out_specs=out_specs, check_vma=False)
```

time: 977 us -> 305 us (0.31)
  waiting for transfers between devices: 794 us -> 76.9 us
  blocking collectives: 86 us -> 144 us
  other arithmetic: 45.7 us -> 0.63 us
  Pallas kernels: 0 us -> 42.9 us
  starting transfers between devices: 0.09 us -> 31.3 us
  matrix products: 23.3 us -> 0 us
  between operations: 13.5 us -> 0.07 us
    psum x3 -> x0, waiting for transfers between devices: 794 us -> none  [the longest x1 268 us: shards(): gram_third = lax.psum(local_third, ('gx', 'gy', 'gz'))]
    all_to_all x0 -> x4, waiting for transfers between devices: none -> 76.9 us  [swap(): return lax.all_to_all(pieces, axes, split_axis=0, concat_axis=0, tiled=True)]
    all_to_all x4 -> x5, blocking collectives: 86 us -> 144 us  [swap(): return lax.all_to_all(pieces, axes, split_axis=0, concat_axis=0, tiled=True)]
    pallas_call x0 -> x7, Pallas kernels: none -> 42.9 us  [call(): pl.pallas_call(kernel, out_shape=out_shape, in_specs=[smem] * scalars + [...]
    another operation x30 -> x0, other arithmetic: 40.5 us -> none  [the longest x18 21.9 us: orthonormal(): factor_low = jnp.linalg.cholesky(inner_gram)]
    all_to_all x0 -> x4, starting transfers between devices: none -> 31.3 us  [swap(): return lax.all_to_all(pieces, axes, split_axis=0, concat_axis=0, tiled=True)]
    dot_general x19 -> x0, matrix products: 21.7 us -> none  [the longest x6 8.94 us: subspace(): current = orthonormal(jnp.dot(gram_mat, current, precision=highest))]
  transfers between devices with their start and end apart: 3 -> 4, of which waited for: 3 -> 4; matrix products, arithmetic and copies ran while one was open for 0% -> 1% of each run, Pallas kernels for 0% -> 0%
where the time goes in v1:
time: 305 us; the launch traced here: 304 us
  blocking collectives  144 us (47%)
  waiting for transfers between devices  76.9 us (25%)
  Pallas kernels  42.9 us (14%)
  starting transfers between devices  31.3 us (10%)
  local copies, waits for them, and re-layouts  7.58 us (2%)
    all_to_all x5, blocking collectives, swap(): return lax.all_to_all(pieces, axes, split_axis=0, concat_axis=0, tiled=True)  144 us
    all_to_all x4, waiting for transfers between devices, swap(): return lax.all_to_all(pieces, axes, split_axis=0, concat_axis=0, tiled=True)  76.9 us
    pallas_call x7, Pallas kernels, call(): pl.pallas_call(kernel, out_shape=out_shape, in_specs=[smem] * scalars + [...  42.9 us
    all_to_all x4, starting transfers between devices, swap(): return lax.all_to_all(pieces, axes, split_axis=0, concat_axis=0, tiled=True)  31.3 us
  transfers between devices with their start and end apart: 4, of which 4 were waited for; matrix products, arithmetic and copies ran while one was open for 1% of the time, Pallas kernels for 0%

profile of v1, /device:TPU:1, one launch (start us, length us, event | category | flops | bytes accessed | tf_op | source)
XLA Modules:
  0.0 303.8 jit_solution(16162838309699789598)
XLA Ops:
  0.0 2.6 shard_map.55
  2.6 54.9 %all_to_all.45 = f32[512,4,128]{2,1,0:T(4,128)} all-to-all(f32[512,4,128]{2,1,0:T(4,128)} %bitcast.15), channel_id=1, replica_groups=mesh['gx'=16,'gy'=4,'gz'=8] {'gy','gx','gz'}, dimensions={0} | all-to-all | bytes 2097152 | tf_op jit(solution)/shard_map/all_to_all | solution.py:166
  57.5 2.9 shard_map.56
  60.4 9.4 %all_to_all.46 = f32[8,16,128]{2,1,0:T(8,128)S(1)} all-to-all(f32[8,16,128]{2,1,0:T(8,128)} %bitcast.21), channel_id=1, replica_groups=mesh['gx'=16,'gy'=4,'gz'=8] {'gz'}, dimensions={0} | all-to-all | bytes 131072 | tf_op jit(solution)/shard_map/all_to_all | solution.py:166
  69.8 22.5 %all_to_all.47 = f32[64,16,128]{2,1,0:T(8,128)S(1)} all-to-all(f32[64,16,128]{2,1,0:T(8,128)S(1)} %broadcast_in_dim.9), channel_id=1, replica_groups=mesh['gx'=16,'gy'=4,'gz'=8] {'gx','gy'}, dimensions={0} | all-to-all | bytes 1048576 | tf_op jit(solution)/shard_map/all_to_all | solution.py:166
  92.4 0.1 reduce_sum.28
  92.4 0.6 broadcast_in_dim.10
  93.1 6.8 %all-to-all-start.3 = ((f32[8,16,128]{2,1,0:T(8,128)}), f32[8,16,128]{2,1,0:T(8,128)S(1)}, u32[]{:S(2)}, u32[]{:S(2)}) async-start(f32[8,16,128]{2,1,0:T(8,128)} %broadcast_in_dim.10), calls=%async_computation.3 | async-start | bytes 131072 | tf_op jit(solution)/shard_map/all_to_all | solution.py:166
  99.9 0.7 copy.9.start_ref
  100.6 4.2 %all-to-all-done.3 = f32[8,16,128]{2,1,0:T(8,128)S(1)} async-done(((f32[8,16,128]{2,1,0:T(8,128)}), f32[8,16,128]{2,1,0:T(8,128)S(1)}, u32[]{:S(2)}, u32[]{:S(2)}) %all-to-all-start.3) | async-done | bytes 65568 | tf_op jit(solution)/shard_map/all_to_all | solution.py:166
  104.7 0.6 copy-done.3
  105.4 10.4 %shard_map.57 = (f32[128,512]{1,0:T(8,128)}, f32[2048,128]{1,0:T(8,128)}) custom-call(f32[128,128]{1,0:T(8,128)} %bitcast.20, f32[128,32]{1,0:T(8,128)} %copy.9.start_ref, f32[2048,128]{1,0:T(8,128)} %bitcast.14), custom_call_target="tpu_custom_call" | custom-call | tf_op jit(solution)/shard_map/pallas_call | solution.py:152
  115.7 42.6 %all_to_all.48 = f32[512,4,128]{2,1,0:T(4,128)S(1)} all-to-all(f32[512,4,128]{2,1,0:T(4,128)} %bitcast.19), channel_id=1, replica_groups=mesh['gx'=16,'gy'=4,'gz'=8] {'gy','gx','gz'}, dimensions={0} | all-to-all | bytes 2097152 | tf_op jit(solution)/shard_map/all_to_all | solution.py:166
  158.4 0.5 reduce_sum.29
  158.9 1.1 broadcast_in_dim.11
  160.0 10.1 %all-to-all-start.5 = ((f32[512,4,128]{2,1,0:T(4,128)}), f32[512,4,128]{2,1,0:T(4,128)S(1)}, u32[]{:S(2)}, u32[]{:S(2)}) async-start(f32[512,4,128]{2,1,0:T(4,128)} %broadcast_in_dim.11), calls=%async_computation.5 | async-start | bytes 2097152 | tf_op jit(solution)/shard_map/all_to_all | solution.py:166
  170.1 0.8 copy.10.start_ref
  171.0 31.6 %all-to-all-done.5 = f32[512,4,128]{2,1,0:T(4,128)S(1)} async-done(((f32[512,4,128]{2,1,0:T(4,128)}), f32[512,4,128]{2,1,0:T(4,128)S(1)}, u32[]{:S(2)}, u32[]{:S(2)}) %all-to-all-start.5) | async-done | bytes 1048608 | tf_op jit(solution)/shard_map/all_to_all | solution.py:166
  202.6 1.0 copy-done.1
  203.6 10.5 %shard_map.58 = f32[2048,128]{1,0:T(8,128)} custom-call(f32[2048,128]{1,0:T(8,128)} %bitcast.16, f32[512,32]{1,0:T(8,128)} %copy.10.start_ref, f32[128,512]{1,0:T(8,128)} %get-tuple-element.8.merged_ref), custom_call_target="tpu_custom_call" | custom-call | tf_op jit(solution)/shard_map/pallas_call | solution.py:152
  214.1 9.9 %all-to-all-start.6 = ((f32[512,4,128]{2,1,0:T(4,128)}), f32[512,4,128]{2,1,0:T(4,128)S(1)}, u32[]{:S(2)}, u32[]{:S(2)}) async-start(f32[512,4,128]{2,1,0:T(4,128)} %bitcast.17), calls=%async_computation.6 | async-start | bytes 2097152 | tf_op jit(solution)/shard_map/all_to_all | solution.py:166
  224.0 0.0 copy-done.5
  224.0 0.8 copy.11.start_ref
  224.8 31.6 %all-to-all-done.6 = f32[512,4,128]{2,1,0:T(4,128)S(1)} async-done(((f32[512,4,128]{2,1,0:T(4,128)}), f32[512,4,128]{2,1,0:T(4,128)S(1)}, u32[]{:S(2)}, u32[]{:S(2)}) %all-to-all-start.6) | async-done | bytes 1048608 | tf_op jit(solution)/shard_map/all_to_all | solution.py:166
  256.5 1.0 copy-done
  257.4 3.9 %shard_map.59 = f32[8,32,512]{2,1,0:T(8,128)} custom-call(s32[32]{0:T(128)} %order_ref.3, f32[512,32]{1,0:T(8,128)} %copy.11.start_ref, f32[2048,128]{1,0:T(8,128)} %bitcast.10), custom_call_target="tpu_custom_call" | custom-call | tf_op jit(solution)/shard_map/pallas_call | solution.py:152
  261.3 15.0 %all_to_all.49.parts_ref = f32[8,32,512]{2,1,0:T(8,128)} all-to-all(f32[8,32,512]{2,1,0:T(8,128)} %shard_map.59), channel_id=1, replica_groups=mesh['gx'=16,'gy'=4,'gz'=8] {'gz'}, dimensions={0} | all-to-all | bytes 1048576 | tf_op jit(solution)/shard_map/all_to_all | solution.py:166
  276.4 6.9 %shard_map.60 = f32[8,32,512]{2,1,0:T(8,128)} custom-call(f32[8,32,512]{2,1,0:T(8,128)} %all_to_all.49.parts_ref, f32[2048,128]{1,0:T(8,128)} %bitcast.11), custom_call_target="tpu_custom_call" | custom-call | tf_op jit(solution)/shard_map/pallas_call | solution.py:152
  283.3 4.4 %all-to-all-start.8 = ((f32[8,32,512]{2,1,0:T(8,128)}), f32[8,32,512]{2,1,0:T(8,128)S(1)}, u32[]{:S(2)}, u32[]{:S(2)}) async-start(f32[8,32,512]{2,1,0:T(8,128)} %shard_map.60), calls=%async_computation.8 | async-start | bytes 1048576 | tf_op jit(solution)/shard_map/all_to_all | solution.py:166
  287.7 9.5 %all-to-all-done.8.parts_ref = f32[8,32,512]{2,1,0:T(8,128)S(1)} async-done(((f32[8,32,512]{2,1,0:T(8,128)}), f32[8,32,512]{2,1,0:T(8,128)S(1)}, u32[]{:S(2)}, u32[]{:S(2)}) %all-to-all-start.8) | async-done | bytes 524320 | tf_op jit(solution)/shard_map/all_to_all | solution.py:166
  297.2 0.8 copy-done.2
  298.1 5.7 %shard_map.61 = f32[2,4,32]{2,1,0:T(4,128)} custom-call(s32[1]{0:T(128)} %bitcast.at_ref, f32[8,32,512]{2,1,0:T(8,128)} %copy-done.2, f32[2048,128]{1,0:T(8,128)} %bitcast.12), custom_call_target="tpu_custom_call" | custom-call | tf_op jit(solution)/shard_map/pallas_call | solution.py:152
  (11 shorter events, 0.1 us)
Async XLA Ops:
  93.1 6.8 %copy-start.6 = (f32[128,32]{0,1:T(8,128)S(1)}, f32[128,32]{0,1:T(8,128)}, u32[]{:S(2)}) copy-start(f32[128,32]{0,1:T(8,128)} %param.7) | copy-start | bytes 49156
  93.1 11.7 %all-to-all-start.3 = ((f32[8,16,128]{2,1,0:T(8,128)}), f32[8,16,128]{2,1,0:T(8,128)S(1)}, u32[]{:S(2)}, u32[]{:S(2)}) async-start(f32[8,16,128]{2,1,0:T(8,128)} %broadcast_in_dim.10), calls=%async_computation.3 | async-start | bytes 131072 | tf_op jit(solution)/shard_map/all_to_all | solution.py:166
  104.7 0.6 copy-start.3
  160.0 10.1 %copy-start.4 = (f32[512,32]{0,1:T(8,128)S(1)}, f32[512,32]{0,1:T(8,128)}, u32[]{:S(2)}) copy-start(f32[512,32]{0,1:T(8,128)} %param.8) | copy-start | bytes 196612
  160.0 42.6 %all-to-all-start.5 = ((f32[512,4,128]{2,1,0:T(4,128)}), f32[512,4,128]{2,1,0:T(4,128)S(1)}, u32[]{:S(2)}, u32[]{:S(2)}) async-start(f32[512,4,128]{2,1,0:T(4,128)} %broadcast_in_dim.11), calls=%async_computation.5 | async-start | bytes 2097152 | tf_op jit(solution)/shard_map/all_to_all | solution.py:166
  202.6 1.0 copy-start.1
  214.1 9.9 %copy-start.5 = (f32[512,32]{0,1:T(8,128)S(1)}, f32[512,32]{0,1:T(8,128)}, u32[]{:S(2)}) copy-start(f32[512,32]{0,1:T(8,128)} %param.9) | copy-start | bytes 196612
  214.1 42.4 %all-to-all-start.6 = ((f32[512,4,128]{2,1,0:T(4,128)}), f32[512,4,128]{2,1,0:T(4,128)S(1)}, u32[]{:S(2)}, u32[]{:S(2)}) async-start(f32[512,4,128]{2,1,0:T(4,128)} %bitcast.17), calls=%async_computation.6 | async-start | bytes 2097152 | tf_op jit(solution)/shard_map/all_to_all | solution.py:166
  256.5 1.0 copy-start
  283.3 13.9 %all-to-all-start.8 = ((f32[8,32,512]{2,1,0:T(8,128)}), f32[8,32,512]{2,1,0:T(8,128)S(1)}, u32[]{:S(2)}, u32[]{:S(2)}) async-start(f32[8,32,512]{2,1,0:T(8,128)} %shard_map.60), calls=%async_computation.8 | async-start | bytes 1048576 | tf_op jit(solution)/shard_map/all_to_all | solution.py:166
  297.2 0.8 copy-start.2

commit v2 on v1

v2 whole, which is shorter than its diff:
```python
import functools

import jax
import jax.numpy as jnp
from jax import lax
from jax.experimental import pallas as pl
from jax.experimental.pallas import tpu as pltpu
from jax.sharding import Mesh, PartitionSpec as P

ITERS = 2
LANES = 128
PANEL = 8
FINE = ("gu", "gv", "gh", "gl", "gw", "gc")
CHIPS = ("gh", "gl", "gu", "gv", "gw")
ORDER = CHIPS + ("gc",)
NEAR = ("gl", "gw")
ACROSS = ("gv", "gc")
ALONG = ("gu", "gh", "gl", "gw")

highest = lax.Precision.HIGHEST
NN = ((1,), (0,))
NT = ((1,), (1,))
TN = ((0,), (0,))


def mm(a, b, dims):
    return lax.dot_general(a, b, (dims, ((), ())), precision=highest, preferred_element_type=jnp.float32)


def halves(x):
    high = x.astype(jnp.bfloat16)
    return high, (x - high.astype(jnp.float32)).astype(jnp.bfloat16)


def mm3(a, b, dims):
    def dot(x, y):
        return lax.dot_general(x, y, (dims, ((), ())), preferred_element_type=jnp.float32)

    return dot(a[0], b[0]) + (dot(a[0], b[1]) + dot(a[1], b[0]))


def orthonormal_rows(wide):
    rank = wide.shape[0]
    inner = mm(wide, wide, NT)
    shape = (rank, rank)
    row_id = lax.broadcasted_iota(jnp.int32, shape, 0)
    inverse = (row_id == lax.broadcasted_iota(jnp.int32, shape, 1)).astype(jnp.float32)
    pivots = jnp.ones(shape, jnp.float32)
    for start in range(0, rank, PANEL):
        columns = [jnp.broadcast_to(inner[:, start + j : start + j + 1], shape) for j in range(PANEL)]
        for j in range(PANEL):
            k = start + j
            pivot = jnp.broadcast_to(columns[j][k : k + 1, :], shape)
            pivots = jnp.where(row_id == k, pivot, pivots)
            if k == rank - 1:
                break
            factor = jnp.where(row_id > k, columns[j] * (1.0 / pivot), 0.0)
            for i in range(j + 1, PANEL):
                columns[i] = columns[i] - factor * columns[i][k : k + 1, :]
            if start + PANEL < rank:
                inner = inner - factor * inner[k : k + 1, :]
            inverse = inverse - factor * inverse[k : k + 1, :]
    return mm(inverse * (1.0 / jnp.sqrt(pivots)), wide, NN)


def send_field_kernel(order_ref, field_ref, out_ref, *, brick_len):
    species, cells_y, cells_z = field_ref.shape
    lane = lax.broadcasted_iota(jnp.int32, (1, cells_z), 1)
    brick = lane // brick_len
    place = jnp.zeros((1, cells_z), jnp.int32)
    for b in range(cells_z // brick_len):
        place = jnp.where(brick == b, order_ref[b] * brick_len, place)
    grid_z = (place + lane % brick_len).astype(jnp.float32)
    taper = 0.5 + 1.5 * grid_z / (cells_z - 1)
    for s in range(species):
        for j in range(cells_z // LANES):
            cut = slice(j * LANES, (j + 1) * LANES)
            block = field_ref[s, :, cut] * taper[:, cut]
            out_ref[pl.ds(j * LANES * species + s, LANES, stride=species), :] = block.T


def fibre(ref, s, species, rows_x, parts):
    return jnp.concatenate(
        [ref[pl.ds(yq * rows_x * species + s, rows_x, stride=species), :] for yq in range(parts)], axis=1
    )


def gram_first_kernel(data_ref, out_ref, *, species, rows_x, parts):
    total = jnp.zeros(out_ref.shape, jnp.float32)
    for s in range(species):
        cut = halves(fibre(data_ref, s, species, rows_x, parts))
        total = total + mm3(cut, cut, NT)
    out_ref[...] = total


def second_kernel(gram_ref, start_ref, data_ref, merged_ref, out_ref, rows_ref, *, species, rows_x, parts):
    gram = gram_ref[...]
    current = start_ref[...]
    for repeat in range(ITERS):
        current = orthonormal_rows(mm(current, gram, NN))
    rank = current.shape[0]
    rows_ref[...] = current
    current = halves(jnp.concatenate([rows_ref[pl.ds(i, rank // 4, stride=4), :] for i in range(4)], axis=0))
    half = rank // 2
    for s in range(species):
        product = mm3(current, halves(fibre(data_ref, s, species, rows_x, parts)), NN)
        merged_ref[s * half : (s + 1) * half, :] = product[:half]
        merged_ref[(species + s) * half : (species + s + 1) * half, :] = product[half:]
    merged = merged_ref[...]
    flipped = halves(merged.T)
    merged = halves(merged)
    size = merged_ref.shape[1]
    product = mm3(flipped, merged, NN)
    for j in range(parts):
        out_ref[pl.ds(j, size, stride=parts), :] = product[:, j * LANES : (j + 1) * LANES]


def third_kernel(core_ref, own_ref, other_ref, start_ref, merged_ref, out_ref, gram_ref, rows_ref, *, parts):
    half = own_ref.shape[0]
    core = core_ref[0]
    gram_ref[pl.ds(pl.multiple_of(core * half, half), half), :] = own_ref[...]
    gram_ref[pl.ds(pl.multiple_of((1 - core) * half, half), half), :] = other_ref[...]
    size = gram_ref.shape[0] // parts
    gram = halves(jnp.concatenate([gram_ref[pl.ds(j, size, stride=parts), :] for j in range(parts)], axis=1))
    current = start_ref[...]
    for repeat in range(ITERS):
        current = orthonormal_rows(mm3(halves(current), gram, NN))
    rows_ref[...] = mm(current, merged_ref[...], NT)
    rank = rows_ref.shape[0]
    even = rows_ref[pl.ds(0, rank // 2, stride=2), :]
    odd = rows_ref[pl.ds(1, rank // 2, stride=2), :]
    low = lax.broadcasted_iota(jnp.int32, even.shape, 1) < LANES // 2
    first = jnp.where(low, even, pltpu.roll(odd, LANES // 2, 1))
    second = jnp.where(low, pltpu.roll(even, LANES // 2, 1), odd)
    per_low = out_ref.shape[2]
    for h in range(out_ref.shape[0]):
        for i in range(per_low):
            out_ref[h, 0, i] = first
            out_ref[h, 1, i] = second


def columns_of(own_ref, other_ref, parts):
    size = own_ref.shape[0] // parts
    return jnp.concatenate(
        [
            jnp.concatenate([ref[pl.ds(q, size, stride=parts), :] for q in range(parts)], axis=1)
            for ref in (own_ref, other_ref)
        ],
        axis=0,
    )


def spread(out_ref, wide):
    for i in range(out_ref.shape[0]):
        out_ref[i] = wide


def start_third_kernel(order_ref, core_ref, start_ref, own_ref, other_ref, out_ref, rows_ref, placed_ref, *, brick_len, parts):
    rows_ref[...] = start_ref[...].T
    size = rows_ref.shape[0]
    for b in range(size // brick_len):
        at = pl.multiple_of(order_ref[b] * brick_len, brick_len)
        placed_ref[b * brick_len : (b + 1) * brick_len, :] = rows_ref[pl.ds(at, brick_len), :]
    core = core_ref[0]
    start = jnp.concatenate(
        [placed_ref[pl.ds(core, size // 2, stride=2), :], placed_ref[pl.ds(1 - core, size // 2, stride=2), :]], axis=0
    )
    data = halves(columns_of(own_ref, other_ref, parts))
    inner = mm3(halves(start.T), data, NN)
    spread(out_ref, mm3(halves(inner), data, NT))


def total_of(parts_ref):
    total = parts_ref[0]
    for i in range(1, parts_ref.shape[0]):
        total = total + parts_ref[i]
    return total


def step_third_kernel(parts_ref, own_ref, other_ref, out_ref, *, parts):
    current = orthonormal_rows(total_of(parts_ref))
    data = halves(columns_of(own_ref, other_ref, parts))
    inner = mm3(halves(current), data, NN)
    spread(out_ref, mm3(halves(inner), data, NT))


def core_kernel(core_ref, at_ref, parts_ref, own_ref, other_ref, out_ref, rows_ref, *, parts):
    current = halves(orthonormal_rows(total_of(parts_ref)))
    size = own_ref.shape[0] // parts
    here = parts // 2
    for jj in range(here):
        at = core_ref[0] * here + jj
        data = jnp.concatenate([ref[pl.ds(at, size, stride=parts), :] for ref in (own_ref, other_ref)], axis=0)
        rows_ref[...] = mm3(current, halves(data), NN).T
        for e in range(2):
            for b in range(out_ref.shape[0]):
                out_ref[b, 2 * jj + e, :] = rows_ref[at_ref[0] + e * (LANES // 2) + 8 * b, :]


def call(kernel, out_shape, *args, scratch=(), scalars=0):
    vmem = pl.BlockSpec(memory_space=pltpu.VMEM)
    smem = pl.BlockSpec(memory_space=pltpu.SMEM)
    return pl.pallas_call(
        kernel,
        out_shape=out_shape,
        in_specs=[smem] * scalars + [vmem] * (len(args) - scalars),
        out_specs=jax.tree.map(lambda _: vmem, out_shape),
        scratch_shapes=[pltpu.VMEM(s, jnp.float32) for s in scratch],
    )(*args)


def f32(*shape):
    return jax.ShapeDtypeStruct(shape, jnp.float32)


def swap(pieces, axes):
    return lax.all_to_all(pieces, axes, split_axis=0, concat_axis=0, tiled=True)


def copies(piece, axes):
    return jnp.broadcast_to(piece, (lax.axis_size(axes),) + piece.shape)


def shards(field, brick_order, start_first, start_second, start_third):
    species, rows_here, cells_y, cells_z = field.shape
    rows_x, rank_one = start_first.shape
    full_y, rank_two = start_second.shape
    rank_three = start_third.shape[1]
    brick_len = cells_z // brick_order.shape[0]
    merged_rows = species * rank_one
    devices = lax.axis_size(ORDER)
    chips = lax.axis_size(CHIPS)
    parts_y = full_y // LANES
    core = lax.axis_index("gc").astype(jnp.int32).reshape(1)
    exchange = [(0, 1), (1, 0)]

    sent = call(
        functools.partial(send_field_kernel, brick_len=brick_len),
        f32(cells_z * species, cells_y),
        brick_order,
        field.reshape(species, cells_y, cells_z),
        scalars=1,
    )
    data = swap(sent.reshape(devices, species, cells_y), ORDER).reshape(devices * species, cells_y)

    gram = call(
        functools.partial(gram_first_kernel, species=species, rows_x=rows_x, parts=parts_y), f32(rows_x, rows_x), data
    )
    gram = jnp.sum(swap(gram.reshape(lax.axis_size(ACROSS), -1, rows_x), ACROSS), axis=0)
    gram = jnp.sum(swap(copies(gram, ALONG), ALONG), axis=0)
    gram = swap(copies(gram, ACROSS), ACROSS).reshape(rows_x, rows_x)

    merged, gram = call(
        functools.partial(second_kernel, species=species, rows_x=rows_x, parts=parts_y),
        (f32(merged_rows, full_y), f32(full_y * parts_y, LANES)),
        gram,
        start_first.T,
        data,
        scratch=[(rank_one, rows_x)],
    )
    gram = jnp.sum(swap(gram.reshape(2, -1, LANES), "gc"), axis=0)
    gram = jnp.sum(swap(gram.reshape(chips, -1, LANES), CHIPS), axis=0)
    own = swap(copies(gram, CHIPS), CHIPS).reshape(-1, LANES)
    other = lax.ppermute(own, "gc", exchange)

    near = lax.axis_size("gl")
    row_groups = lax.axis_size("gw") * 4
    sent = call(
        functools.partial(third_kernel, parts=parts_y),
        f32(lax.axis_size("gh"), near, lax.axis_size(("gu", "gv")), row_groups, LANES),
        core,
        own,
        other,
        start_second.T,
        merged,
        scratch=[(full_y * parts_y, LANES), (rank_two, merged_rows)],
        scalars=1,
    )
    own = swap(sent.reshape(chips, 4, LANES), CHIPS).reshape(chips * 4, LANES)
    other = lax.ppermute(own, "gc", exchange)

    spread_shape = f32(lax.axis_size(NEAR), rank_three, cells_z)
    pieces = call(
        functools.partial(start_third_kernel, brick_len=brick_len, parts=4),
        spread_shape,
        brick_order,
        core,
        start_third.T,
        own,
        other,
        scratch=[start_third.shape, start_third.shape],
        scalars=2,
    )
    for repeat in range(ITERS - 1):
        pieces = call(functools.partial(step_third_kernel, parts=4), spread_shape, swap(pieces, NEAR), own, other)
    gx = lax.axis_index(("gu", "gv"))
    at = ((gx // 4) * 16 + (gx % 4) * 2 + lax.axis_index("gh")).astype(jnp.int32).reshape(1)
    return call(
        functools.partial(core_kernel, parts=4),
        f32(2, 4, rank_three),
        core,
        at,
        swap(pieces, NEAR),
        own,
        other,
        scratch=[(merged_rows, rank_three)],
        scalars=2,
    )


def solution(mesh):
    gx, gy, gz = mesh.devices.shape
    fine = Mesh(mesh.devices.reshape(2, gx // 2, 2, gy // 2, gz // 2, 2), FINE)
    in_specs = (P(None, ("gu", "gv", "gw", "gc"), ("gh", "gl"), None), P(), P(), P(), P())
    out_specs = P(("gu", "gv", "gh", "gl"), ("gw", "gc"), None)
    return jax.shard_map(shards, mesh=fine, in_specs=in_specs, out_specs=out_specs, check_vma=False)
```

time: 305 us -> 252 us (0.83)
  waiting for transfers between devices: 76.9 us -> 10.5 us
  blocking collectives: 144 us -> 195 us
  starting transfers between devices: 31.3 us -> 12.4 us
  Pallas kernels: 42.9 us -> 27.7 us
  local copies, waits for them, and re-layouts: 7.58 us -> 2.53 us
    all_to_all x4 -> x1, waiting for transfers between devices: 76.9 us -> 7.44 us  [swap(): return lax.all_to_all(pieces, axes, split_axis=0, concat_axis=0, tiled=True)]
    all_to_all x5 -> x9, blocking collectives: 144 us -> 195 us  [swap(): return lax.all_to_all(pieces, axes, split_axis=0, concat_axis=0, tiled=True)]
    all_to_all x4 -> x1, starting transfers between devices: 31.3 us -> 4.11 us  [swap(): return lax.all_to_all(pieces, axes, split_axis=0, concat_axis=0, tiled=True)]
    pallas_call x7, Pallas kernels: 42.9 us -> 27.7 us  [call(): pl.pallas_call(kernel, out_shape=out_shape, in_specs=[smem] * scalars + [...]
    ppermute x0 -> x2, starting transfers between devices: none -> 8.28 us  [shards(): other = lax.ppermute(own, 'gc', exchange)]
    unnamed x17 -> x10, local copies, waits for them, and re-layouts: 5.82 us -> 2.44 us
  transfers between devices with their start and end apart: 4 -> 3, of which waited for: 4 -> 3; matrix products, arithmetic and copies ran while one was open for 1% -> 0% of each run, Pallas kernels for 0% -> 0%
where the time goes in v2:
time: 252 us; the launch traced here: 249 us
  blocking collectives  195 us (77%)
  Pallas kernels  27.7 us (11%)
  starting transfers between devices  12.4 us (5%)
  waiting for transfers between devices  10.5 us (4%)
  local copies, waits for them, and re-layouts  2.53 us (1%)
    all_to_all x9, blocking collectives, swap(): return lax.all_to_all(pieces, axes, split_axis=0, concat_axis=0, tiled=True)  195 us
    pallas_call x7, Pallas kernels, call(): pl.pallas_call(kernel, out_shape=out_shape, in_specs=[smem] * scalars + [...  27.7 us
    ppermute x2, starting transfers between devices, shards(): other = lax.ppermute(own, 'gc', exchange)  8.28 us
    all_to_all x1, waiting for transfers between devices, swap(): return lax.all_to_all(pieces, axes, split_axis=0, concat_axis=0, tiled=True)  7.44 us
  transfers between devices with their start and end apart: 3, of which 3 were waited for; matrix products, arithmetic and copies ran while one was open for 0% of the time, Pallas kernels for 0%

profile of v2, /device:TPU:1, one launch (start us, length us, event | category | flops | bytes accessed | tf_op | source)
XLA Modules:
  0.0 249.0 jit_solution(7620319433607918321)
XLA Ops:
  0.0 2.6 %shard_map.55 = f32[2048,128]{1,0:T(8,128)} custom-call(s32[32]{0:T(128)} %order_ref.3, f32[4,128,512]{2,1,0:T(8,128)} %bitcast.26), custom_call_target="tpu_custom_call" | custom-call | tf_op jit(solution)/shard_map/pallas_call | solution.py:203
  2.6 54.9 %all_to_all.50 = f32[512,4,128]{2,1,0:T(4,128)} all-to-all(f32[512,4,128]{2,1,0:T(4,128)} %bitcast.21), channel_id=1, replica_groups=mesh['gu'=2,'gv'=8,'gh'=2,'gl'=2,'gw'=4,'gc'=2] {'gh','gl','gu','gv','gw..., dimensions={0} | all-to-all | bytes 2097152 | tf_op jit(solution)/shard_map/all_to_all | solution.py:217
  57.5 2.4 shard_map.56
  59.9 12.9 %all_to_all.51 = f32[16,8,128]{2,1,0:T(8,128)S(1)} all-to-all(f32[16,8,128]{2,1,0:T(8,128)} %bitcast.29), channel_id=1, replica_groups=mesh['gu'=2,'gv'=8,'gh'=2,'gl'=2,'gw'=4,'gc'=2] {'gv','gc'}, dimensions={0} | all-to-all | bytes 131072 | tf_op jit(solution)/shard_map/all_to_all | solution.py:217
  72.9 13.3 %all_to_all.52 = f32[32,8,128]{2,1,0:T(8,128)S(1)} all-to-all(f32[32,8,128]{2,1,0:T(8,128)S(1)} %broadcast_in_dim.9), channel_id=1, replica_groups=mesh['gu'=2,'gv'=8,'gh'=2,'gl'=2,'gw'=4,'gc'=2] {'gu','gh','gl','gw'}, dimensions={0} | all-to-all | bytes 262144 | tf_op jit(solution)/shard_map/all_to_all | solution.py:217
  86.2 12.5 %all_to_all.53 = f32[16,8,128]{2,1,0:T(8,128)} all-to-all(f32[16,8,128]{2,1,0:T(8,128)S(1)} %broadcast_in_dim.10), channel_id=1, replica_groups=mesh['gu'=2,'gv'=8,'gh'=2,'gl'=2,'gw'=4,'gc'=2] {'gv','gc'}, dimensions={0} | all-to-all | bytes 131072 | tf_op jit(solution)/shard_map/all_to_all | solution.py:217
  98.7 5.9 %shard_map.57 = (f32[128,512]{1,0:T(8,128)}, f32[2048,128]{1,0:T(8,128)}) custom-call(f32[128,128]{1,0:T(8,128)} %bitcast.28, f32[32,128]{1,0:T(8,128)} %bitcast.32, f32[2048,128]{1,0:T(8,128)} %bitcast.16), custom_call_target="tpu_custom_call" | custom-call | tf_op jit(solution)/shard_map/pallas_call | solution.py:203
  104.5 5.5 %all_to_all.54 = f32[2,1024,128]{2,1,0:T(8,128)S(1)} all-to-all(f32[2,1024,128]{2,1,0:T(8,128)} %bitcast.27), channel_id=1, replica_groups=mesh['gu'=2,'gv'=8,'gh'=2,'gl'=2,'gw'=4,'gc'=2] {'gc'}, dimensions={0} | all-to-all | bytes 2097152 | tf_op jit(solution)/shard_map/all_to_all | solution.py:217
  110.0 0.1 reduce_sum.38
  110.1 27.5 %all_to_all.55 = f32[256,4,128]{2,1,0:T(4,128)S(1)} all-to-all(f32[256,4,128]{2,1,0:T(4,128)S(1)} %bitcast.22), channel_id=1, replica_groups=mesh['gu'=2,'gv'=8,'gh'=2,'gl'=2,'gw'=4,'gc'=2] {'gh','gl','gu','gv','gw'}, dimensions={0} | all-to-all | bytes 1048576 | tf_op jit(solution)/shard_map/all_to_all | solution.py:217
  137.6 0.3 reduce_sum.39
  137.9 0.1 broadcast_in_dim.11
  138.0 27.7 %all_to_all.56 = f32[256,4,128]{2,1,0:T(4,128)S(1)} all-to-all(f32[256,4,128]{2,1,0:T(4,128)S(1)} %broadcast_in_dim.11), channel_id=1, replica_groups=mesh['gu'=2,'gv'=8,'gh'=2,'gl'=2,'gw'=4,'gc'=2] {'gh','gl','gu','gv','gw'}, dimensions={0} | all-to-all | bytes 1048576 | tf_op jit(solution)/shard_map/all_to_all | solution.py:217
  165.7 0.0 copy-start.3
  165.7 4.5 %collective-permute-start = (f32[1024,128]{1,0:T(8,128)S(1)}, f32[1024,128]{1,0:T(8,128)S(1)}, u32[]{:S(2)}, u32[]{:S(2)}) collective-permute-start(f32[1024,128]{1,0:T(8,128)S(1)} %bitcast.23), channel_id=1, source_target_pairs={{0,1},{1,0},{2,3},{3,2},{4,5},{5,4},{6,7},{7,6},{8,9},{9,8},{10,11... | collective-permute-start | bytes 1572872 | tf_op jit(solution)/shard_map/ppermute | solution.py:264
  170.3 1.5 collective-permute-done.other_ref
  171.8 0.0 copy-start.4
  171.8 0.0 copy-done.3
  171.8 0.8 copy-done.4
  172.6 5.9 %shard_map.58 = f32[2,2,16,16,128]{4,3,2,1,0:T(8,128)} custom-call(s32[1]{0:T(128)} %bitcast.core_ref, f32[1024,128]{1,0:T(8,128)} %bitcast.24, f32[1024,128]{1,0:T(8,128)} %copy-done.4, f32[32,512]{1,0:T(8,128)} %bitcast.30, f32[128,512]{1,0:T(8,128)} %get-tuple-element.8.merged_ref), custom_call_target="tpu_custom_call" | custom-call | tf_op jit(solution)/shard_map/pallas_call | solution.py:203
  178.5 28.2 %all_to_all.57 = f32[256,4,128]{2,1,0:T(4,128)S(1)} all-to-all(f32[256,4,128]{2,1,0:T(4,128)} %bitcast.25), channel_id=1, replica_groups=mesh['gu'=2,'gv'=8,'gh'=2,'gl'=2,'gw'=4,'gc'=2] {'gh','gl','gu','gv','gw'}, dimensions={0} | all-to-all | bytes 1048576 | tf_op jit(solution)/shard_map/all_to_all | solution.py:217
  206.7 3.7 %collective-permute-start.1 = (f32[1024,128]{1,0:T(8,128)S(1)}, f32[1024,128]{1,0:T(8,128)S(1)}, u32[]{:S(2)}, u32[]{:S(2)}) collective-permute-start(f32[1024,128]{1,0:T(8,128)S(1)} %bitcast.17), channel_id=1, source_target_pairs={{0,1},{1,0},{2,3},{3,2},{4,5},{5,4},{6,7},{7,6},{8,9},{9,8},{10,11... | collective-permute-start | bytes 1572872 | tf_op jit(solution)/shard_map/ppermute | solution.py:280
  210.5 1.5 collective-permute-done.1.other_ref
  212.0 0.0 copy-done
  212.0 0.8 copy-done.1
  212.8 3.2 %shard_map.59 = f32[8,32,512]{2,1,0:T(8,128)} custom-call(s32[32]{0:T(128)} %order_ref.3, s32[1]{0:T(128)} %bitcast.core_ref, f32[32,512]{1,0:T(8,128)} %bitcast.31, f32[1024,128]{1,0:T(8,128)} %bitcast.18, f32[1024,128]{1,0:T(8,128)} %copy-done.1), custom_call_target="tpu_custom_call" | custom-call | tf_op jit(solution)/shard_map/pallas_call | solution.py:203
  215.9 13.0 %all_to_all.58.parts_ref = f32[8,32,512]{2,1,0:T(8,128)} all-to-all(f32[8,32,512]{2,1,0:T(8,128)} %shard_map.59), channel_id=1, replica_groups=mesh['gu'=2,'gv'=8,'gh'=2,'gl'=2,'gw'=4,'gc'=2] {'gl','gw'}, dimensions={0} | all-to-all | bytes 1048576 | tf_op jit(solution)/shard_map/all_to_all | solution.py:217
  228.9 4.2 %shard_map.60 = f32[8,32,512]{2,1,0:T(8,128)} custom-call(f32[8,32,512]{2,1,0:T(8,128)} %all_to_all.58.parts_ref, f32[1024,128]{1,0:T(8,128)} %bitcast.19, f32[1024,128]{1,0:T(8,128)} %copy-done.1), custom_call_target="tpu_custom_call" | custom-call | tf_op jit(solution)/shard_map/pallas_call | solution.py:203
  233.1 4.1 %all-to-all-start.9 = ((f32[8,32,512]{2,1,0:T(8,128)}), f32[8,32,512]{2,1,0:T(8,128)S(1)}, u32[]{:S(2)}, u32[]{:S(2)}) async-start(f32[8,32,512]{2,1,0:T(8,128)} %shard_map.60), calls=%async_computation.9 | async-start | bytes 1048576 | tf_op jit(solution)/shard_map/all_to_all | solution.py:217
  237.3 7.4 %all-to-all-done.9.parts_ref = f32[8,32,512]{2,1,0:T(8,128)S(1)} async-done(((f32[8,32,512]{2,1,0:T(8,128)}), f32[8,32,512]{2,1,0:T(8,128)S(1)}, u32[]{:S(2)}, u32[]{:S(2)}) %all-to-all-start.9) | async-done | bytes 524320 | tf_op jit(solution)/shard_map/all_to_all | solution.py:217
  244.7 0.8 copy-done.2
  245.5 3.5 %shard_map.61 = f32[2,4,32]{2,1,0:T(4,128)} custom-call(s32[1]{0:T(128)} %bitcast.core_ref, s32[1]{0:T(128)} %bitcast.1.at_ref, f32[8,32,512]{2,1,0:T(8,128)} %copy-done.2, f32[1024,128]{1,0:T(8,128)} %bitcast.20, f32[1024,128]{1,0:T(8,128)} %copy-done.1), custom_call_target="tpu_custom_call" | custom-call | tf_op jit(solution)/shard_map/pallas_call | solution.py:203
  (7 shorter events, 0.1 us)
Async XLA Ops:
  165.7 6.1 %copy-start.3 = (f32[256,4,128]{2,1,0:T(4,128)}, f32[256,4,128]{2,1,0:T(4,128)S(1)}, u32[]{:S(2)}) copy-start(f32[256,4,128]{2,1,0:T(4,128)S(1)} %all_to_all.56) | copy-start | bytes 1572868
  165.7 6.1 %collective-permute-start = (f32[1024,128]{1,0:T(8,128)S(1)}, f32[1024,128]{1,0:T(8,128)S(1)}, u32[]{:S(2)}, u32[]{:S(2)}) collective-permute-start(f32[1024,128]{1,0:T(8,128)S(1)} %bitcast.23), channel_id=1, source_target_pairs={{0,1},{1,0},{2,3},{3,2},{4,5},{5,4},{6,7},{7,6},{8,9},{9,8},{10,11... | collective-permute-start | bytes 1572872 | tf_op jit(solution)/shard_map/ppermute | solution.py:264
  171.8 0.8 copy-start.4
  206.7 5.3 %copy-start = (f32[256,4,128]{2,1,0:T(4,128)}, f32[256,4,128]{2,1,0:T(4,128)S(1)}, u32[]{:S(2)}) copy-start(f32[256,4,128]{2,1,0:T(4,128)S(1)} %all_to_all.57) | copy-start | bytes 1572868
  206.7 5.3 %collective-permute-start.1 = (f32[1024,128]{1,0:T(8,128)S(1)}, f32[1024,128]{1,0:T(8,128)S(1)}, u32[]{:S(2)}, u32[]{:S(2)}) collective-permute-start(f32[1024,128]{1,0:T(8,128)S(1)} %bitcast.17), channel_id=1, source_target_pairs={{0,1},{1,0},{2,3},{3,2},{4,5},{5,4},{6,7},{7,6},{8,9},{9,8},{10,11... | collective-permute-start | bytes 1572872 | tf_op jit(solution)/shard_map/ppermute | solution.py:280
  212.0 0.8 copy-start.1
  233.1 11.5 %all-to-all-start.9 = ((f32[8,32,512]{2,1,0:T(8,128)}), f32[8,32,512]{2,1,0:T(8,128)S(1)}, u32[]{:S(2)}, u32[]{:S(2)}) async-start(f32[8,32,512]{2,1,0:T(8,128)} %shard_map.60), calls=%async_computation.9 | async-start | bytes 1048576 | tf_op jit(solution)/shard_map/all_to_all | solution.py:217
  244.7 0.8 copy-start.2

commit v3 on v2

--- a/solution.py
+++ b/solution.py
@@ -10,12 +10,14 @@
 ITERS = 2
 LANES = 128
 PANEL = 8
+VMEM_BYTES = 20 << 20
 FINE = ("gu", "gv", "gh", "gl", "gw", "gc")
 CHIPS = ("gh", "gl", "gu", "gv", "gw")
 ORDER = CHIPS + ("gc",)
 NEAR = ("gl", "gw")
 ACROSS = ("gv", "gc")
 ALONG = ("gu", "gh", "gl", "gw")
+FAR = ("gh", "gu", "gv")
 
 highest = lax.Precision.HIGHEST
 NN = ((1,), (0,))
@@ -63,8 +65,11 @@
     return mm(inverse * (1.0 / jnp.sqrt(pivots)), wide, NN)
 
 
-def send_field_kernel(order_ref, field_ref, out_ref, *, brick_len):
-    species, cells_y, cells_z = field_ref.shape
+def send_field_kernel(order_ref, field_hbm, out_ref, field_ref, sems, *, brick_len):
+    species, cells_y, cells_z = field_hbm.shape
+    loads = [pltpu.make_async_copy(field_hbm.at[s], field_ref.at[s], sems.at[s]) for s in range(species)]
+    for load in loads:
+        load.start()
     lane = lax.broadcasted_iota(jnp.int32, (1, cells_z), 1)
     brick = lane // brick_len
     place = jnp.zeros((1, cells_z), jnp.int32)
@@ -73,6 +78,7 @@
     grid_z = (place + lane % brick_len).astype(jnp.float32)
     taper = 0.5 + 1.5 * grid_z / (cells_z - 1)
     for s in range(species):
+        loads[s].wait()
         for j in range(cells_z // LANES):
             cut = slice(j * LANES, (j + 1) * LANES)
             block = field_ref[s, :, cut] * taper[:, cut]
@@ -93,7 +99,9 @@
     out_ref[...] = total
 
 
-def second_kernel(gram_ref, start_ref, data_ref, merged_ref, out_ref, rows_ref, *, species, rows_x, parts):
+def second_kernel(
+    core_ref, gram_ref, start_ref, data_ref, merged_ref, kept_ref, sent_ref, rows_ref, flipped_ref, *, species, rows_x, parts
+):
     gram = gram_ref[...]
     current = start_ref[...]
     for repeat in range(ITERS):
@@ -107,23 +115,23 @@
         merged_ref[s * half : (s + 1) * half, :] = product[:half]
         merged_ref[(species + s) * half : (species + s + 1) * half, :] = product[half:]
     merged = merged_ref[...]
-    flipped = halves(merged.T)
+    flipped_ref[...] = merged.T
     merged = halves(merged)
-    size = merged_ref.shape[1]
-    product = mm3(flipped, merged, NN)
-    for j in range(parts):
-        out_ref[pl.ds(j, size, stride=parts), :] = product[:, j * LANES : (j + 1) * LANES]
-
-
-def third_kernel(core_ref, own_ref, other_ref, start_ref, merged_ref, out_ref, gram_ref, rows_ref, *, parts):
-    half = own_ref.shape[0]
-    core = core_ref[0]
-    gram_ref[pl.ds(pl.multiple_of(core * half, half), half), :] = own_ref[...]
-    gram_ref[pl.ds(pl.multiple_of((1 - core) * half, half), half), :] = other_ref[...]
-    size = gram_ref.shape[0] // parts
-    gram = halves(jnp.concatenate([gram_ref[pl.ds(j, size, stride=parts), :] for j in range(parts)], axis=1))
+    size = merged_ref.shape[1] // 2
+    for out_ref, at in ((sent_ref, 1 - core_ref[0]), (kept_ref, core_ref[0])):
+        rows = flipped_ref[pl.ds(pl.multiple_of(at * size, size), size), :]
+        product = mm3(halves(rows), merged, NN)
+        for j in range(parts):
+            out_ref[pl.ds(j, size, stride=parts), :] = product[:, j * LANES : (j + 1) * LANES]
+
+
+def third_kernel(core_ref, own_ref, other_ref, start_ref, merged_ref, out_ref, rows_ref, *, parts):
+    gram = halves(columns_of(own_ref, other_ref, parts))
     current = start_ref[...]
+    size = current.shape[1] // 2
     for repeat in range(ITERS):
+        swapped = jnp.concatenate([current[:, size:], current[:, :size]], axis=1)
+        current = jnp.where(core_ref[0] == 0, current, swapped)
         current = orthonormal_rows(mm3(halves(current), gram, NN))
     rows_ref[...] = mm(current, merged_ref[...], NT)
     rank = rows_ref.shape[0]
@@ -155,7 +163,7 @@
         out_ref[i] = wide
 
 
-def start_third_kernel(order_ref, core_ref, start_ref, own_ref, other_ref, out_ref, rows_ref, placed_ref, *, brick_len, parts):
+def start_third_kernel(order_ref, core_ref, start_ref, own_ref, other_ref, out_ref, high_ref, low_ref, rows_ref, placed_ref, *, brick_len, parts):
     rows_ref[...] = start_ref[...].T
     size = rows_ref.shape[0]
     for b in range(size // brick_len):
@@ -166,6 +174,7 @@
         [placed_ref[pl.ds(core, size // 2, stride=2), :], placed_ref[pl.ds(1 - core, size // 2, stride=2), :]], axis=0
     )
     data = halves(columns_of(own_ref, other_ref, parts))
+    high_ref[...], low_ref[...] = data
     inner = mm3(halves(start.T), data, NN)
     spread(out_ref, mm3(halves(inner), data, NT))
 
@@ -177,40 +186,41 @@
     return total
 
 
-def step_third_kernel(parts_ref, own_ref, other_ref, out_ref, *, parts):
+def step_third_kernel(parts_ref, high_ref, low_ref, out_ref):
     current = orthonormal_rows(total_of(parts_ref))
-    data = halves(columns_of(own_ref, other_ref, parts))
+    data = high_ref[...], low_ref[...]
     inner = mm3(halves(current), data, NN)
     spread(out_ref, mm3(halves(inner), data, NT))
 
 
-def core_kernel(core_ref, at_ref, parts_ref, own_ref, other_ref, out_ref, rows_ref, *, parts):
+def core_kernel(core_ref, at_ref, parts_ref, high_ref, low_ref, out_ref, rows_ref, *, parts):
     current = halves(orthonormal_rows(total_of(parts_ref)))
-    size = own_ref.shape[0] // parts
     here = parts // 2
     for jj in range(here):
-        at = core_ref[0] * here + jj
-        data = jnp.concatenate([ref[pl.ds(at, size, stride=parts), :] for ref in (own_ref, other_ref)], axis=0)
-        rows_ref[...] = mm3(current, halves(data), NN).T
+        cut = pl.ds(pl.multiple_of((core_ref[0] * here + jj) * LANES, LANES), LANES)
+        rows_ref[...] = mm3(current, (high_ref[:, cut], low_ref[:, cut]), NN).T
         for e in range(2):
             for b in range(out_ref.shape[0]):
                 out_ref[b, 2 * jj + e, :] = rows_ref[at_ref[0] + e * (LANES // 2) + 8 * b, :]
 
 
-def call(kernel, out_shape, *args, scratch=(), scalars=0):
+def call(kernel, out_shape, *args, scratch=(), scalars=0, in_hbm=0):
     vmem = pl.BlockSpec(memory_space=pltpu.VMEM)
     smem = pl.BlockSpec(memory_space=pltpu.SMEM)
+    hbm = pl.BlockSpec(memory_space=pltpu.HBM)
+    lead = scalars + in_hbm
     return pl.pallas_call(
         kernel,
         out_shape=out_shape,
-        in_specs=[smem] * scalars + [vmem] * (len(args) - scalars),
+        in_specs=[smem] * scalars + [hbm] * in_hbm + [vmem] * (len(args) - lead),
         out_specs=jax.tree.map(lambda _: vmem, out_shape),
-        scratch_shapes=[pltpu.VMEM(s, jnp.float32) for s in scratch],
-    )(*args)
-
-
-def f32(*shape):
-    return jax.ShapeDtypeStruct(shape, jnp.float32)
+        compiler_params=pltpu.CompilerParams(vmem_limit_bytes=None if in_hbm else VMEM_BYTES),
+        scratch_shapes=[pltpu.VMEM(s, jnp.float32) if isinstance(s, tuple) else s for s in scratch],
+    )(*args[:lead], *[pltpu.with_memory_space_constraint(a, pltpu.VMEM) for a in args[lead:]])
+
+
+def vm(*shape, dtype=jnp.float32):
+    return pltpu.VMEM(shape, dtype)
 
 
 def swap(pieces, axes):
@@ -236,53 +246,60 @@
 
     sent = call(
         functools.partial(send_field_kernel, brick_len=brick_len),
-        f32(cells_z * species, cells_y),
+        vm(cells_z * species, cells_y),
         brick_order,
         field.reshape(species, cells_y, cells_z),
+        scratch=[(species, cells_y, cells_z), pltpu.SemaphoreType.DMA((species,))],
         scalars=1,
+        in_hbm=1,
     )
     data = swap(sent.reshape(devices, species, cells_y), ORDER).reshape(devices * species, cells_y)
 
     gram = call(
-        functools.partial(gram_first_kernel, species=species, rows_x=rows_x, parts=parts_y), f32(rows_x, rows_x), data
+        functools.partial(gram_first_kernel, species=species, rows_x=rows_x, parts=parts_y), vm(rows_x, rows_x), data
     )
     gram = jnp.sum(swap(gram.reshape(lax.axis_size(ACROSS), -1, rows_x), ACROSS), axis=0)
     gram = jnp.sum(swap(copies(gram, ALONG), ALONG), axis=0)
     gram = swap(copies(gram, ACROSS), ACROSS).reshape(rows_x, rows_x)
 
-    merged, gram = call(
+    merged, kept, sent = call(
         functools.partial(second_kernel, species=species, rows_x=rows_x, parts=parts_y),
-        (f32(merged_rows, full_y), f32(full_y * parts_y, LANES)),
+        (vm(merged_rows, full_y),) + (vm(full_y * parts_y // 2, LANES),) * 2,
+        core,
         gram,
         start_first.T,
         data,
-        scratch=[(rank_one, rows_x)],
-    )
-    gram = jnp.sum(swap(gram.reshape(2, -1, LANES), "gc"), axis=0)
-    gram = jnp.sum(swap(gram.reshape(chips, -1, LANES), CHIPS), axis=0)
-    own = swap(copies(gram, CHIPS), CHIPS).reshape(-1, LANES)
+        scratch=[(rank_one, rows_x), (full_y, merged_rows)],
+        scalars=1,
+    )
+    gram = kept + lax.ppermute(sent, "gc", exchange)
+    gram = jnp.sum(swap(gram.reshape(lax.axis_size(NEAR), -1, LANES), NEAR), axis=0)
+    gram = jnp.sum(swap(gram.reshape(lax.axis_size(FAR), -1, LANES), FAR), axis=0)
+    gram = swap(copies(gram, FAR), FAR).reshape(-1, LANES)
+    own = swap(copies(gram, NEAR), NEAR).reshape(-1, LANES)
     other = lax.ppermute(own, "gc", exchange)
 
     near = lax.axis_size("gl")
     row_groups = lax.axis_size("gw") * 4
     sent = call(
         functools.partial(third_kernel, parts=parts_y),
-        f32(lax.axis_size("gh"), near, lax.axis_size(("gu", "gv")), row_groups, LANES),
+        vm(lax.axis_size("gh"), near, lax.axis_size(("gu", "gv")), row_groups, LANES),
         core,
         own,
         other,
         start_second.T,
         merged,
-        scratch=[(full_y * parts_y, LANES), (rank_two, merged_rows)],
+        scratch=[(rank_two, merged_rows)],
         scalars=1,
     )
     own = swap(sent.reshape(chips, 4, LANES), CHIPS).reshape(chips * 4, LANES)
     other = lax.ppermute(own, "gc", exchange)
 
-    spread_shape = f32(lax.axis_size(NEAR), rank_three, cells_z)
-    pieces = call(
+    spread_shape = vm(lax.axis_size(NEAR), rank_three, cells_z)
+    cut = vm(cells_z, 4 * LANES, dtype=jnp.bfloat16)
+    pieces, high, low = call(
         functools.partial(start_third_kernel, brick_len=brick_len, parts=4),
-        spread_shape,
+        (spread_shape, cut, cut),
         brick_order,
         core,
         start_third.T,
@@ -292,17 +309,17 @@
         scalars=2,
     )
     for repeat in range(ITERS - 1):
-        pieces = call(functools.partial(step_third_kernel, parts=4), spread_shape, swap(pieces, NEAR), own, other)
+        pieces = call(step_third_kernel, spread_shape, swap(pieces, NEAR), high, low)
     gx = lax.axis_index(("gu", "gv"))
     at = ((gx // 4) * 16 + (gx % 4) * 2 + lax.axis_index("gh")).astype(jnp.int32).reshape(1)
     return call(
         functools.partial(core_kernel, parts=4),
-        f32(2, 4, rank_three),
+        jax.ShapeDtypeStruct((2, 4, rank_three), jnp.float32),
         core,
         at,
         swap(pieces, NEAR),
-        own,
-        other,
+        high,
+        low,
         scratch=[(merged_rows, rank_three)],
         scalars=2,
     )

time: 252 us -> 233 us (0.925)
  blocking collectives: 195 us -> 171 us
  Pallas kernels: 27.7 us -> 16.8 us
  waiting for transfers between devices: 10.5 us -> 19.8 us
  starting transfers between devices: 12.4 us -> 21.1 us
    all_to_all x9, blocking collectives: 195 us -> 171 us  [swap(): return lax.all_to_all(pieces, axes, split_axis=0, concat_axis=0, tiled=True)]
    pallas_call x7, Pallas kernels: 27.7 us -> 16.8 us  [call(): pl.pallas_call(kernel, out_shape=out_shape, in_specs=[smem] * scalars + [...]
    all_to_all x1 -> x2, waiting for transfers between devices: 7.44 us -> 15 us  [swap(): return lax.all_to_all(pieces, axes, split_axis=0, concat_axis=0, tiled=True)]
    all_to_all x1 -> x2, starting transfers between devices: 4.11 us -> 8.56 us  [swap(): return lax.all_to_all(pieces, axes, split_axis=0, concat_axis=0, tiled=True)]
  transfers between devices with their start and end apart: 3 -> 5, of which waited for: 3 -> 5; matrix products, arithmetic and copies ran while one was open for 0% -> 0% of each run, Pallas kernels for 0% -> 0%
where the time goes in v3:
time: 233 us; the launch traced here: 230 us
  blocking collectives  171 us (73%)
  starting transfers between devices  21.1 us (9%)
  waiting for transfers between devices  19.8 us (8%)
  Pallas kernels  16.8 us (7%)
    all_to_all x9, blocking collectives, swap(): return lax.all_to_all(pieces, axes, split_axis=0, concat_axis=0, tiled=True)  171 us
    pallas_call x7, Pallas kernels, call(): pl.pallas_call(kernel, out_shape=out_shape, in_specs=[smem] * scalars + [...  16.8 us
    all_to_all x2, waiting for transfers between devices, swap(): return lax.all_to_all(pieces, axes, split_axis=0, concat_axis=0, tiled=True)  15 us
    ppermute x2, starting transfers between devices, shards(): other = lax.ppermute(own, 'gc', exchange)  10.4 us
    all_to_all x2, starting transfers between devices, swap(): return lax.all_to_all(pieces, axes, split_axis=0, concat_axis=0, tiled=True)  8.56 us
  transfers between devices with their start and end apart: 5, of which 5 were waited for; matrix products, arithmetic and copies ran while one was open for 0% of the time, Pallas kernels for 0%

profile of v3, /device:TPU:1, one launch (start us, length us, event | category | flops | bytes accessed | tf_op | source)
XLA Modules:
  0.0 230.0 jit_solution(6195738381257772003)
XLA Ops:
  0.0 2.2 shard_map.55
  2.2 54.3 %all_to_all.55 = f32[512,4,128]{2,1,0:T(4,128)S(1)} all-to-all(f32[512,4,128]{2,1,0:T(4,128)S(1)} %bitcast.18), channel_id=1, replica_groups=mesh['gu'=2,'gv'=8,'gh'=2,'gl'=2,'gw'=4,'gc'=2] {'gh','gl','gu','gv','gw..., dimensions={0} | all-to-all | bytes 2097152 | tf_op jit(solution)/shard_map/all_to_all | solution.py:227
  56.5 0.6 shard_map.56
  57.1 13.0 %all_to_all.56 = f32[16,8,128]{2,1,0:T(8,128)S(1)} all-to-all(f32[16,8,128]{2,1,0:T(8,128)S(1)} %bitcast.25), channel_id=1, replica_groups=mesh['gu'=2,'gv'=8,'gh'=2,'gl'=2,'gw'=4,'gc'=2] {'gv','gc'}, dimensions={0} | all-to-all | bytes 131072 | tf_op jit(solution)/shard_map/all_to_all | solution.py:227
  70.1 13.3 %all_to_all.57 = f32[32,8,128]{2,1,0:T(8,128)S(1)} all-to-all(f32[32,8,128]{2,1,0:T(8,128)S(1)} %broadcast_in_dim.12), channel_id=1, replica_groups=mesh['gu'=2,'gv'=8,'gh'=2,'gl'=2,'gw'=4,'gc'=2] {'gu','gh','gl','gw'}, dimensions={0} | all-to-all | bytes 262144 | tf_op jit(solution)/shard_map/all_to_all | solution.py:227
  83.4 0.6 broadcast_in_dim.13
  84.0 5.0 %all-to-all-start.3 = ((f32[16,8,128]{2,1,0:T(8,128)}), f32[16,8,128]{2,1,0:T(8,128)S(1)}, u32[]{:S(2)}, u32[]{:S(2)}) async-start(f32[16,8,128]{2,1,0:T(8,128)} %broadcast_in_dim.13), calls=%async_computation.3 | async-start | bytes 131072 | tf_op jit(solution)/shard_map/all_to_all | solution.py:227
  89.0 7.8 %all-to-all-done.3 = f32[16,8,128]{2,1,0:T(8,128)S(1)} async-done(((f32[16,8,128]{2,1,0:T(8,128)}), f32[16,8,128]{2,1,0:T(8,128)S(1)}, u32[]{:S(2)}, u32[]{:S(2)}) %all-to-all-start.3) | async-done | bytes 65568 | tf_op jit(solution)/shard_map/all_to_all | solution.py:227
  96.8 0.0 copy-done.2
  96.8 3.6 %shard_map.57 = (f32[128,512]{1,0:T(8,128)S(1)}, f32[1024,128]{1,0:T(8,128)S(1)}, f32[1024,128]{1,0:T(8,128)S(1)}) custom-call(s32[1]{0:T(128)} %bitcast.core_ref, f32[128,128]{1,0:T(8,128)S(1)} %bitcast.24, f32[32,128]{1,0:T(8,128)S(1)} %bitcast.28, f32[2048,128]{1,0:T(8,128)S(1)} %bitcast.17), custom_call_target="tpu_custom_call" | custom-call | tf_op jit(solution)/shard_map/pallas_call | solution.py:212
  100.4 2.1 collective-permute-start
  102.5 1.7 collective-permute-done
  104.2 0.1 add.21
  104.3 11.2 %all_to_all.58 = f32[8,128,128]{2,1,0:T(8,128)S(1)} all-to-all(f32[8,128,128]{2,1,0:T(8,128)S(1)} %bitcast.29), channel_id=1, replica_groups=mesh['gu'=2,'gv'=8,'gh'=2,'gl'=2,'gw'=4,'gc'=2] {'gl','gw'}, dimensions={0} | all-to-all | bytes 1048576 | tf_op jit(solution)/shard_map/all_to_all | solution.py:227
  115.5 14.5 %all_to_all.59 = f32[32,4,128]{2,1,0:T(4,128)S(1)} all-to-all(f32[32,4,128]{2,1,0:T(4,128)S(1)} %bitcast.32), channel_id=1, replica_groups=mesh['gu'=2,'gv'=8,'gh'=2,'gl'=2,'gw'=4,'gc'=2] {'gh','gu','gv'}, dimensions={0} | all-to-all | bytes 131072 | tf_op jit(solution)/shard_map/all_to_all | solution.py:227
  130.0 14.2 %all_to_all.60 = f32[32,4,128]{2,1,0:T(4,128)S(1)} all-to-all(f32[32,4,128]{2,1,0:T(4,128)S(1)} %broadcast_in_dim.14), channel_id=1, replica_groups=mesh['gu'=2,'gv'=8,'gh'=2,'gl'=2,'gw'=4,'gc'=2] {'gh','gu','gv'}, dimensions={0} | all-to-all | bytes 131072 | tf_op jit(solution)/shard_map/all_to_all | solution.py:227
  144.3 0.0 copy-start
  144.3 11.3 %all_to_all.61 = f32[8,128,128]{2,1,0:T(8,128)S(1)} all-to-all(f32[8,128,128]{2,1,0:T(8,128)S(1)} %broadcast_in_dim.15), channel_id=1, replica_groups=mesh['gu'=2,'gv'=8,'gh'=2,'gl'=2,'gw'=4,'gc'=2] {'gl','gw'}, dimensions={0} | all-to-all | bytes 1048576 | tf_op jit(solution)/shard_map/all_to_all | solution.py:227
  155.6 6.7 %collective-permute-start.1 = (f32[1024,128]{1,0:T(8,128)S(1)}, f32[1024,128]{1,0:T(8,128)S(1)}, u32[]{:S(2)}, u32[]{:S(2)}) collective-permute-start(f32[1024,128]{1,0:T(8,128)S(1)} %bitcast.21), channel_id=1, source_target_pairs={{0,1},{1,0},{2,3},{3,2},{4,5},{5,4},{6,7},{7,6},{8,9},{9,8},{10,11... | collective-permute-start | bytes 1572872 | tf_op jit(solution)/shard_map/ppermute | solution.py:280
  162.3 1.5 collective-permute-done.1.other_ref
  163.8 0.0 copy-done
  163.8 3.8 %shard_map.58 = f32[2,2,16,16,128]{4,3,2,1,0:T(8,128)S(1)} custom-call(s32[1]{0:T(128)} %bitcast.core_ref, f32[1024,128]{1,0:T(8,128)S(1)} %bitcast.22, f32[1024,128]{1,0:T(8,128)S(1)} %collective-permute-done.1.other_ref, f32[32,512]{1,0:T(8,128)S(1)} %bitcast.26, f32[128,512]{1,0:T(8,128)S(1)} %get-tuple-element.13.merged_ref), custom_call_target="tpu_custom_call" | custom-call | tf_op jit(solution)/shard_map/pallas_call | solution.py:212
  167.6 0.0 copy-start.1
  167.6 27.9 %all_to_all.62 = f32[256,4,128]{2,1,0:T(4,128)S(1)} all-to-all(f32[256,4,128]{2,1,0:T(4,128)S(1)} %bitcast.23), channel_id=1, replica_groups=mesh['gu'=2,'gv'=8,'gh'=2,'gl'=2,'gw'=4,'gc'=2] {'gh','gl','gu','gv','gw'}, dimensions={0} | all-to-all | bytes 1048576 | tf_op jit(solution)/shard_map/all_to_all | solution.py:227
  195.5 3.7 %collective-permute-start.2 = (f32[1024,128]{1,0:T(8,128)S(1)}, f32[1024,128]{1,0:T(8,128)S(1)}, u32[]{:S(2)}, u32[]{:S(2)}) collective-permute-start(f32[1024,128]{1,0:T(8,128)S(1)} %bitcast.19), channel_id=1, source_target_pairs={{0,1},{1,0},{2,3},{3,2},{4,5},{5,4},{6,7},{7,6},{8,9},{9,8},{10,11... | collective-permute-start | bytes 1572872 | tf_op jit(solution)/shard_map/ppermute | solution.py:296
  199.2 1.5 collective-permute-done.2.other_ref
  200.7 1.7 shard_map.59
  202.4 11.9 %all_to_all.63.parts_ref = f32[8,32,512]{2,1,0:T(8,128)S(1)} all-to-all(f32[8,32,512]{2,1,0:T(8,128)S(1)} %get-tuple-element.14), channel_id=1, replica_groups=mesh['gu'=2,'gv'=8,'gh'=2,'gl'=2,'gw'=4,'gc'=2] {'gl','gw'}, dimensions={0} | all-to-all | bytes 1048576 | tf_op jit(solution)/shard_map/all_to_all | solution.py:227
  214.3 2.8 %shard_map.60 = f32[8,32,512]{2,1,0:T(8,128)} custom-call(f32[8,32,512]{2,1,0:T(8,128)S(1)} %all_to_all.63.parts_ref, bf16[512,512]{1,0:T(8,128)(2,1)S(1)} %get-tuple-element.15.high_ref, bf16[512,512]{1,0:T(8,128)(2,1)S(1)} %get-tuple-element.16.low_ref), custom_call_target="tpu_custom_call" | custom-call | tf_op jit(solution)/shard_map/pallas_call | solution.py:212
  217.1 3.6 %all-to-all-start.10 = ((f32[8,32,512]{2,1,0:T(8,128)}), f32[8,32,512]{2,1,0:T(8,128)S(1)}, u32[]{:S(2)}, u32[]{:S(2)}) async-start(f32[8,32,512]{2,1,0:T(8,128)} %shard_map.60), calls=%async_computation.10 | async-start | bytes 1048576 | tf_op jit(solution)/shard_map/all_to_all | solution.py:227
  220.7 7.2 %all-to-all-done.10.parts_ref = f32[8,32,512]{2,1,0:T(8,128)S(1)} async-done(((f32[8,32,512]{2,1,0:T(8,128)}), f32[8,32,512]{2,1,0:T(8,128)S(1)}, u32[]{:S(2)}, u32[]{:S(2)}) %all-to-all-start.10) | async-done | bytes 524320 | tf_op jit(solution)/shard_map/all_to_all | solution.py:227
  227.9 2.1 shard_map.61
  (11 shorter events, 0.2 us)
Async XLA Ops:
  84.0 12.8 %copy-start.2 = (f32[128,32]{0,1:T(8,128)S(1)}, f32[128,32]{0,1:T(8,128)}, u32[]{:S(2)}) copy-start(f32[128,32]{0,1:T(8,128)} %param.7) | copy-start | bytes 49156
  84.0 12.8 %all-to-all-start.3 = ((f32[16,8,128]{2,1,0:T(8,128)}), f32[16,8,128]{2,1,0:T(8,128)S(1)}, u32[]{:S(2)}, u32[]{:S(2)}) async-start(f32[16,8,128]{2,1,0:T(8,128)} %broadcast_in_dim.13), calls=%async_computation.3 | async-start | bytes 131072 | tf_op jit(solution)/shard_map/all_to_all | solution.py:227
  100.4 3.8 %collective-permute-start = (f32[1024,128]{1,0:T(8,128)S(1)}, f32[1024,128]{1,0:T(8,128)S(1)}, u32[]{:S(2)}, u32[]{:S(2)}) collective-permute-start(f32[1024,128]{1,0:T(8,128)S(1)} %get-tuple-element.12), channel_id=1, source_target_pairs={{0,1},{1,0},{2,3},{3,2},{4,5},{5,4},{6,7},{7,6},{8,9},{9,8},{10,11... | collective-permute-start | bytes 1572872 | tf_op jit(solution)/shard_map/ppermute | solution.py:275
  144.3 19.6 %copy-start = (f32[512,32]{0,1:T(8,128)S(1)}, f32[512,32]{0,1:T(8,128)}, u32[]{:S(2)}) copy-start(f32[512,32]{0,1:T(8,128)} %param.8) | copy-start | bytes 196612
  155.6 8.3 %collective-permute-start.1 = (f32[1024,128]{1,0:T(8,128)S(1)}, f32[1024,128]{1,0:T(8,128)S(1)}, u32[]{:S(2)}, u32[]{:S(2)}) collective-permute-start(f32[1024,128]{1,0:T(8,128)S(1)} %bitcast.21), channel_id=1, source_target_pairs={{0,1},{1,0},{2,3},{3,2},{4,5},{5,4},{6,7},{7,6},{8,9},{9,8},{10,11... | collective-permute-start | bytes 1572872 | tf_op jit(solution)/shard_map/ppermute | solution.py:280
  167.6 33.1 %copy-start.1 = (f32[512,32]{0,1:T(8,128)S(1)}, f32[512,32]{0,1:T(8,128)}, u32[]{:S(2)}) copy-start(f32[512,32]{0,1:T(8,128)} %param.9) | copy-start | bytes 196612
  195.5 5.2 %copy-start.3 = (s32[32]{0:T(128)S(1)}, s32[32]{0:T(128)}, u32[]{:S(2)}) copy-start(s32[32]{0:T(128)} %order_ref.3) | copy-start | bytes 388
  195.5 5.2 %collective-permute-start.2 = (f32[1024,128]{1,0:T(8,128)S(1)}, f32[1024,128]{1,0:T(8,128)S(1)}, u32[]{:S(2)}, u32[]{:S(2)}) collective-permute-start(f32[1024,128]{1,0:T(8,128)S(1)} %bitcast.19), channel_id=1, source_target_pairs={{0,1},{1,0},{2,3},{3,2},{4,5},{5,4},{6,7},{7,6},{8,9},{9,8},{10,11... | collective-permute-start | bytes 1572872 | tf_op jit(solution)/shard_map/ppermute | solution.py:296
  217.1 10.8 %all-to-all-start.10 = ((f32[8,32,512]{2,1,0:T(8,128)}), f32[8,32,512]{2,1,0:T(8,128)S(1)}, u32[]{:S(2)}, u32[]{:S(2)}) async-start(f32[8,32,512]{2,1,0:T(8,128)} %shard_map.60), calls=%async_computation.10 | async-start | bytes 1048576 | tf_op jit(solution)/shard_map/all_to_all | solution.py:227

commit v4 on v3

--- a/solution.py
+++ b/solution.py
@@ -15,9 +15,10 @@
 CHIPS = ("gh", "gl", "gu", "gv", "gw")
 ORDER = CHIPS + ("gc",)
 NEAR = ("gl", "gw")
-ACROSS = ("gv", "gc")
-ALONG = ("gu", "gh", "gl", "gw")
+CLOSE = ("gl", "gw", "gc")
 FAR = ("gh", "gu", "gv")
+PLANE = ("gw", "gv")
+RING = ("gu", "gh", "gl")
 
 highest = lax.Precision.HIGHEST
 NN = ((1,), (0,))
@@ -100,7 +101,7 @@
 
 
 def second_kernel(
-    core_ref, gram_ref, start_ref, data_ref, merged_ref, kept_ref, sent_ref, rows_ref, flipped_ref, *, species, rows_x, parts
+    core_ref, gram_ref, start_ref, data_ref, merged_ref, kept_ref, sent_ref, rows_ref, *, species, rows_x, parts
 ):
     gram = gram_ref[...]
     current = start_ref[...]
@@ -115,23 +116,39 @@
         merged_ref[s * half : (s + 1) * half, :] = product[:half]
         merged_ref[(species + s) * half : (species + s + 1) * half, :] = product[half:]
     merged = merged_ref[...]
-    flipped_ref[...] = merged.T
+    flipped = halves(merged.T)
     merged = halves(merged)
-    size = merged_ref.shape[1] // 2
-    for out_ref, at in ((sent_ref, 1 - core_ref[0]), (kept_ref, core_ref[0])):
-        rows = flipped_ref[pl.ds(pl.multiple_of(at * size, size), size), :]
-        product = mm3(halves(rows), merged, NN)
-        for j in range(parts):
-            out_ref[pl.ds(j, size, stride=parts), :] = product[:, j * LANES : (j + 1) * LANES]
+    blocks = []
+    for i in range(parts):
+        cut = slice(i * LANES, (i + 1) * LANES)
+        product = mm3([x[cut] for x in flipped], [x[:, i * LANES :] for x in merged], NN)
+        blocks += [product[:, j * LANES : (j + 1) * LANES] for j in range(parts - i)]
+    count = len(blocks) // 2
+    for i in range(count):
+        rows = slice(i * LANES, (i + 1) * LANES)
+        kept_ref[rows, :] = jnp.where(core_ref[0] == 0, blocks[i], blocks[count + i])
+        sent_ref[rows, :] = jnp.where(core_ref[0] == 0, blocks[count + i], blocks[i])
+
+
+def symmetric_of(core, own_ref, other_ref, parts):
+    pairs = (own_ref, other_ref), (other_ref, own_ref)
+    blocks = []
+    for first, second in pairs:
+        for i in range(own_ref.shape[0] // LANES):
+            rows = slice(i * LANES, (i + 1) * LANES)
+            blocks.append(jnp.where(core == 0, first[rows, :], second[rows, :]))
+    upper = {}
+    for i in range(parts):
+        for j in range(i, parts):
+            upper[i, j] = blocks[len(upper)]
+    lines = [[upper[i, j] if i <= j else upper[j, i].T for j in range(parts)] for i in range(parts)]
+    return jnp.concatenate([jnp.concatenate(line, axis=1) for line in lines], axis=0)
 
 
 def third_kernel(core_ref, own_ref, other_ref, start_ref, merged_ref, out_ref, rows_ref, *, parts):
-    gram = halves(columns_of(own_ref, other_ref, parts))
+    gram = halves(symmetric_of(core_ref[0], own_ref, other_ref, parts))
     current = start_ref[...]
-    size = current.shape[1] // 2
     for repeat in range(ITERS):
-        swapped = jnp.concatenate([current[:, size:], current[:, :size]], axis=1)
-        current = jnp.where(core_ref[0] == 0, current, swapped)
         current = orthonormal_rows(mm3(halves(current), gram, NN))
     rows_ref[...] = mm(current, merged_ref[...], NT)
     rank = rows_ref.shape[0]
@@ -258,25 +275,25 @@
     gram = call(
         functools.partial(gram_first_kernel, species=species, rows_x=rows_x, parts=parts_y), vm(rows_x, rows_x), data
     )
-    gram = jnp.sum(swap(gram.reshape(lax.axis_size(ACROSS), -1, rows_x), ACROSS), axis=0)
-    gram = jnp.sum(swap(copies(gram, ALONG), ALONG), axis=0)
-    gram = swap(copies(gram, ACROSS), ACROSS).reshape(rows_x, rows_x)
+    gram = jnp.sum(swap(gram.reshape(lax.axis_size(CLOSE), -1, rows_x), CLOSE), axis=0)
+    gram = jnp.sum(swap(copies(gram, FAR), FAR), axis=0)
+    gram = swap(copies(gram, CLOSE), CLOSE).reshape(rows_x, rows_x)
 
     merged, kept, sent = call(
         functools.partial(second_kernel, species=species, rows_x=rows_x, parts=parts_y),
-        (vm(merged_rows, full_y),) + (vm(full_y * parts_y // 2, LANES),) * 2,
+        (vm(merged_rows, full_y),) + (vm(parts_y * (parts_y + 1) // 4 * LANES, LANES),) * 2,
         core,
         gram,
         start_first.T,
         data,
-        scratch=[(rank_one, rows_x), (full_y, merged_rows)],
+        scratch=[(rank_one, rows_x)],
         scalars=1,
     )
     gram = kept + lax.ppermute(sent, "gc", exchange)
-    gram = jnp.sum(swap(gram.reshape(lax.axis_size(NEAR), -1, LANES), NEAR), axis=0)
-    gram = jnp.sum(swap(gram.reshape(lax.axis_size(FAR), -1, LANES), FAR), axis=0)
-    gram = swap(copies(gram, FAR), FAR).reshape(-1, LANES)
-    own = swap(copies(gram, NEAR), NEAR).reshape(-1, LANES)
+    plane = lax.axis_size(PLANE)
+    gram = jnp.sum(swap(gram.reshape(-1, 4, LANES), PLANE).reshape(plane, -1, 4, LANES), axis=0)
+    gram = jnp.sum(swap(copies(gram, RING), RING), axis=0)
+    own = swap(copies(gram, PLANE).reshape(-1, 4, LANES), PLANE).reshape(-1, LANES)
     other = lax.ppermute(own, "gc", exchange)
 
     near = lax.axis_size("gl")

time: 233 us -> 220 us (0.944)
  blocking collectives: 171 us -> 161 us
  waiting for transfers between devices: 19.8 us -> 17.1 us
    all_to_all x9 -> x8, blocking collectives: 171 us -> 161 us  [swap(): return lax.all_to_all(pieces, axes, split_axis=0, concat_axis=0, tiled=True)]
where the time goes in v4:
time: 220 us; the launch traced here: 217 us
  blocking collectives  161 us (73%)
  starting transfers between devices  21.5 us (10%)
  waiting for transfers between devices  17.1 us (8%)
  Pallas kernels  16.6 us (8%)
    all_to_all x8, blocking collectives, swap(): return lax.all_to_all(pieces, axes, split_axis=0, concat_axis=0, tiled=True)  161 us
    pallas_call x7, Pallas kernels, call(): pl.pallas_call(kernel, out_shape=out_shape, in_specs=[smem] * scalars + [...  16.6 us
    all_to_all x2, waiting for transfers between devices, swap(): return lax.all_to_all(pieces, axes, split_axis=0, concat_axis=0, tiled=True)  13.1 us
    ppermute x2, starting transfers between devices, shards(): other = lax.ppermute(own, 'gc', exchange)  10.1 us
    all_to_all x2, starting transfers between devices, swap(): return lax.all_to_all(pieces, axes, split_axis=0, concat_axis=0, tiled=True)  8.99 us
  transfers between devices with their start and end apart: 5, of which 5 were waited for; matrix products, arithmetic and copies ran while one was open for 0% of the time, Pallas kernels for 0%

profile of v4, /device:TPU:1, one launch (start us, length us, event | category | flops | bytes accessed | tf_op | source)
XLA Modules:
  0.0 217.5 jit_solution(2277134257461379782)
XLA Ops:
  0.0 2.2 %shard_map.55 = f32[2048,128]{1,0:T(8,128)S(1)} custom-call(s32[32]{0:T(128)} %order_ref.3, f32[4,128,512]{2,1,0:T(8,128)} %bitcast.32), custom_call_target="tpu_custom_call" | custom-call | tf_op jit(solution)/shard_map/pallas_call | solution.py:229
  2.2 54.3 %all_to_all.50 = f32[512,4,128]{2,1,0:T(4,128)S(1)} all-to-all(f32[512,4,128]{2,1,0:T(4,128)S(1)} %bitcast.18), channel_id=1, replica_groups=mesh['gu'=2,'gv'=8,'gh'=2,'gl'=2,'gw'=4,'gc'=2] {'gh','gl','gu','gv','gw..., dimensions={0} | all-to-all | bytes 2097152 | tf_op jit(solution)/shard_map/all_to_all | solution.py:244
  56.5 0.6 shard_map.56
  57.1 9.9 %all_to_all.51 = f32[16,8,128]{2,1,0:T(8,128)S(1)} all-to-all(f32[16,8,128]{2,1,0:T(8,128)S(1)} %bitcast.25), channel_id=1, replica_groups=mesh['gu'=2,'gv'=8,'gh'=2,'gl'=2,'gw'=4,'gc'=2] {'gl','gw','gc'}, dimensions={0} | all-to-all | bytes 131072 | tf_op jit(solution)/shard_map/all_to_all | solution.py:244
  67.0 16.9 %all_to_all.52 = f32[32,8,128]{2,1,0:T(8,128)S(1)} all-to-all(f32[32,8,128]{2,1,0:T(8,128)S(1)} %broadcast_in_dim.12), channel_id=1, replica_groups=mesh['gu'=2,'gv'=8,'gh'=2,'gl'=2,'gw'=4,'gc'=2] {'gh','gu','gv'}, dimensions={0} | all-to-all | bytes 262144 | tf_op jit(solution)/shard_map/all_to_all | solution.py:244
  83.9 0.6 broadcast_in_dim.13
  84.5 5.4 %all-to-all-start.3 = ((f32[16,8,128]{2,1,0:T(8,128)}), f32[16,8,128]{2,1,0:T(8,128)S(1)}, u32[]{:S(2)}, u32[]{:S(2)}) async-start(f32[16,8,128]{2,1,0:T(8,128)} %broadcast_in_dim.13), calls=%async_computation.3 | async-start | bytes 131072 | tf_op jit(solution)/shard_map/all_to_all | solution.py:244
  89.9 5.9 %all-to-all-done.3 = f32[16,8,128]{2,1,0:T(8,128)S(1)} async-done(((f32[16,8,128]{2,1,0:T(8,128)}), f32[16,8,128]{2,1,0:T(8,128)S(1)}, u32[]{:S(2)}, u32[]{:S(2)}) %all-to-all-start.3) | async-done | bytes 65568 | tf_op jit(solution)/shard_map/all_to_all | solution.py:244
  95.8 0.0 copy-done.2
  95.8 3.4 %shard_map.57 = (f32[128,512]{1,0:T(8,128)S(1)}, f32[640,128]{1,0:T(8,128)S(1)}, f32[640,128]{1,0:T(8,128)S(1)}) custom-call(s32[1]{0:T(128)} %bitcast.core_ref, f32[128,128]{1,0:T(8,128)S(1)} %bitcast.24, f32[32,128]{1,0:T(8,128)S(1)} %bitcast.28, f32[2048,128]{1,0:T(8,128)S(1)} %bitcast.17), custom_call_target="tpu_custom_call" | custom-call | tf_op jit(solution)/shard_map/pallas_call | solution.py:229
  99.2 2.3 %collective-permute-start = (f32[640,128]{1,0:T(8,128)S(1)}, f32[640,128]{1,0:T(8,128)S(1)}, u32[]{:S(2)}, u32[]{:S(2)}) collective-permute-start(f32[640,128]{1,0:T(8,128)S(1)} %get-tuple-element.12), channel_id=1, source_target_pairs={{0,1},{1,0},{2,3},{3,2},{4,5},{5,4},{6,7},{7,6},{8,9},{9,8},{10,11... | collective-permute-start | bytes 983048 | tf_op jit(solution)/shard_map/ppermute | solution.py:292
  101.6 1.2 collective-permute-done
  102.8 13.5 %all_to_all.53 = f32[160,4,128]{2,1,0:T(4,128)S(1)} all-to-all(f32[160,4,128]{2,1,0:T(4,128)S(1)} %bitcast.31), channel_id=1, replica_groups=mesh['gu'=2,'gv'=8,'gh'=2,'gl'=2,'gw'=4,'gc'=2] {'gw','gv'}, dimensions={0} | all-to-all | bytes 655360 | tf_op jit(solution)/shard_map/all_to_all | solution.py:244
  116.3 0.1 reduce_sum.38
  116.4 9.8 %all_to_all.54 = f32[8,5,4,128]{3,2,1,0:T(4,128)S(1)} all-to-all(f32[8,5,4,128]{3,2,1,0:T(4,128)S(1)} %broadcast_in_dim.14), channel_id=1, replica_groups=mesh['gu'=2,'gv'=8,'gh'=2,'gl'=2,'gw'=4,'gc'=2] {'gu','gh','gl'}, dimensions={0} | all-to-all | bytes 163840 | tf_op jit(solution)/shard_map/all_to_all | solution.py:244
  126.3 0.0 copy-start
  126.3 17.4 %all_to_all.55 = f32[160,4,128]{2,1,0:T(4,128)S(1)} all-to-all(f32[160,4,128]{2,1,0:T(4,128)S(1)} %bitcast.30), channel_id=1, replica_groups=mesh['gu'=2,'gv'=8,'gh'=2,'gl'=2,'gw'=4,'gc'=2] {'gw','gv'}, dimensions={0} | all-to-all | bytes 655360 | tf_op jit(solution)/shard_map/all_to_all | solution.py:244
  143.7 6.3 %collective-permute-start.1 = (f32[640,128]{1,0:T(8,128)S(1)}, f32[640,128]{1,0:T(8,128)S(1)}, u32[]{:S(2)}, u32[]{:S(2)}) collective-permute-start(f32[640,128]{1,0:T(8,128)S(1)} %bitcast.22), channel_id=1, source_target_pairs={{0,1},{1,0},{2,3},{3,2},{4,5},{5,4},{6,7},{7,6},{8,9},{9,8},{10,11... | collective-permute-start | bytes 983048 | tf_op jit(solution)/shard_map/ppermute | solution.py:297
  150.0 1.2 collective-permute-done.1.other_ref
  151.2 0.0 copy-done
  151.2 3.8 %shard_map.58 = f32[2,2,16,16,128]{4,3,2,1,0:T(8,128)S(1)} custom-call(s32[1]{0:T(128)} %bitcast.core_ref, f32[640,128]{1,0:T(8,128)S(1)} %bitcast.23, f32[640,128]{1,0:T(8,128)S(1)} %collective-permute-done.1.other_ref, f32[32,512]{1,0:T(8,128)S(1)} %bitcast.26, f32[128,512]{1,0:T(8,128)S(1)} %get-tuple-element.13.merged_ref), custom_call_target="tpu_custom_call" | custom-call | tf_op jit(solution)/shard_map/pallas_call | solution.py:229
  155.1 0.0 copy-start.1
  155.1 27.7 %all_to_all.56 = f32[256,4,128]{2,1,0:T(4,128)S(1)} all-to-all(f32[256,4,128]{2,1,0:T(4,128)S(1)} %bitcast.21), channel_id=1, replica_groups=mesh['gu'=2,'gv'=8,'gh'=2,'gl'=2,'gw'=4,'gc'=2] {'gh','gl','gu','gv','gw'}, dimensions={0} | all-to-all | bytes 1048576 | tf_op jit(solution)/shard_map/all_to_all | solution.py:244
  182.7 3.9 %collective-permute-start.2 = (f32[1024,128]{1,0:T(8,128)S(1)}, f32[1024,128]{1,0:T(8,128)S(1)}, u32[]{:S(2)}, u32[]{:S(2)}) collective-permute-start(f32[1024,128]{1,0:T(8,128)S(1)} %bitcast.19), channel_id=1, source_target_pairs={{0,1},{1,0},{2,3},{3,2},{4,5},{5,4},{6,7},{7,6},{8,9},{9,8},{10,11... | collective-permute-start | bytes 1572872 | tf_op jit(solution)/shard_map/ppermute | solution.py:313
  186.6 1.5 collective-permute-done.2.other_ref
  188.1 0.0 copy-done.1
  188.1 1.7 shard_map.59
  189.8 11.9 %all_to_all.57.parts_ref = f32[8,32,512]{2,1,0:T(8,128)S(1)} all-to-all(f32[8,32,512]{2,1,0:T(8,128)S(1)} %get-tuple-element.14), channel_id=1, replica_groups=mesh['gu'=2,'gv'=8,'gh'=2,'gl'=2,'gw'=4,'gc'=2] {'gl','gw'}, dimensions={0} | all-to-all | bytes 1048576 | tf_op jit(solution)/shard_map/all_to_all | solution.py:244
  201.7 2.8 %shard_map.60 = f32[8,32,512]{2,1,0:T(8,128)} custom-call(f32[8,32,512]{2,1,0:T(8,128)S(1)} %all_to_all.57.parts_ref, bf16[512,512]{1,0:T(8,128)(2,1)S(1)} %get-tuple-element.15.high_ref, bf16[512,512]{1,0:T(8,128)(2,1)S(1)} %get-tuple-element.16.low_ref), custom_call_target="tpu_custom_call" | custom-call | tf_op jit(solution)/shard_map/pallas_call | solution.py:229
  204.5 3.6 %all-to-all-start.9 = ((f32[8,32,512]{2,1,0:T(8,128)}), f32[8,32,512]{2,1,0:T(8,128)S(1)}, u32[]{:S(2)}, u32[]{:S(2)}) async-start(f32[8,32,512]{2,1,0:T(8,128)} %shard_map.60), calls=%async_computation.9 | async-start | bytes 1048576 | tf_op jit(solution)/shard_map/all_to_all | solution.py:244
  208.1 7.2 %all-to-all-done.9.parts_ref = f32[8,32,512]{2,1,0:T(8,128)S(1)} async-done(((f32[8,32,512]{2,1,0:T(8,128)}), f32[8,32,512]{2,1,0:T(8,128)S(1)}, u32[]{:S(2)}, u32[]{:S(2)}) %all-to-all-start.9) | async-done | bytes 524320 | tf_op jit(solution)/shard_map/all_to_all | solution.py:244
  215.3 2.1 shard_map.61
  (10 shorter events, 0.2 us)
Async XLA Ops:
  84.5 11.3 %copy-start.2 = (f32[128,32]{0,1:T(8,128)S(1)}, f32[128,32]{0,1:T(8,128)}, u32[]{:S(2)}) copy-start(f32[128,32]{0,1:T(8,128)} %param.7) | copy-start | bytes 49156
  84.5 11.3 %all-to-all-start.3 = ((f32[16,8,128]{2,1,0:T(8,128)}), f32[16,8,128]{2,1,0:T(8,128)S(1)}, u32[]{:S(2)}, u32[]{:S(2)}) async-start(f32[16,8,128]{2,1,0:T(8,128)} %broadcast_in_dim.13), calls=%async_computation.3 | async-start | bytes 131072 | tf_op jit(solution)/shard_map/all_to_all | solution.py:244
  99.2 3.6 %collective-permute-start = (f32[640,128]{1,0:T(8,128)S(1)}, f32[640,128]{1,0:T(8,128)S(1)}, u32[]{:S(2)}, u32[]{:S(2)}) collective-permute-start(f32[640,128]{1,0:T(8,128)S(1)} %get-tuple-element.12), channel_id=1, source_target_pairs={{0,1},{1,0},{2,3},{3,2},{4,5},{5,4},{6,7},{7,6},{8,9},{9,8},{10,11... | collective-permute-start | bytes 983048 | tf_op jit(solution)/shard_map/ppermute | solution.py:292
  126.3 25.0 %copy-start = (f32[512,32]{0,1:T(8,128)S(1)}, f32[512,32]{0,1:T(8,128)}, u32[]{:S(2)}) copy-start(f32[512,32]{0,1:T(8,128)} %param.8) | copy-start | bytes 196612
  143.7 7.5 %collective-permute-start.1 = (f32[640,128]{1,0:T(8,128)S(1)}, f32[640,128]{1,0:T(8,128)S(1)}, u32[]{:S(2)}, u32[]{:S(2)}) collective-permute-start(f32[640,128]{1,0:T(8,128)S(1)} %bitcast.22), channel_id=1, source_target_pairs={{0,1},{1,0},{2,3},{3,2},{4,5},{5,4},{6,7},{7,6},{8,9},{9,8},{10,11... | collective-permute-start | bytes 983048 | tf_op jit(solution)/shard_map/ppermute | solution.py:297
  155.1 33.1 %copy-start.1 = (f32[512,32]{0,1:T(8,128)S(1)}, f32[512,32]{0,1:T(8,128)}, u32[]{:S(2)}) copy-start(f32[512,32]{0,1:T(8,128)} %param.9) | copy-start | bytes 196612
  182.7 5.4 %copy-start.3 = (s32[32]{0:T(128)S(1)}, s32[32]{0:T(128)}, u32[]{:S(2)}) copy-start(s32[32]{0:T(128)} %order_ref.3) | copy-start | bytes 388
  182.7 5.4 %collective-permute-start.2 = (f32[1024,128]{1,0:T(8,128)S(1)}, f32[1024,128]{1,0:T(8,128)S(1)}, u32[]{:S(2)}, u32[]{:S(2)}) collective-permute-start(f32[1024,128]{1,0:T(8,128)S(1)} %bitcast.19), channel_id=1, source_target_pairs={{0,1},{1,0},{2,3},{3,2},{4,5},{5,4},{6,7},{7,6},{8,9},{9,8},{10,11... | collective-permute-start | bytes 1572872 | tf_op jit(solution)/shard_map/ppermute | solution.py:313
  204.5 10.8 %all-to-all-start.9 = ((f32[8,32,512]{2,1,0:T(8,128)}), f32[8,32,512]{2,1,0:T(8,128)S(1)}, u32[]{:S(2)}, u32[]{:S(2)}) async-start(f32[8,32,512]{2,1,0:T(8,128)} %shard_map.60), calls=%async_computation.9 | async-start | bytes 1048576 | tf_op jit(solution)/shard_map/all_to_all | solution.py:244

commit v5 on v4

--- a/solution.py
+++ b/solution.py
@@ -9,7 +9,7 @@
 
 ITERS = 2
 LANES = 128
-PANEL = 8
+PANEL = 16
 VMEM_BYTES = 20 << 20
 FINE = ("gu", "gv", "gh", "gl", "gw", "gc")
 CHIPS = ("gh", "gl", "gu", "gv", "gw")
@@ -39,7 +39,9 @@
     def dot(x, y):
         return lax.dot_general(x, y, (dims, ((), ())), preferred_element_type=jnp.float32)
 
-    return dot(a[0], b[0]) + (dot(a[0], b[1]) + dot(a[1], b[0]))
+    size = a[0].shape[0]
+    both = dot(jnp.concatenate(a, axis=0), b[0])
+    return both[:size] + (both[size:] + dot(a[0], b[1]))
 
 
 def orthonormal_rows(wide):
@@ -66,10 +68,15 @@
     return mm(inverse * (1.0 / jnp.sqrt(pivots)), wide, NN)
 
 
-def send_field_kernel(order_ref, field_hbm, out_ref, field_ref, sems, *, brick_len):
+def send_field_kernel(
+    order_ref, core_ref, field_hbm, first_hbm, second_hbm, third_hbm, out_ref, first_ref, second_ref, third_ref, field_ref,
+    raw_ref, rows_ref, placed_ref, sems, start_sems, *, brick_len
+):
     species, cells_y, cells_z = field_hbm.shape
     loads = [pltpu.make_async_copy(field_hbm.at[s], field_ref.at[s], sems.at[s]) for s in range(species)]
-    for load in loads:
+    pairs = (third_hbm, raw_ref), (second_hbm, second_ref), (first_hbm, first_ref)
+    starts = [pltpu.make_async_copy(source, target, start_sems.at[i]) for i, (source, target) in enumerate(pairs)]
+    for load in starts[:1] + loads + starts[1:]:
         load.start()
     lane = lax.broadcasted_iota(jnp.int32, (1, cells_z), 1)
     brick = lane // brick_len
@@ -78,12 +85,23 @@
         place = jnp.where(brick == b, order_ref[b] * brick_len, place)
     grid_z = (place + lane % brick_len).astype(jnp.float32)
     taper = 0.5 + 1.5 * grid_z / (cells_z - 1)
+    starts[0].wait()
+    rows_ref[...] = raw_ref[...].T
+    for b in range(cells_z // brick_len):
+        at = pl.multiple_of(order_ref[b] * brick_len, brick_len)
+        placed_ref[b * brick_len : (b + 1) * brick_len, :] = rows_ref[pl.ds(at, brick_len), :]
+    core = core_ref[0]
+    half = cells_z // 2
+    third_ref[:, :half] = placed_ref[pl.ds(core, half, stride=2), :].T
+    third_ref[:, half:] = placed_ref[pl.ds(1 - core, half, stride=2), :].T
     for s in range(species):
         loads[s].wait()
         for j in range(cells_z // LANES):
             cut = slice(j * LANES, (j + 1) * LANES)
             block = field_ref[s, :, cut] * taper[:, cut]
             out_ref[pl.ds(j * LANES * species + s, LANES, stride=species), :] = block.T
+    for load in starts[1:]:
+        load.wait()
 
 
 def fibre(ref, s, species, rows_x, parts):
@@ -180,19 +198,10 @@
         out_ref[i] = wide
 
 
-def start_third_kernel(order_ref, core_ref, start_ref, own_ref, other_ref, out_ref, high_ref, low_ref, rows_ref, placed_ref, *, brick_len, parts):
-    rows_ref[...] = start_ref[...].T
-    size = rows_ref.shape[0]
-    for b in range(size // brick_len):
-        at = pl.multiple_of(order_ref[b] * brick_len, brick_len)
-        placed_ref[b * brick_len : (b + 1) * brick_len, :] = rows_ref[pl.ds(at, brick_len), :]
-    core = core_ref[0]
-    start = jnp.concatenate(
-        [placed_ref[pl.ds(core, size // 2, stride=2), :], placed_ref[pl.ds(1 - core, size // 2, stride=2), :]], axis=0
-    )
+def start_third_kernel(start_ref, own_ref, other_ref, out_ref, high_ref, low_ref, *, parts):
     data = halves(columns_of(own_ref, other_ref, parts))
     high_ref[...], low_ref[...] = data
-    inner = mm3(halves(start.T), data, NN)
+    inner = mm3(halves(start_ref[...]), data, NN)
     spread(out_ref, mm3(halves(inner), data, NT))
 
 
@@ -261,14 +270,25 @@
     core = lax.axis_index("gc").astype(jnp.int32).reshape(1)
     exchange = [(0, 1), (1, 0)]
 
-    sent = call(
+    sent, start_first, start_second, start_third = call(
         functools.partial(send_field_kernel, brick_len=brick_len),
-        vm(cells_z * species, cells_y),
+        (vm(cells_z * species, cells_y), vm(rank_one, rows_x), vm(rank_two, full_y), vm(rank_three, cells_z)),
         brick_order,
+        core,
         field.reshape(species, cells_y, cells_z),
-        scratch=[(species, cells_y, cells_z), pltpu.SemaphoreType.DMA((species,))],
-        scalars=1,
-        in_hbm=1,
+        start_first.T,
+        start_second.T,
+        start_third.T,
+        scratch=[
+            (species, cells_y, cells_z),
+            (rank_three, cells_z),
+            (cells_z, rank_three),
+            (cells_z, rank_three),
+            pltpu.SemaphoreType.DMA((species,)),
+            pltpu.SemaphoreType.DMA((3,)),
+        ],
+        scalars=2,
+        in_hbm=4,
     )
     data = swap(sent.reshape(devices, species, cells_y), ORDER).reshape(devices * species, cells_y)
 
@@ -284,7 +304,7 @@
         (vm(merged_rows, full_y),) + (vm(parts_y * (parts_y + 1) // 4 * LANES, LANES),) * 2,
         core,
         gram,
-        start_first.T,
+        start_first,
         data,
         scratch=[(rank_one, rows_x)],
         scalars=1,
@@ -304,7 +324,7 @@
         core,
         own,
         other,
-        start_second.T,
+        start_second,
         merged,
         scratch=[(rank_two, merged_rows)],
         scalars=1,
@@ -315,15 +335,11 @@
     spread_shape = vm(lax.axis_size(NEAR), rank_three, cells_z)
     cut = vm(cells_z, 4 * LANES, dtype=jnp.bfloat16)
     pieces, high, low = call(
-        functools.partial(start_third_kernel, brick_len=brick_len, parts=4),
+        functools.partial(start_third_kernel, parts=4),
         (spread_shape, cut, cut),
-        brick_order,
-        core,
-        start_third.T,
+        start_third,
         own,
         other,
-        scratch=[start_third.shape, start_third.shape],
-        scalars=2,
     )
     for repeat in range(ITERS - 1):
         pieces = call(step_third_kernel, spread_shape, swap(pieces, NEAR), high, low)

time: 220 us -> 216 us (0.982)
  blocking collectives: 161 us -> 172 us
  waiting for transfers between devices: 17.1 us -> 11.2 us
  starting transfers between devices: 21.5 us -> 15.9 us
  Pallas kernels: 16.6 us -> 14.4 us
    all_to_all x8 -> x9, blocking collectives: 161 us -> 172 us  [swap(): return lax.all_to_all(pieces, axes, split_axis=0, concat_axis=0, tiled=True)]
    all_to_all x2 -> x1, waiting for transfers between devices: 13.1 us -> 7.18 us  [swap(): return lax.all_to_all(pieces, axes, split_axis=0, concat_axis=0, tiled=True)]
    all_to_all x2 -> x1, starting transfers between devices: 8.99 us -> 3.59 us  [swap(): return lax.all_to_all(pieces, axes, split_axis=0, concat_axis=0, tiled=True)]
    pallas_call x7, Pallas kernels: 16.6 us -> 14.4 us  [call(): pl.pallas_call(kernel, out_shape=out_shape, in_specs=[smem] * scalars + [...]
  transfers between devices with their start and end apart: 5 -> 4, of which waited for: 5 -> 4; matrix products, arithmetic and copies ran while one was open for 0% -> 0% of each run, Pallas kernels for 0% -> 0%
where the time goes in v5:
time: 216 us; the launch traced here: 213 us
  blocking collectives  172 us (80%)
  starting transfers between devices  15.9 us (7%)
  Pallas kernels  14.4 us (7%)
  waiting for transfers between devices  11.2 us (5%)
    all_to_all x9, blocking collectives, swap(): return lax.all_to_all(pieces, axes, split_axis=0, concat_axis=0, tiled=True)  172 us
    pallas_call x7, Pallas kernels, call(): pl.pallas_call(kernel, out_shape=out_shape, in_specs=[smem] * scalars + [...  14.4 us
    ppermute x2, starting transfers between devices, shards(): other = lax.ppermute(own, 'gc', exchange)  9.99 us
    all_to_all x1, waiting for transfers between devices, swap(): return lax.all_to_all(pieces, axes, split_axis=0, concat_axis=0, tiled=True)  7.18 us
  transfers between devices with their start and end apart: 4, of which 4 were waited for; matrix products, arithmetic and copies ran while one was open for 0% of the time, Pallas kernels for 0%

profile of v5, /device:TPU:1, one launch (start us, length us, event | category | flops | bytes accessed | tf_op | source)
XLA Modules:
  0.0 213.4 jit_solution(8678968664266067220)
XLA Ops:
  0.0 2.5 %shard_map.55 = (f32[2048,128]{1,0:T(8,128)S(1)}, f32[32,128]{1,0:T(8,128)S(1)}, f32[32,512]{1,0:T(8,128)S(1)}, f32[32,512]{1,0:T(8,128)S(1)}) custom-call(s32[32]{0:T(128)} %order_ref.1, s32[1]{0:T(128)} %bitcast.core_ref, f32[4,128,512]{2,1,0:T(8,128)} %bitcast.29, f32[32,128]{1,0:T(8,128)} %bitcast.32, f32[32,512]{1,0:T(8,128)} %bitcast.30, ...), custom_call_target="tpu_custom_call" | custom-call | tf_op jit(solution)/shard_map/pallas_call | solution.py:238
  2.5 54.3 %all_to_all.50 = f32[512,4,128]{2,1,0:T(4,128)S(1)} all-to-all(f32[512,4,128]{2,1,0:T(4,128)S(1)} %bitcast.23), channel_id=1, replica_groups=mesh['gu'=2,'gv'=8,'gh'=2,'gl'=2,'gw'=4,'gc'=2] {'gh','gl','gu','gv','gw..., dimensions={0} | all-to-all | bytes 2097152 | tf_op jit(solution)/shard_map/all_to_all | solution.py:253
  56.7 0.6 shard_map.56
  57.3 9.9 %all_to_all.51 = f32[16,8,128]{2,1,0:T(8,128)S(1)} all-to-all(f32[16,8,128]{2,1,0:T(8,128)S(1)} %bitcast.25), channel_id=1, replica_groups=mesh['gu'=2,'gv'=8,'gh'=2,'gl'=2,'gw'=4,'gc'=2] {'gl','gw','gc'}, dimensions={0} | all-to-all | bytes 131072 | tf_op jit(solution)/shard_map/all_to_all | solution.py:253
  67.2 16.9 %all_to_all.52 = f32[32,8,128]{2,1,0:T(8,128)S(1)} all-to-all(f32[32,8,128]{2,1,0:T(8,128)S(1)} %broadcast_in_dim.12), channel_id=1, replica_groups=mesh['gu'=2,'gv'=8,'gh'=2,'gl'=2,'gw'=4,'gc'=2] {'gh','gu','gv'}, dimensions={0} | all-to-all | bytes 262144 | tf_op jit(solution)/shard_map/all_to_all | solution.py:253
  84.1 10.5 %all_to_all.53 = f32[16,8,128]{2,1,0:T(8,128)S(1)} all-to-all(f32[16,8,128]{2,1,0:T(8,128)S(1)} %broadcast_in_dim.13), channel_id=1, replica_groups=mesh['gu'=2,'gv'=8,'gh'=2,'gl'=2,'gw'=4,'gc'=2] {'gl','gw','gc'}, dimensions={0} | all-to-all | bytes 131072 | tf_op jit(solution)/shard_map/all_to_all | solution.py:253
  94.6 3.1 %shard_map.57 = (f32[128,512]{1,0:T(8,128)S(1)}, f32[640,128]{1,0:T(8,128)S(1)}, f32[640,128]{1,0:T(8,128)S(1)}) custom-call(s32[1]{0:T(128)} %bitcast.core_ref, f32[128,128]{1,0:T(8,128)S(1)} %bitcast.24, f32[32,128]{1,0:T(8,128)S(1)} %get-tuple-element.17.start_ref, f32[2048,128]{1,0:T(8,128)S(1)} %bitcast.17), custom_call_target="tpu_custom_call" | custom-call | tf_op jit(solution)/shard_map/pallas_call | solution.py:238
  97.7 2.3 %collective-permute-start = (f32[640,128]{1,0:T(8,128)S(1)}, f32[640,128]{1,0:T(8,128)S(1)}, u32[]{:S(2)}, u32[]{:S(2)}) collective-permute-start(f32[640,128]{1,0:T(8,128)S(1)} %get-tuple-element.19), channel_id=1, source_target_pairs={{0,1},{1,0},{2,3},{3,2},{4,5},{5,4},{6,7},{7,6},{8,9},{9,8},{10,11... | collective-permute-start | bytes 983048 | tf_op jit(solution)/shard_map/ppermute | solution.py:312
  100.0 1.2 collective-permute-done
  101.3 13.5 %all_to_all.54 = f32[160,4,128]{2,1,0:T(4,128)S(1)} all-to-all(f32[160,4,128]{2,1,0:T(4,128)S(1)} %bitcast.28), channel_id=1, replica_groups=mesh['gu'=2,'gv'=8,'gh'=2,'gl'=2,'gw'=4,'gc'=2] {'gw','gv'}, dimensions={0} | all-to-all | bytes 655360 | tf_op jit(solution)/shard_map/all_to_all | solution.py:253
  114.8 0.1 reduce_sum.38
  114.9 9.8 %all_to_all.55 = f32[8,5,4,128]{3,2,1,0:T(4,128)S(1)} all-to-all(f32[8,5,4,128]{3,2,1,0:T(4,128)S(1)} %broadcast_in_dim.14), channel_id=1, replica_groups=mesh['gu'=2,'gv'=8,'gh'=2,'gl'=2,'gw'=4,'gc'=2] {'gu','gh','gl'}, dimensions={0} | all-to-all | bytes 163840 | tf_op jit(solution)/shard_map/all_to_all | solution.py:253
  124.8 17.3 %all_to_all.56 = f32[160,4,128]{2,1,0:T(4,128)S(1)} all-to-all(f32[160,4,128]{2,1,0:T(4,128)S(1)} %bitcast.27), channel_id=1, replica_groups=mesh['gu'=2,'gv'=8,'gh'=2,'gl'=2,'gw'=4,'gc'=2] {'gw','gv'}, dimensions={0} | all-to-all | bytes 655360 | tf_op jit(solution)/shard_map/all_to_all | solution.py:253
  142.1 6.3 %collective-permute-start.1 = (f32[640,128]{1,0:T(8,128)S(1)}, f32[640,128]{1,0:T(8,128)S(1)}, u32[]{:S(2)}, u32[]{:S(2)}) collective-permute-start(f32[640,128]{1,0:T(8,128)S(1)} %bitcast.21), channel_id=1, source_target_pairs={{0,1},{1,0},{2,3},{3,2},{4,5},{5,4},{6,7},{7,6},{8,9},{9,8},{10,11... | collective-permute-start | bytes 983048 | tf_op jit(solution)/shard_map/ppermute | solution.py:317
  148.4 1.2 collective-permute-done.1.other_ref
  149.6 3.3 %shard_map.58 = f32[2,2,16,16,128]{4,3,2,1,0:T(8,128)S(1)} custom-call(s32[1]{0:T(128)} %bitcast.core_ref, f32[640,128]{1,0:T(8,128)S(1)} %bitcast.22, f32[640,128]{1,0:T(8,128)S(1)} %collective-permute-done.1.other_ref, f32[32,512]{1,0:T(8,128)S(1)} %get-tuple-element.20.start_ref, f32[128,512]{1,0:T(8,128)S(1)} %get-tuple-element.21.merged_ref), custom_call_target="tpu_custom_call" | custom-call | tf_op jit(solution)/shard_map/pallas_call | solution.py:238
  152.9 27.5 %all_to_all.57 = f32[256,4,128]{2,1,0:T(4,128)S(1)} all-to-all(f32[256,4,128]{2,1,0:T(4,128)S(1)} %bitcast.20), channel_id=1, replica_groups=mesh['gu'=2,'gv'=8,'gh'=2,'gl'=2,'gw'=4,'gc'=2] {'gh','gl','gu','gv','gw'}, dimensions={0} | all-to-all | bytes 1048576 | tf_op jit(solution)/shard_map/all_to_all | solution.py:253
  180.4 3.7 %collective-permute-start.2 = (f32[1024,128]{1,0:T(8,128)S(1)}, f32[1024,128]{1,0:T(8,128)S(1)}, u32[]{:S(2)}, u32[]{:S(2)}) collective-permute-start(f32[1024,128]{1,0:T(8,128)S(1)} %bitcast.18), channel_id=1, source_target_pairs={{0,1},{1,0},{2,3},{3,2},{4,5},{5,4},{6,7},{7,6},{8,9},{9,8},{10,11... | collective-permute-start | bytes 1572872 | tf_op jit(solution)/shard_map/ppermute | solution.py:333
  184.2 1.5 collective-permute-done.2.other_ref
  185.7 0.7 shard_map.59
  186.4 11.9 %all_to_all.58.parts_ref = f32[8,32,512]{2,1,0:T(8,128)S(1)} all-to-all(f32[8,32,512]{2,1,0:T(8,128)S(1)} %get-tuple-element.22), channel_id=1, replica_groups=mesh['gu'=2,'gv'=8,'gh'=2,'gl'=2,'gw'=4,'gc'=2] {'gl','gw'}, dimensions={0} | all-to-all | bytes 1048576 | tf_op jit(solution)/shard_map/all_to_all | solution.py:253
  198.3 2.4 %shard_map.60 = f32[8,32,512]{2,1,0:T(8,128)} custom-call(f32[8,32,512]{2,1,0:T(8,128)S(1)} %all_to_all.58.parts_ref, bf16[512,512]{1,0:T(8,128)(2,1)S(1)} %get-tuple-element.23.high_ref, bf16[512,512]{1,0:T(8,128)(2,1)S(1)} %get-tuple-element.24.low_ref), custom_call_target="tpu_custom_call" | custom-call | tf_op jit(solution)/shard_map/pallas_call | solution.py:238
  200.7 3.6 %all-to-all-start.9 = ((f32[8,32,512]{2,1,0:T(8,128)}), f32[8,32,512]{2,1,0:T(8,128)S(1)}, u32[]{:S(2)}, u32[]{:S(2)}) async-start(f32[8,32,512]{2,1,0:T(8,128)} %shard_map.60), calls=%async_computation.9 | async-start | bytes 1048576 | tf_op jit(solution)/shard_map/all_to_all | solution.py:253
  204.3 7.2 %all-to-all-done.9.parts_ref = f32[8,32,512]{2,1,0:T(8,128)S(1)} async-done(((f32[8,32,512]{2,1,0:T(8,128)}), f32[8,32,512]{2,1,0:T(8,128)S(1)}, u32[]{:S(2)}, u32[]{:S(2)}) %all-to-all-start.9) | async-done | bytes 524320 | tf_op jit(solution)/shard_map/all_to_all | solution.py:253
  211.5 1.9 shard_map.61
  (8 shorter events, 0.2 us)
Async XLA Ops:
  97.7 3.6 %collective-permute-start = (f32[640,128]{1,0:T(8,128)S(1)}, f32[640,128]{1,0:T(8,128)S(1)}, u32[]{:S(2)}, u32[]{:S(2)}) collective-permute-start(f32[640,128]{1,0:T(8,128)S(1)} %get-tuple-element.19), channel_id=1, source_target_pairs={{0,1},{1,0},{2,3},{3,2},{4,5},{5,4},{6,7},{7,6},{8,9},{9,8},{10,11... | collective-permute-start | bytes 983048 | tf_op jit(solution)/shard_map/ppermute | solution.py:312
  142.1 7.5 %collective-permute-start.1 = (f32[640,128]{1,0:T(8,128)S(1)}, f32[640,128]{1,0:T(8,128)S(1)}, u32[]{:S(2)}, u32[]{:S(2)}) collective-permute-start(f32[640,128]{1,0:T(8,128)S(1)} %bitcast.21), channel_id=1, source_target_pairs={{0,1},{1,0},{2,3},{3,2},{4,5},{5,4},{6,7},{7,6},{8,9},{9,8},{10,11... | collective-permute-start | bytes 983048 | tf_op jit(solution)/shard_map/ppermute | solution.py:317
  180.4 5.2 %collective-permute-start.2 = (f32[1024,128]{1,0:T(8,128)S(1)}, f32[1024,128]{1,0:T(8,128)S(1)}, u32[]{:S(2)}, u32[]{:S(2)}) collective-permute-start(f32[1024,128]{1,0:T(8,128)S(1)} %bitcast.18), channel_id=1, source_target_pairs={{0,1},{1,0},{2,3},{3,2},{4,5},{5,4},{6,7},{7,6},{8,9},{9,8},{10,11... | collective-permute-start | bytes 1572872 | tf_op jit(solution)/shard_map/ppermute | solution.py:333
  200.7 10.8 %all-to-all-start.9 = ((f32[8,32,512]{2,1,0:T(8,128)}), f32[8,32,512]{2,1,0:T(8,128)S(1)}, u32[]{:S(2)}, u32[]{:S(2)}) async-start(f32[8,32,512]{2,1,0:T(8,128)} %shard_map.60), calls=%async_computation.9 | async-start | bytes 1048576 | tf_op jit(solution)/shard_map/all_to_all | solution.py:253

commit v6 on v5

--- a/solution.py
+++ b/solution.py
@@ -17,8 +17,8 @@
 NEAR = ("gl", "gw")
 CLOSE = ("gl", "gw", "gc")
 FAR = ("gh", "gu", "gv")
-PLANE = ("gw", "gv")
-RING = ("gu", "gh", "gl")
+PLANE = ("gu", "gh", "gl", "gw")
+RING = ("gv",)
 
 highest = lax.Precision.HIGHEST
 NN = ((1,), (0,))

time: 216 us -> 217 us (level)
  no operation moved by 1% of the time
where the time goes in v6:
time: 217 us; the launch traced here: 214 us
  blocking collectives  172 us (79%)
  starting transfers between devices  16 us (7%)
  Pallas kernels  14.4 us (7%)
  waiting for transfers between devices  11.2 us (5%)
    all_to_all x9, blocking collectives, swap(): return lax.all_to_all(pieces, axes, split_axis=0, concat_axis=0, tiled=True)  172 us
    pallas_call x7, Pallas kernels, call(): pl.pallas_call(kernel, out_shape=out_shape, in_specs=[smem] * scalars + [...  14.4 us
    ppermute x2, starting transfers between devices, shards(): other = lax.ppermute(own, 'gc', exchange)  10.1 us
    all_to_all x1, waiting for transfers between devices, swap(): return lax.all_to_all(pieces, axes, split_axis=0, concat_axis=0, tiled=True)  7.18 us
  transfers between devices with their start and end apart: 4, of which 4 were waited for; matrix products, arithmetic and copies ran while one was open for 0% of the time, Pallas kernels for 0%

profile of v6, /device:TPU:1, one launch (start us, length us, event | category | flops | bytes accessed | tf_op | source)
XLA Modules:
  0.0 214.0 jit_solution(11068972046261288277)
XLA Ops:
  0.0 2.4 %shard_map.55 = (f32[2048,128]{1,0:T(8,128)S(1)}, f32[32,128]{1,0:T(8,128)S(1)}, f32[32,512]{1,0:T(8,128)S(1)}, f32[32,512]{1,0:T(8,128)S(1)}) custom-call(s32[32]{0:T(128)} %order_ref.1, s32[1]{0:T(128)} %bitcast.core_ref, f32[4,128,512]{2,1,0:T(8,128)} %bitcast.29, f32[32,128]{1,0:T(8,128)} %bitcast.32, f32[32,512]{1,0:T(8,128)} %bitcast.30, ...), custom_call_target="tpu_custom_call" | custom-call | tf_op jit(solution)/shard_map/pallas_call | solution.py:238
  2.5 54.3 %all_to_all.50 = f32[512,4,128]{2,1,0:T(4,128)S(1)} all-to-all(f32[512,4,128]{2,1,0:T(4,128)S(1)} %bitcast.23), channel_id=1, replica_groups=mesh['gu'=2,'gv'=8,'gh'=2,'gl'=2,'gw'=4,'gc'=2] {'gh','gl','gu','gv','gw..., dimensions={0} | all-to-all | bytes 2097152 | tf_op jit(solution)/shard_map/all_to_all | solution.py:253
  56.7 0.6 shard_map.56
  57.3 9.9 %all_to_all.51 = f32[16,8,128]{2,1,0:T(8,128)S(1)} all-to-all(f32[16,8,128]{2,1,0:T(8,128)S(1)} %bitcast.25), channel_id=1, replica_groups=mesh['gu'=2,'gv'=8,'gh'=2,'gl'=2,'gw'=4,'gc'=2] {'gl','gw','gc'}, dimensions={0} | all-to-all | bytes 131072 | tf_op jit(solution)/shard_map/all_to_all | solution.py:253
  67.2 16.9 %all_to_all.52 = f32[32,8,128]{2,1,0:T(8,128)S(1)} all-to-all(f32[32,8,128]{2,1,0:T(8,128)S(1)} %broadcast_in_dim.12), channel_id=1, replica_groups=mesh['gu'=2,'gv'=8,'gh'=2,'gl'=2,'gw'=4,'gc'=2] {'gh','gu','gv'}, dimensions={0} | all-to-all | bytes 262144 | tf_op jit(solution)/shard_map/all_to_all | solution.py:253
  84.1 10.5 %all_to_all.53 = f32[16,8,128]{2,1,0:T(8,128)S(1)} all-to-all(f32[16,8,128]{2,1,0:T(8,128)S(1)} %broadcast_in_dim.13), channel_id=1, replica_groups=mesh['gu'=2,'gv'=8,'gh'=2,'gl'=2,'gw'=4,'gc'=2] {'gl','gw','gc'}, dimensions={0} | all-to-all | bytes 131072 | tf_op jit(solution)/shard_map/all_to_all | solution.py:253
  94.6 3.1 %shard_map.57 = (f32[128,512]{1,0:T(8,128)S(1)}, f32[640,128]{1,0:T(8,128)S(1)}, f32[640,128]{1,0:T(8,128)S(1)}) custom-call(s32[1]{0:T(128)} %bitcast.core_ref, f32[128,128]{1,0:T(8,128)S(1)} %bitcast.24, f32[32,128]{1,0:T(8,128)S(1)} %get-tuple-element.17.start_ref, f32[2048,128]{1,0:T(8,128)S(1)} %bitcast.17), custom_call_target="tpu_custom_call" | custom-call | tf_op jit(solution)/shard_map/pallas_call | solution.py:238
  97.7 2.3 %collective-permute-start = (f32[640,128]{1,0:T(8,128)S(1)}, f32[640,128]{1,0:T(8,128)S(1)}, u32[]{:S(2)}, u32[]{:S(2)}) collective-permute-start(f32[640,128]{1,0:T(8,128)S(1)} %get-tuple-element.19), channel_id=1, source_target_pairs={{0,1},{1,0},{2,3},{3,2},{4,5},{5,4},{6,7},{7,6},{8,9},{9,8},{10,11... | collective-permute-start | bytes 983048 | tf_op jit(solution)/shard_map/ppermute | solution.py:312
  100.0 1.2 collective-permute-done
  101.3 15.8 %all_to_all.54 = f32[160,4,128]{2,1,0:T(4,128)S(1)} all-to-all(f32[160,4,128]{2,1,0:T(4,128)S(1)} %bitcast.28), channel_id=1, replica_groups=mesh['gu'=2,'gv'=8,'gh'=2,'gl'=2,'gw'=4,'gc'=2] {'gu','gh','gl','gw'}, dimensions={0} | all-to-all | bytes 655360 | tf_op jit(solution)/shard_map/all_to_all | solution.py:253
  117.1 0.1 reduce_sum.38
  117.2 9.8 %all_to_all.55 = f32[8,5,4,128]{3,2,1,0:T(4,128)S(1)} all-to-all(f32[8,5,4,128]{3,2,1,0:T(4,128)S(1)} %broadcast_in_dim.14), channel_id=1, replica_groups=mesh['gu'=2,'gv'=8,'gh'=2,'gl'=2,'gw'=4,'gc'=2] {'gv'}, dimensions={0} | all-to-all | bytes 163840 | tf_op jit(solution)/shard_map/all_to_all | solution.py:253
  127.0 15.3 %all_to_all.56 = f32[160,4,128]{2,1,0:T(4,128)S(1)} all-to-all(f32[160,4,128]{2,1,0:T(4,128)S(1)} %bitcast.27), channel_id=1, replica_groups=mesh['gu'=2,'gv'=8,'gh'=2,'gl'=2,'gw'=4,'gc'=2] {'gu','gh','gl','gw'}, dimensions={0} | all-to-all | bytes 655360 | tf_op jit(solution)/shard_map/all_to_all | solution.py:253
  142.3 6.5 %collective-permute-start.1 = (f32[640,128]{1,0:T(8,128)S(1)}, f32[640,128]{1,0:T(8,128)S(1)}, u32[]{:S(2)}, u32[]{:S(2)}) collective-permute-start(f32[640,128]{1,0:T(8,128)S(1)} %bitcast.21), channel_id=1, source_target_pairs={{0,1},{1,0},{2,3},{3,2},{4,5},{5,4},{6,7},{7,6},{8,9},{9,8},{10,11... | collective-permute-start | bytes 983048 | tf_op jit(solution)/shard_map/ppermute | solution.py:317
  148.9 1.2 collective-permute-done.1.other_ref
  150.1 3.3 %shard_map.58 = f32[2,2,16,16,128]{4,3,2,1,0:T(8,128)S(1)} custom-call(s32[1]{0:T(128)} %bitcast.core_ref, f32[640,128]{1,0:T(8,128)S(1)} %bitcast.22, f32[640,128]{1,0:T(8,128)S(1)} %collective-permute-done.1.other_ref, f32[32,512]{1,0:T(8,128)S(1)} %get-tuple-element.20.start_ref, f32[128,512]{1,0:T(8,128)S(1)} %get-tuple-element.21.merged_ref), custom_call_target="tpu_custom_call" | custom-call | tf_op jit(solution)/shard_map/pallas_call | solution.py:238
  153.4 27.7 %all_to_all.57 = f32[256,4,128]{2,1,0:T(4,128)S(1)} all-to-all(f32[256,4,128]{2,1,0:T(4,128)S(1)} %bitcast.20), channel_id=1, replica_groups=mesh['gu'=2,'gv'=8,'gh'=2,'gl'=2,'gw'=4,'gc'=2] {'gh','gl','gu','gv','gw'}, dimensions={0} | all-to-all | bytes 1048576 | tf_op jit(solution)/shard_map/all_to_all | solution.py:253
  181.1 3.6 %collective-permute-start.2 = (f32[1024,128]{1,0:T(8,128)S(1)}, f32[1024,128]{1,0:T(8,128)S(1)}, u32[]{:S(2)}, u32[]{:S(2)}) collective-permute-start(f32[1024,128]{1,0:T(8,128)S(1)} %bitcast.18), channel_id=1, source_target_pairs={{0,1},{1,0},{2,3},{3,2},{4,5},{5,4},{6,7},{7,6},{8,9},{9,8},{10,11... | collective-permute-start | bytes 1572872 | tf_op jit(solution)/shard_map/ppermute | solution.py:333
  184.7 1.5 collective-permute-done.2.other_ref
  186.2 0.7 shard_map.59
  186.9 11.9 %all_to_all.58.parts_ref = f32[8,32,512]{2,1,0:T(8,128)S(1)} all-to-all(f32[8,32,512]{2,1,0:T(8,128)S(1)} %get-tuple-element.22), channel_id=1, replica_groups=mesh['gu'=2,'gv'=8,'gh'=2,'gl'=2,'gw'=4,'gc'=2] {'gl','gw'}, dimensions={0} | all-to-all | bytes 1048576 | tf_op jit(solution)/shard_map/all_to_all | solution.py:253
  198.8 2.4 %shard_map.60 = f32[8,32,512]{2,1,0:T(8,128)} custom-call(f32[8,32,512]{2,1,0:T(8,128)S(1)} %all_to_all.58.parts_ref, bf16[512,512]{1,0:T(8,128)(2,1)S(1)} %get-tuple-element.23.high_ref, bf16[512,512]{1,0:T(8,128)(2,1)S(1)} %get-tuple-element.24.low_ref), custom_call_target="tpu_custom_call" | custom-call | tf_op jit(solution)/shard_map/pallas_call | solution.py:238
  201.3 3.6 %all-to-all-start.9 = ((f32[8,32,512]{2,1,0:T(8,128)}), f32[8,32,512]{2,1,0:T(8,128)S(1)}, u32[]{:S(2)}, u32[]{:S(2)}) async-start(f32[8,32,512]{2,1,0:T(8,128)} %shard_map.60), calls=%async_computation.9 | async-start | bytes 1048576 | tf_op jit(solution)/shard_map/all_to_all | solution.py:253
  204.9 7.2 %all-to-all-done.9.parts_ref = f32[8,32,512]{2,1,0:T(8,128)S(1)} async-done(((f32[8,32,512]{2,1,0:T(8,128)}), f32[8,32,512]{2,1,0:T(8,128)S(1)}, u32[]{:S(2)}, u32[]{:S(2)}) %all-to-all-start.9) | async-done | bytes 524320 | tf_op jit(solution)/shard_map/all_to_all | solution.py:253
  212.0 1.9 shard_map.61
  (8 shorter events, 0.2 us)
Async XLA Ops:
  97.7 3.6 %collective-permute-start = (f32[640,128]{1,0:T(8,128)S(1)}, f32[640,128]{1,0:T(8,128)S(1)}, u32[]{:S(2)}, u32[]{:S(2)}) collective-permute-start(f32[640,128]{1,0:T(8,128)S(1)} %get-tuple-element.19), channel_id=1, source_target_pairs={{0,1},{1,0},{2,3},{3,2},{4,5},{5,4},{6,7},{7,6},{8,9},{9,8},{10,11... | collective-permute-start | bytes 983048 | tf_op jit(solution)/shard_map/ppermute | solution.py:312
  142.3 7.8 %collective-permute-start.1 = (f32[640,128]{1,0:T(8,128)S(1)}, f32[640,128]{1,0:T(8,128)S(1)}, u32[]{:S(2)}, u32[]{:S(2)}) collective-permute-start(f32[640,128]{1,0:T(8,128)S(1)} %bitcast.21), channel_id=1, source_target_pairs={{0,1},{1,0},{2,3},{3,2},{4,5},{5,4},{6,7},{7,6},{8,9},{9,8},{10,11... | collective-permute-start | bytes 983048 | tf_op jit(solution)/shard_map/ppermute | solution.py:317
  181.1 5.1 %collective-permute-start.2 = (f32[1024,128]{1,0:T(8,128)S(1)}, f32[1024,128]{1,0:T(8,128)S(1)}, u32[]{:S(2)}, u32[]{:S(2)}) collective-permute-start(f32[1024,128]{1,0:T(8,128)S(1)} %bitcast.18), channel_id=1, source_target_pairs={{0,1},{1,0},{2,3},{3,2},{4,5},{5,4},{6,7},{7,6},{8,9},{9,8},{10,11... | collective-permute-start | bytes 1572872 | tf_op jit(solution)/shard_map/ppermute | solution.py:333
  201.3 10.8 %all-to-all-start.9 = ((f32[8,32,512]{2,1,0:T(8,128)}), f32[8,32,512]{2,1,0:T(8,128)S(1)}, u32[]{:S(2)}, u32[]{:S(2)}) async-start(f32[8,32,512]{2,1,0:T(8,128)} %shard_map.60), calls=%async_computation.9 | async-start | bytes 1048576 | tf_op jit(solution)/shard_map/all_to_all | solution.py:253

commit v7 on v6

--- a/solution.py
+++ b/solution.py
@@ -11,14 +11,14 @@
 LANES = 128
 PANEL = 16
 VMEM_BYTES = 20 << 20
-FINE = ("gu", "gv", "gh", "gl", "gw", "gc")
-CHIPS = ("gh", "gl", "gu", "gv", "gw")
+FINE = ("gu", "gv", "gk", "gh", "gl", "gw", "gc")
+CHIPS = ("gh", "gl", "gu", "gv", "gk", "gw")
 ORDER = CHIPS + ("gc",)
 NEAR = ("gl", "gw")
 CLOSE = ("gl", "gw", "gc")
-FAR = ("gh", "gu", "gv")
-PLANE = ("gu", "gh", "gl", "gw")
-RING = ("gv",)
+FAR = ("gh", "gu", "gv", "gk")
+BLOCK = ("gk", "gl", "gw")
+BEYOND = ("gu", "gh", "gv")
 
 highest = lax.Precision.HIGHEST
 NN = ((1,), (0,))
@@ -310,17 +310,16 @@
         scalars=1,
     )
     gram = kept + lax.ppermute(sent, "gc", exchange)
-    plane = lax.axis_size(PLANE)
-    gram = jnp.sum(swap(gram.reshape(-1, 4, LANES), PLANE).reshape(plane, -1, 4, LANES), axis=0)
-    gram = jnp.sum(swap(copies(gram, RING), RING), axis=0)
-    own = swap(copies(gram, PLANE).reshape(-1, 4, LANES), PLANE).reshape(-1, LANES)
+    gram = jnp.sum(swap(gram.reshape(lax.axis_size(BLOCK), -1, LANES), BLOCK), axis=0)
+    gram = jnp.sum(swap(copies(gram, BEYOND), BEYOND), axis=0)
+    own = swap(copies(gram, BLOCK), BLOCK).reshape(-1, LANES)
     other = lax.ppermute(own, "gc", exchange)
 
     near = lax.axis_size("gl")
     row_groups = lax.axis_size("gw") * 4
     sent = call(
         functools.partial(third_kernel, parts=parts_y),
-        vm(lax.axis_size("gh"), near, lax.axis_size(("gu", "gv")), row_groups, LANES),
+        vm(lax.axis_size("gh"), near, lax.axis_size(("gu", "gv", "gk")), row_groups, LANES),
         core,
         own,
         other,
@@ -343,7 +342,7 @@
     )
     for repeat in range(ITERS - 1):
         pieces = call(step_third_kernel, spread_shape, swap(pieces, NEAR), high, low)
-    gx = lax.axis_index(("gu", "gv"))
+    gx = lax.axis_index(("gu", "gv", "gk"))
     at = ((gx // 4) * 16 + (gx % 4) * 2 + lax.axis_index("gh")).astype(jnp.int32).reshape(1)
     return call(
         functools.partial(core_kernel, parts=4),
@@ -360,7 +359,7 @@
 
 def solution(mesh):
     gx, gy, gz = mesh.devices.shape
-    fine = Mesh(mesh.devices.reshape(2, gx // 2, 2, gy // 2, gz // 2, 2), FINE)
-    in_specs = (P(None, ("gu", "gv", "gw", "gc"), ("gh", "gl"), None), P(), P(), P(), P())
-    out_specs = P(("gu", "gv", "gh", "gl"), ("gw", "gc"), None)
+    fine = Mesh(mesh.devices.reshape(2, gx // 4, 2, 2, gy // 2, gz // 2, 2), FINE)
+    in_specs = (P(None, ("gu", "gv", "gk", "gw", "gc"), ("gh", "gl"), None), P(), P(), P(), P())
+    out_specs = P(("gu", "gv", "gk", "gh", "gl"), ("gw", "gc"), None)
     return jax.shard_map(shards, mesh=fine, in_specs=in_specs, out_specs=out_specs, check_vma=False)

time: 217 us -> 214 us (0.986)
  no operation moved by 1% of the time
where the time goes in v7:
time: 214 us; the launch traced here: 211 us
  blocking collectives  171 us (80%)
  Pallas kernels  14.4 us (7%)
  starting transfers between devices  14.3 us (7%)
  waiting for transfers between devices  11.2 us (5%)
    all_to_all x9, blocking collectives, swap(): return lax.all_to_all(pieces, axes, split_axis=0, concat_axis=0, tiled=True)  171 us
    pallas_call x7, Pallas kernels, call(): pl.pallas_call(kernel, out_shape=out_shape, in_specs=[smem] * scalars + [...  14.4 us
    ppermute x2, starting transfers between devices, shards(): other = lax.ppermute(own, 'gc', exchange)  8.36 us
    all_to_all x1, waiting for transfers between devices, swap(): return lax.all_to_all(pieces, axes, split_axis=0, concat_axis=0, tiled=True)  7.18 us
  transfers between devices with their start and end apart: 4, of which 4 were waited for; matrix products, arithmetic and copies ran while one was open for 0% of the time, Pallas kernels for 0%

profile of v7, /device:TPU:1, one launch (start us, length us, event | category | flops | bytes accessed | tf_op | source)
XLA Modules:
  0.0 211.0 jit_solution(17775925061231114958)
XLA Ops:
  0.0 2.5 %shard_map.55 = (f32[2048,128]{1,0:T(8,128)S(1)}, f32[32,128]{1,0:T(8,128)S(1)}, f32[32,512]{1,0:T(8,128)S(1)}, f32[32,512]{1,0:T(8,128)S(1)}) custom-call(s32[32]{0:T(128)} %order_ref.1, s32[1]{0:T(128)} %bitcast.core_ref, f32[4,128,512]{2,1,0:T(8,128)} %bitcast.25, f32[32,128]{1,0:T(8,128)} %bitcast.28, f32[32,512]{1,0:T(8,128)} %bitcast.26, ...), custom_call_target="tpu_custom_call" | custom-call | tf_op jit(solution)/shard_map/pallas_call | solution.py:238
  2.5 54.3 %all_to_all.50 = f32[512,4,128]{2,1,0:T(4,128)S(1)} all-to-all(f32[512,4,128]{2,1,0:T(4,128)S(1)} %bitcast.21), channel_id=1, replica_groups=mesh['gu'=2,'gv'=4,'gk'=2,'gh'=2,'gl'=2,'gw'=4,'gc'=2] {'gh','gl','gu','..., dimensions={0} | all-to-all | bytes 2097152 | tf_op jit(solution)/shard_map/all_to_all | solution.py:253
  56.7 0.6 shard_map.56
  57.3 9.9 %all_to_all.51 = f32[16,8,128]{2,1,0:T(8,128)S(1)} all-to-all(f32[16,8,128]{2,1,0:T(8,128)S(1)} %bitcast.23), channel_id=1, replica_groups=mesh['gu'=2,'gv'=4,'gk'=2,'gh'=2,'gl'=2,'gw'=4,'gc'=2] {'gl','gw','gc'}, dimensions={0} | all-to-all | bytes 131072 | tf_op jit(solution)/shard_map/all_to_all | solution.py:253
  67.2 16.9 %all_to_all.52 = f32[32,8,128]{2,1,0:T(8,128)S(1)} all-to-all(f32[32,8,128]{2,1,0:T(8,128)S(1)} %broadcast_in_dim.12), channel_id=1, replica_groups=mesh['gu'=2,'gv'=4,'gk'=2,'gh'=2,'gl'=2,'gw'=4,'gc'=2] {'gh','gu','gv','..., dimensions={0} | all-to-all | bytes 262144 | tf_op jit(solution)/shard_map/all_to_all | solution.py:253
  84.1 10.5 %all_to_all.53 = f32[16,8,128]{2,1,0:T(8,128)S(1)} all-to-all(f32[16,8,128]{2,1,0:T(8,128)S(1)} %broadcast_in_dim.13), channel_id=1, replica_groups=mesh['gu'=2,'gv'=4,'gk'=2,'gh'=2,'gl'=2,'gw'=4,'gc'=2] {'gl','gw','gc'}, dimensions={0} | all-to-all | bytes 131072 | tf_op jit(solution)/shard_map/all_to_all | solution.py:253
  94.6 3.1 %shard_map.57 = (f32[128,512]{1,0:T(8,128)S(1)}, f32[640,128]{1,0:T(8,128)S(1)}, f32[640,128]{1,0:T(8,128)S(1)}) custom-call(s32[1]{0:T(128)} %bitcast.core_ref, f32[128,128]{1,0:T(8,128)S(1)} %bitcast.22, f32[32,128]{1,0:T(8,128)S(1)} %get-tuple-element.17.start_ref, f32[2048,128]{1,0:T(8,128)S(1)} %bitcast.15), custom_call_target="tpu_custom_call" | custom-call | tf_op jit(solution)/shard_map/pallas_call | solution.py:238
  97.7 2.3 %collective-permute-start = (f32[640,128]{1,0:T(8,128)S(1)}, f32[640,128]{1,0:T(8,128)S(1)}, u32[]{:S(2)}, u32[]{:S(2)}) collective-permute-start(f32[640,128]{1,0:T(8,128)S(1)} %get-tuple-element.19), channel_id=1, source_target_pairs={{0,1},{1,0},{2,3},{3,2},{4,5},{5,4},{6,7},{7,6},{8,9},{9,8},{10,11... | collective-permute-start | bytes 983048 | tf_op jit(solution)/shard_map/ppermute | solution.py:312
  100.0 1.2 collective-permute-done
  101.3 11.1 %all_to_all.54 = f32[16,40,128]{2,1,0:T(8,128)S(1)} all-to-all(f32[16,40,128]{2,1,0:T(8,128)S(1)} %bitcast.24), channel_id=1, replica_groups=mesh['gu'=2,'gv'=4,'gk'=2,'gh'=2,'gl'=2,'gw'=4,'gc'=2] {'gk','gl','gw'}, dimensions={0} | all-to-all | bytes 655360 | tf_op jit(solution)/shard_map/all_to_all | solution.py:253
  112.5 17.6 %all_to_all.55 = f32[16,40,128]{2,1,0:T(8,128)S(1)} all-to-all(f32[16,40,128]{2,1,0:T(8,128)S(1)} %broadcast_in_dim.14), channel_id=1, replica_groups=mesh['gu'=2,'gv'=4,'gk'=2,'gh'=2,'gl'=2,'gw'=4,'gc'=2] {'gu','gh','gv'}, dimensions={0} | all-to-all | bytes 655360 | tf_op jit(solution)/shard_map/all_to_all | solution.py:253
  130.1 10.8 %all_to_all.56 = f32[16,40,128]{2,1,0:T(8,128)S(1)} all-to-all(f32[16,40,128]{2,1,0:T(8,128)S(1)} %broadcast_in_dim.15), channel_id=1, replica_groups=mesh['gu'=2,'gv'=4,'gk'=2,'gh'=2,'gl'=2,'gw'=4,'gc'=2] {'gk','gl','gw'}, dimensions={0} | all-to-all | bytes 655360 | tf_op jit(solution)/shard_map/all_to_all | solution.py:253
  141.0 4.4 %collective-permute-start.1 = (f32[640,128]{1,0:T(8,128)S(1)}, f32[640,128]{1,0:T(8,128)S(1)}, u32[]{:S(2)}, u32[]{:S(2)}) collective-permute-start(f32[640,128]{1,0:T(8,128)S(1)} %bitcast.19), channel_id=1, source_target_pairs={{0,1},{1,0},{2,3},{3,2},{4,5},{5,4},{6,7},{7,6},{8,9},{9,8},{10,11... | collective-permute-start | bytes 983048 | tf_op jit(solution)/shard_map/ppermute | solution.py:316
  145.4 1.2 collective-permute-done.1.other_ref
  146.6 3.3 %shard_map.58 = f32[2,2,16,16,128]{4,3,2,1,0:T(8,128)S(1)} custom-call(s32[1]{0:T(128)} %bitcast.core_ref, f32[640,128]{1,0:T(8,128)S(1)} %bitcast.20, f32[640,128]{1,0:T(8,128)S(1)} %collective-permute-done.1.other_ref, f32[32,512]{1,0:T(8,128)S(1)} %get-tuple-element.20.start_ref, f32[128,512]{1,0:T(8,128)S(1)} %get-tuple-element.21.merged_ref), custom_call_target="tpu_custom_call" | custom-call | tf_op jit(solution)/shard_map/pallas_call | solution.py:238
  149.9 27.9 %all_to_all.57 = f32[256,4,128]{2,1,0:T(4,128)S(1)} all-to-all(f32[256,4,128]{2,1,0:T(4,128)S(1)} %bitcast.18), channel_id=1, replica_groups=mesh['gu'=2,'gv'=4,'gk'=2,'gh'=2,'gl'=2,'gw'=4,'gc'=2] {'gh','gl','gu','..., dimensions={0} | all-to-all | bytes 1048576 | tf_op jit(solution)/shard_map/all_to_all | solution.py:253
  177.8 4.0 %collective-permute-start.2 = (f32[1024,128]{1,0:T(8,128)S(1)}, f32[1024,128]{1,0:T(8,128)S(1)}, u32[]{:S(2)}, u32[]{:S(2)}) collective-permute-start(f32[1024,128]{1,0:T(8,128)S(1)} %bitcast.16), channel_id=1, source_target_pairs={{0,1},{1,0},{2,3},{3,2},{4,5},{5,4},{6,7},{7,6},{8,9},{9,8},{10,11... | collective-permute-start | bytes 1572872 | tf_op jit(solution)/shard_map/ppermute | solution.py:332
  181.8 1.5 collective-permute-done.2.other_ref
  183.3 0.7 shard_map.59
  184.0 11.9 %all_to_all.58.parts_ref = f32[8,32,512]{2,1,0:T(8,128)S(1)} all-to-all(f32[8,32,512]{2,1,0:T(8,128)S(1)} %get-tuple-element.22), channel_id=1, replica_groups=mesh['gu'=2,'gv'=4,'gk'=2,'gh'=2,'gl'=2,'gw'=4,'gc'=2] {'gl','gw'}, dimensions={0} | all-to-all | bytes 1048576 | tf_op jit(solution)/shard_map/all_to_all | solution.py:253
  195.9 2.4 %shard_map.60 = f32[8,32,512]{2,1,0:T(8,128)} custom-call(f32[8,32,512]{2,1,0:T(8,128)S(1)} %all_to_all.58.parts_ref, bf16[512,512]{1,0:T(8,128)(2,1)S(1)} %get-tuple-element.23.high_ref, bf16[512,512]{1,0:T(8,128)(2,1)S(1)} %get-tuple-element.24.low_ref), custom_call_target="tpu_custom_call" | custom-call | tf_op jit(solution)/shard_map/pallas_call | solution.py:238
  198.3 3.6 %all-to-all-start.9 = ((f32[8,32,512]{2,1,0:T(8,128)}), f32[8,32,512]{2,1,0:T(8,128)S(1)}, u32[]{:S(2)}, u32[]{:S(2)}) async-start(f32[8,32,512]{2,1,0:T(8,128)} %shard_map.60), calls=%async_computation.9 | async-start | bytes 1048576 | tf_op jit(solution)/shard_map/all_to_all | solution.py:253
  201.9 7.2 %all-to-all-done.9.parts_ref = f32[8,32,512]{2,1,0:T(8,128)S(1)} async-done(((f32[8,32,512]{2,1,0:T(8,128)}), f32[8,32,512]{2,1,0:T(8,128)S(1)}, u32[]{:S(2)}, u32[]{:S(2)}) %all-to-all-start.9) | async-done | bytes 524320 | tf_op jit(solution)/shard_map/all_to_all | solution.py:253
  209.1 1.9 shard_map.61
  (9 shorter events, 0.2 us)
Async XLA Ops:
  97.7 3.6 %collective-permute-start = (f32[640,128]{1,0:T(8,128)S(1)}, f32[640,128]{1,0:T(8,128)S(1)}, u32[]{:S(2)}, u32[]{:S(2)}) collective-permute-start(f32[640,128]{1,0:T(8,128)S(1)} %get-tuple-element.19), channel_id=1, source_target_pairs={{0,1},{1,0},{2,3},{3,2},{4,5},{5,4},{6,7},{7,6},{8,9},{9,8},{10,11... | collective-permute-start | bytes 983048 | tf_op jit(solution)/shard_map/ppermute | solution.py:312
  141.0 5.6 %collective-permute-start.1 = (f32[640,128]{1,0:T(8,128)S(1)}, f32[640,128]{1,0:T(8,128)S(1)}, u32[]{:S(2)}, u32[]{:S(2)}) collective-permute-start(f32[640,128]{1,0:T(8,128)S(1)} %bitcast.19), channel_id=1, source_target_pairs={{0,1},{1,0},{2,3},{3,2},{4,5},{5,4},{6,7},{7,6},{8,9},{9,8},{10,11... | collective-permute-start | bytes 983048 | tf_op jit(solution)/shard_map/ppermute | solution.py:316
  177.8 5.5 %collective-permute-start.2 = (f32[1024,128]{1,0:T(8,128)S(1)}, f32[1024,128]{1,0:T(8,128)S(1)}, u32[]{:S(2)}, u32[]{:S(2)}) collective-permute-start(f32[1024,128]{1,0:T(8,128)S(1)} %bitcast.16), channel_id=1, source_target_pairs={{0,1},{1,0},{2,3},{3,2},{4,5},{5,4},{6,7},{7,6},{8,9},{9,8},{10,11... | collective-permute-start | bytes 1572872 | tf_op jit(solution)/shard_map/ppermute | solution.py:332
  198.3 10.8 %all-to-all-start.9 = ((f32[8,32,512]{2,1,0:T(8,128)}), f32[8,32,512]{2,1,0:T(8,128)S(1)}, u32[]{:S(2)}, u32[]{:S(2)}) async-start(f32[8,32,512]{2,1,0:T(8,128)} %shard_map.60), calls=%async_computation.9 | async-start | bytes 1048576 | tf_op jit(solution)/shard_map/all_to_all | solution.py:253

commit v8 on v7

--- a/solution.py
+++ b/solution.py
@@ -11,13 +11,13 @@
 LANES = 128
 PANEL = 16
 VMEM_BYTES = 20 << 20
-FINE = ("gu", "gv", "gk", "gh", "gl", "gw", "gc")
-CHIPS = ("gh", "gl", "gu", "gv", "gk", "gw")
+FINE = ("gu", "gv", "gk", "gh", "gl", "gw", "gp", "gc")
+CHIPS = ("gh", "gl", "gu", "gv", "gk", "gw", "gp")
 ORDER = CHIPS + ("gc",)
-NEAR = ("gl", "gw")
-CLOSE = ("gl", "gw", "gc")
+NEAR = ("gl", "gk", "gp")
+CLOSE = ("gl", "gw", "gp", "gc")
 FAR = ("gh", "gu", "gv", "gk")
-BLOCK = ("gk", "gl", "gw")
+BLOCK = ("gk", "gl", "gw", "gp")
 BEYOND = ("gu", "gh", "gv")
 
 highest = lax.Precision.HIGHEST
@@ -90,7 +90,7 @@
     for b in range(cells_z // brick_len):
         at = pl.multiple_of(order_ref[b] * brick_len, brick_len)
         placed_ref[b * brick_len : (b + 1) * brick_len, :] = rows_ref[pl.ds(at, brick_len), :]
-    core = core_ref[0]
+    core = (core_ref[0] & 1)
     half = cells_z // 2
     third_ref[:, :half] = placed_ref[pl.ds(core, half, stride=2), :].T
     third_ref[:, half:] = placed_ref[pl.ds(1 - core, half, stride=2), :].T
@@ -127,12 +127,15 @@
         current = orthonormal_rows(mm(current, gram, NN))
     rank = current.shape[0]
     rows_ref[...] = current
-    current = halves(jnp.concatenate([rows_ref[pl.ds(i, rank // 4, stride=4), :] for i in range(4)], axis=0))
-    half = rank // 2
+    quarter = rank // 4
+    order = [r for c in range(4) for r in range(rank) if (r >> 3 & 1) * 2 + (r >> 1 & 1) == c]
+    current = halves(jnp.concatenate([rows_ref[r : r + 1, :] for r in order], axis=0))
     for s in range(species):
         product = mm3(current, halves(fibre(data_ref, s, species, rows_x, parts)), NN)
-        merged_ref[s * half : (s + 1) * half, :] = product[:half]
-        merged_ref[(species + s) * half : (species + s + 1) * half, :] = product[half:]
+        for c in range(4):
+            merged_ref[(c * species + s) * quarter : (c * species + s + 1) * quarter, :] = product[
+                c * quarter : (c + 1) * quarter
+            ]
     merged = merged_ref[...]
     flipped = halves(merged.T)
     merged = halves(merged)
@@ -144,8 +147,8 @@
     count = len(blocks) // 2
     for i in range(count):
         rows = slice(i * LANES, (i + 1) * LANES)
-        kept_ref[rows, :] = jnp.where(core_ref[0] == 0, blocks[i], blocks[count + i])
-        sent_ref[rows, :] = jnp.where(core_ref[0] == 0, blocks[count + i], blocks[i])
+        kept_ref[rows, :] = jnp.where((core_ref[0] & 1) == 0, blocks[i], blocks[count + i])
+        sent_ref[rows, :] = jnp.where((core_ref[0] & 1) == 0, blocks[count + i], blocks[i])
 
 
 def symmetric_of(core, own_ref, other_ref, parts):
@@ -164,22 +167,26 @@
 
 
 def third_kernel(core_ref, own_ref, other_ref, start_ref, merged_ref, out_ref, rows_ref, *, parts):
-    gram = halves(symmetric_of(core_ref[0], own_ref, other_ref, parts))
+    gram = halves(symmetric_of((core_ref[0] & 1), own_ref, other_ref, parts))
     current = start_ref[...]
     for repeat in range(ITERS):
         current = orthonormal_rows(mm3(halves(current), gram, NN))
     rows_ref[...] = mm(current, merged_ref[...], NT)
-    rank = rows_ref.shape[0]
-    even = rows_ref[pl.ds(0, rank // 2, stride=2), :]
-    odd = rows_ref[pl.ds(1, rank // 2, stride=2), :]
-    low = lax.broadcasted_iota(jnp.int32, even.shape, 1) < LANES // 2
-    first = jnp.where(low, even, pltpu.roll(odd, LANES // 2, 1))
-    second = jnp.where(low, pltpu.roll(even, LANES // 2, 1), odd)
-    per_low = out_ref.shape[2]
-    for h in range(out_ref.shape[0]):
-        for i in range(per_low):
-            out_ref[h, 0, i] = first
-            out_ref[h, 1, i] = second
+    quarter = LANES // 4
+    groups = [rows_ref[pl.ds(e, rows_ref.shape[0] // 4, stride=4), :] for e in range(4)]
+    group_id = lax.broadcasted_iota(jnp.int32, groups[0].shape, 1) // quarter
+    for k in range(out_ref.shape[3]):
+        for h in range(out_ref.shape[1]):
+            c = k * 2 + h
+            piece = pltpu.roll(groups[0], (4 - c) % 4 * quarter, 1) if c else groups[0]
+            for e in range(1, 4):
+                shift = (e - c) % 4 * quarter
+                piece = jnp.where(group_id == e, pltpu.roll(groups[e], shift, 1) if shift else groups[e], piece)
+            piece = jnp.concatenate([piece[0:2], piece[4:6], piece[2:4], piece[6:8]], axis=0)
+            for i in range(out_ref.shape[0]):
+                for j in range(out_ref.shape[2]):
+                    for w in range(out_ref.shape[4]):
+                        out_ref[i, h, j, k, w] = piece
 
 
 def columns_of(own_ref, other_ref, parts):
@@ -219,15 +226,15 @@
     spread(out_ref, mm3(halves(inner), data, NT))
 
 
-def core_kernel(core_ref, at_ref, parts_ref, high_ref, low_ref, out_ref, rows_ref, *, parts):
+def core_kernel(place_ref, parts_ref, high_ref, low_ref, out_ref, rows_ref):
     current = halves(orthonormal_rows(total_of(parts_ref)))
-    here = parts // 2
-    for jj in range(here):
-        cut = pl.ds(pl.multiple_of((core_ref[0] * here + jj) * LANES, LANES), LANES)
-        rows_ref[...] = mm3(current, (high_ref[:, cut], low_ref[:, cut]), NN).T
-        for e in range(2):
-            for b in range(out_ref.shape[0]):
-                out_ref[b, 2 * jj + e, :] = rows_ref[at_ref[0] + e * (LANES // 2) + 8 * b, :]
+    block = (place_ref[0] >> 1 & 1) * 2 + (place_ref[0] & 1)
+    cut = pl.ds(pl.multiple_of(block * LANES, LANES), LANES)
+    rows_ref[...] = mm3(current, (high_ref[:, cut], low_ref[:, cut]), NN).T
+    at = place_ref[0] >> 2
+    for e in range(out_ref.shape[1]):
+        for b in range(out_ref.shape[0]):
+            out_ref[b, e, :] = rows_ref[at + e * (LANES // 4) + b, :]
 
 
 def call(kernel, out_shape, *args, scratch=(), scalars=0, in_hbm=0):
@@ -267,7 +274,9 @@
     devices = lax.axis_size(ORDER)
     chips = lax.axis_size(CHIPS)
     parts_y = full_y // LANES
-    core = lax.axis_index("gc").astype(jnp.int32).reshape(1)
+    gx = lax.axis_index(("gu", "gv", "gk"))
+    row = (gx >> 2) * 8 + (gx >> 1 & 1) * 4 + lax.axis_index("gh") * 2
+    core = (row * 4 + lax.axis_index("gw") * 2 + lax.axis_index("gc")).astype(jnp.int32).reshape(1)
     exchange = [(0, 1), (1, 0)]
 
     sent, start_first, start_second, start_third = call(
@@ -315,11 +324,9 @@
     own = swap(copies(gram, BLOCK), BLOCK).reshape(-1, LANES)
     other = lax.ppermute(own, "gc", exchange)
 
-    near = lax.axis_size("gl")
-    row_groups = lax.axis_size("gw") * 4
     sent = call(
         functools.partial(third_kernel, parts=parts_y),
-        vm(lax.axis_size("gh"), near, lax.axis_size(("gu", "gv", "gk")), row_groups, LANES),
+        vm(lax.axis_size("gh"), lax.axis_size("gl"), lax.axis_size(("gu", "gv")), lax.axis_size("gk"), 2, 8, LANES),
         core,
         own,
         other,
@@ -342,24 +349,21 @@
     )
     for repeat in range(ITERS - 1):
         pieces = call(step_third_kernel, spread_shape, swap(pieces, NEAR), high, low)
-    gx = lax.axis_index(("gu", "gv", "gk"))
-    at = ((gx // 4) * 16 + (gx % 4) * 2 + lax.axis_index("gh")).astype(jnp.int32).reshape(1)
     return call(
-        functools.partial(core_kernel, parts=4),
+        core_kernel,
         jax.ShapeDtypeStruct((2, 4, rank_three), jnp.float32),
         core,
-        at,
         swap(pieces, NEAR),
         high,
         low,
         scratch=[(merged_rows, rank_three)],
-        scalars=2,
+        scalars=1,
     )
 
 
 def solution(mesh):
     gx, gy, gz = mesh.devices.shape
-    fine = Mesh(mesh.devices.reshape(2, gx // 4, 2, 2, gy // 2, gz // 2, 2), FINE)
-    in_specs = (P(None, ("gu", "gv", "gk", "gw", "gc"), ("gh", "gl"), None), P(), P(), P(), P())
-    out_specs = P(("gu", "gv", "gk", "gh", "gl"), ("gw", "gc"), None)
+    fine = Mesh(mesh.devices.reshape(2, gx // 4, 2, 2, gy // 2, gz // 4, 2, 2), FINE)
+    in_specs = (P(None, ("gu", "gv", "gk", "gw", "gp", "gc"), ("gh", "gl"), None), P(), P(), P(), P())
+    out_specs = P(("gu", "gv", "gk", "gh", "gl"), ("gw", "gp", "gc"), None)
     return jax.shard_map(shards, mesh=fine, in_specs=in_specs, out_specs=out_specs, check_vma=False)

time: 214 us -> 211 us (0.986)
  blocking collectives: 171 us -> 180 us
  waiting for transfers between devices: 11.2 us -> 3.98 us
  starting transfers between devices: 14.3 us -> 10.7 us
    all_to_all x9 -> x10, blocking collectives: 171 us -> 180 us  [swap(): return lax.all_to_all(pieces, axes, split_axis=0, concat_axis=0, tiled=True)]
    all_to_all x1 -> x0, waiting for transfers between devices: 7.18 us -> none  [swap(): return lax.all_to_all(pieces, axes, split_axis=0, concat_axis=0, tiled=True)]
    all_to_all x1 -> x0, starting transfers between devices: 3.59 us -> none  [swap(): return lax.all_to_all(pieces, axes, split_axis=0, concat_axis=0, tiled=True)]
  transfers between devices with their start and end apart: 4 -> 3, of which waited for: 4 -> 3; matrix products, arithmetic and copies ran while one was open for 0% -> 0% of each run, Pallas kernels for 0% -> 0%
where the time goes in v8:
time: 211 us; the launch traced here: 208 us
  blocking collectives  180 us (85%)
  Pallas kernels  13.6 us (6%)
  starting transfers between devices  10.7 us (5%)
  waiting for transfers between devices  3.98 us (2%)
    all_to_all x10, blocking collectives, swap(): return lax.all_to_all(pieces, axes, split_axis=0, concat_axis=0, tiled=True)  180 us
    pallas_call x7, Pallas kernels, call(): pl.pallas_call(kernel, out_shape=out_shape, in_specs=[smem] * scalars + [...  13.6 us
    ppermute x2, starting transfers between devices, shards(): other = lax.ppermute(own, 'gc', exchange)  8.36 us
  transfers between devices with their start and end apart: 3, of which 3 were waited for; matrix products, arithmetic and copies ran while one was open for 0% of the time, Pallas kernels for 0%

profile of v8, /device:TPU:1, one launch (start us, length us, event | category | flops | bytes accessed | tf_op | source)
XLA Modules:
  0.0 208.4 jit_solution(14102670670381937071)
XLA Ops:
  0.0 2.5 %shard_map.55 = (f32[2048,128]{1,0:T(8,128)S(1)}, f32[32,128]{1,0:T(8,128)S(1)}, f32[32,512]{1,0:T(8,128)S(1)}, f32[32,512]{1,0:T(8,128)S(1)}) custom-call(s32[32]{0:T(128)} %order_ref.1, s32[1]{0:T(128)} %bitcast.core_ref.place_ref, f32[4,128,512]{2,1,0:T(8,128)} %bitcast.24, f32[32,128]{1,0:T(8,128)} %bitcast.27, f32[32,512]{1,0:T(8,128)} %bitcast.25, ...), custom_call_target="tpu_custom_call" | custom-call | tf_op jit(solution)/shard_map/pallas_call | solution.py:245
  2.5 54.3 %all_to_all.50 = f32[512,4,128]{2,1,0:T(4,128)S(1)} all-to-all(f32[512,4,128]{2,1,0:T(4,128)S(1)} %bitcast.20), channel_id=1, replica_groups=mesh['gu'=2,'gv'=4,'gk'=2,'gh'=2,'gl'=2,'gw'=2,'gp'=2,'gc'=2] {'gh','gl'..., dimensions={0} | all-to-all | bytes 2097152 | tf_op jit(solution)/shard_map/all_to_all | solution.py:260
  56.7 0.6 shard_map.56
  57.3 9.9 %all_to_all.51 = f32[16,8,128]{2,1,0:T(8,128)S(1)} all-to-all(f32[16,8,128]{2,1,0:T(8,128)S(1)} %bitcast.22), channel_id=1, replica_groups=mesh['gu'=2,'gv'=4,'gk'=2,'gh'=2,'gl'=2,'gw'=2,'gp'=2,'gc'=2] {'gl','gw'..., dimensions={0} | all-to-all | bytes 131072 | tf_op jit(solution)/shard_map/all_to_all | solution.py:260
  67.2 16.9 %all_to_all.52 = f32[32,8,128]{2,1,0:T(8,128)S(1)} all-to-all(f32[32,8,128]{2,1,0:T(8,128)S(1)} %broadcast_in_dim.12), channel_id=1, replica_groups=mesh['gu'=2,'gv'=4,'gk'=2,'gh'=2,'gl'=2,'gw'=2,'gp'=2,'gc'=2] {'gh','gu'..., dimensions={0} | all-to-all | bytes 262144 | tf_op jit(solution)/shard_map/all_to_all | solution.py:260
  84.1 10.5 %all_to_all.53 = f32[16,8,128]{2,1,0:T(8,128)S(1)} all-to-all(f32[16,8,128]{2,1,0:T(8,128)S(1)} %broadcast_in_dim.13), channel_id=1, replica_groups=mesh['gu'=2,'gv'=4,'gk'=2,'gh'=2,'gl'=2,'gw'=2,'gp'=2,'gc'=2] {'gl','gw'..., dimensions={0} | all-to-all | bytes 131072 | tf_op jit(solution)/shard_map/all_to_all | solution.py:260
  94.6 3.1 %shard_map.57 = (f32[128,512]{1,0:T(8,128)S(1)}, f32[640,128]{1,0:T(8,128)S(1)}, f32[640,128]{1,0:T(8,128)S(1)}) custom-call(s32[1]{0:T(128)} %bitcast.core_ref.place_ref, f32[128,128]{1,0:T(8,128)S(1)} %bitcast.21, f32[32,128]{1,0:T(8,128)S(1)} %get-tuple-element.17.start_ref, f32[2048,128]{1,0:T(8,128)S(1)} %bitcast.14), custom_call_target="tpu_custom_call" | custom-call | tf_op jit(solution)/shard_map/pallas_call | solution.py:245
  97.7 2.3 %collective-permute-start = (f32[640,128]{1,0:T(8,128)S(1)}, f32[640,128]{1,0:T(8,128)S(1)}, u32[]{:S(2)}, u32[]{:S(2)}) collective-permute-start(f32[640,128]{1,0:T(8,128)S(1)} %get-tuple-element.19), channel_id=1, source_target_pairs={{0,1},{1,0},{2,3},{3,2},{4,5},{5,4},{6,7},{7,6},{8,9},{9,8},{10,11... | collective-permute-start | bytes 983048 | tf_op jit(solution)/shard_map/ppermute | solution.py:321
  100.0 1.2 collective-permute-done
  101.3 11.1 %all_to_all.54 = f32[16,40,128]{2,1,0:T(8,128)S(1)} all-to-all(f32[16,40,128]{2,1,0:T(8,128)S(1)} %bitcast.23), channel_id=1, replica_groups=mesh['gu'=2,'gv'=4,'gk'=2,'gh'=2,'gl'=2,'gw'=2,'gp'=2,'gc'=2] {'gk','gl'..., dimensions={0} | all-to-all | bytes 655360 | tf_op jit(solution)/shard_map/all_to_all | solution.py:260
  112.5 17.6 %all_to_all.55 = f32[16,40,128]{2,1,0:T(8,128)S(1)} all-to-all(f32[16,40,128]{2,1,0:T(8,128)S(1)} %broadcast_in_dim.14), channel_id=1, replica_groups=mesh['gu'=2,'gv'=4,'gk'=2,'gh'=2,'gl'=2,'gw'=2,'gp'=2,'gc'=2] {'gu','gh'..., dimensions={0} | all-to-all | bytes 655360 | tf_op jit(solution)/shard_map/all_to_all | solution.py:260
  130.2 10.9 %all_to_all.56 = f32[16,40,128]{2,1,0:T(8,128)S(1)} all-to-all(f32[16,40,128]{2,1,0:T(8,128)S(1)} %broadcast_in_dim.15), channel_id=1, replica_groups=mesh['gu'=2,'gv'=4,'gk'=2,'gh'=2,'gl'=2,'gw'=2,'gp'=2,'gc'=2] {'gk','gl'..., dimensions={0} | all-to-all | bytes 655360 | tf_op jit(solution)/shard_map/all_to_all | solution.py:260
  141.0 4.4 %collective-permute-start.1 = (f32[640,128]{1,0:T(8,128)S(1)}, f32[640,128]{1,0:T(8,128)S(1)}, u32[]{:S(2)}, u32[]{:S(2)}) collective-permute-start(f32[640,128]{1,0:T(8,128)S(1)} %bitcast.18), channel_id=1, source_target_pairs={{0,1},{1,0},{2,3},{3,2},{4,5},{5,4},{6,7},{7,6},{8,9},{9,8},{10,11... | collective-permute-start | bytes 983048 | tf_op jit(solution)/shard_map/ppermute | solution.py:325
  145.4 1.2 collective-permute-done.1.other_ref
  146.6 3.3 %shard_map.58 = f32[2,2,8,2,2,8,128]{6,5,4,3,2,1,0:T(8,128)S(1)} custom-call(s32[1]{0:T(128)} %bitcast.core_ref.place_ref, f32[640,128]{1,0:T(8,128)S(1)} %bitcast.19, f32[640,128]{1,0:T(8,128)S(1)} %collective-permute-done.1.other_ref, f32[32,512]{1,0:T(8,128)S(1)} %get-tuple-element.20.start_ref, f32[128,512]{1,0:T(8,128)S(1)} %get-tuple-element.21.merged_ref), custom_call_target="tpu_custom_call" | custom-call | tf_op jit(solution)/shard_map/pallas_call | solution.py:245
  149.9 27.9 %all_to_all.57 = f32[256,4,128]{2,1,0:T(4,128)S(1)} all-to-all(f32[256,4,128]{2,1,0:T(4,128)S(1)} %bitcast.17), channel_id=1, replica_groups=mesh['gu'=2,'gv'=4,'gk'=2,'gh'=2,'gl'=2,'gw'=2,'gp'=2,'gc'=2] {'gh','gl'..., dimensions={0} | all-to-all | bytes 1048576 | tf_op jit(solution)/shard_map/all_to_all | solution.py:260
  177.8 4.0 %collective-permute-start.2 = (f32[1024,128]{1,0:T(8,128)S(1)}, f32[1024,128]{1,0:T(8,128)S(1)}, u32[]{:S(2)}, u32[]{:S(2)}) collective-permute-start(f32[1024,128]{1,0:T(8,128)S(1)} %bitcast.15), channel_id=1, source_target_pairs={{0,1},{1,0},{2,3},{3,2},{4,5},{5,4},{6,7},{7,6},{8,9},{9,8},{10,11... | collective-permute-start | bytes 1572872 | tf_op jit(solution)/shard_map/ppermute | solution.py:339
  181.8 1.5 collective-permute-done.2.other_ref
  183.3 0.7 shard_map.59
  184.0 11.4 %all_to_all.58.parts_ref = f32[8,32,512]{2,1,0:T(8,128)S(1)} all-to-all(f32[8,32,512]{2,1,0:T(8,128)S(1)} %get-tuple-element.22), channel_id=1, replica_groups=mesh['gu'=2,'gv'=4,'gk'=2,'gh'=2,'gl'=2,'gw'=2,'gp'=2,'gc'=2] {'gl','gk'..., dimensions={0} | all-to-all | bytes 1048576 | tf_op jit(solution)/shard_map/all_to_all | solution.py:260
  195.4 1.6 shard_map.60
  197.0 9.4 %all_to_all.59.parts_ref = f32[8,32,512]{2,1,0:T(8,128)S(1)} all-to-all(f32[8,32,512]{2,1,0:T(8,128)S(1)} %shard_map.60), channel_id=1, replica_groups=mesh['gu'=2,'gv'=4,'gk'=2,'gh'=2,'gl'=2,'gw'=2,'gp'=2,'gc'=2] {'gl','gk'..., dimensions={0} | all-to-all | bytes 1048576 | tf_op jit(solution)/shard_map/all_to_all | solution.py:260
  206.5 1.9 shard_map.61
  (9 shorter events, 0.2 us)
Async XLA Ops:
  97.7 3.6 %collective-permute-start = (f32[640,128]{1,0:T(8,128)S(1)}, f32[640,128]{1,0:T(8,128)S(1)}, u32[]{:S(2)}, u32[]{:S(2)}) collective-permute-start(f32[640,128]{1,0:T(8,128)S(1)} %get-tuple-element.19), channel_id=1, source_target_pairs={{0,1},{1,0},{2,3},{3,2},{4,5},{5,4},{6,7},{7,6},{8,9},{9,8},{10,11... | collective-permute-start | bytes 983048 | tf_op jit(solution)/shard_map/ppermute | solution.py:321
  141.0 5.6 %collective-permute-start.1 = (f32[640,128]{1,0:T(8,128)S(1)}, f32[640,128]{1,0:T(8,128)S(1)}, u32[]{:S(2)}, u32[]{:S(2)}) collective-permute-start(f32[640,128]{1,0:T(8,128)S(1)} %bitcast.18), channel_id=1, source_target_pairs={{0,1},{1,0},{2,3},{3,2},{4,5},{5,4},{6,7},{7,6},{8,9},{9,8},{10,11... | collective-permute-start | bytes 983048 | tf_op jit(solution)/shard_map/ppermute | solution.py:325
  177.8 5.5 %collective-permute-start.2 = (f32[1024,128]{1,0:T(8,128)S(1)}, f32[1024,128]{1,0:T(8,128)S(1)}, u32[]{:S(2)}, u32[]{:S(2)}) collective-permute-start(f32[1024,128]{1,0:T(8,128)S(1)} %bitcast.15), channel_id=1, source_target_pairs={{0,1},{1,0},{2,3},{3,2},{4,5},{5,4},{6,7},{7,6},{8,9},{9,8},{10,11... | collective-permute-start | bytes 1572872 | tf_op jit(solution)/shard_map/ppermute | solution.py:339

commit v9 on v8

--- a/solution.py
+++ b/solution.py
@@ -69,15 +69,16 @@
 
 
 def send_field_kernel(
-    order_ref, core_ref, field_hbm, first_hbm, second_hbm, third_hbm, out_ref, first_ref, second_ref, third_ref, field_ref,
-    raw_ref, rows_ref, placed_ref, sems, start_sems, *, brick_len
+    order_hbm, field_hbm, first_hbm, second_hbm, third_hbm, out_ref, first_ref, second_ref, third_ref, field_ref,
+    raw_ref, rows_ref, placed_ref, order_ref, sems, start_sems, *, brick_len
 ):
     species, cells_y, cells_z = field_hbm.shape
     loads = [pltpu.make_async_copy(field_hbm.at[s], field_ref.at[s], sems.at[s]) for s in range(species)]
-    pairs = (third_hbm, raw_ref), (second_hbm, second_ref), (first_hbm, first_ref)
+    pairs = (order_hbm, order_ref), (third_hbm, raw_ref), (second_hbm, second_ref), (first_hbm, first_ref)
     starts = [pltpu.make_async_copy(source, target, start_sems.at[i]) for i, (source, target) in enumerate(pairs)]
-    for load in starts[:1] + loads + starts[1:]:
+    for load in starts[:2] + loads + starts[2:]:
         load.start()
+    starts[0].wait()
     lane = lax.broadcasted_iota(jnp.int32, (1, cells_z), 1)
     brick = lane // brick_len
     place = jnp.zeros((1, cells_z), jnp.int32)
@@ -85,12 +86,12 @@
         place = jnp.where(brick == b, order_ref[b] * brick_len, place)
     grid_z = (place + lane % brick_len).astype(jnp.float32)
     taper = 0.5 + 1.5 * grid_z / (cells_z - 1)
-    starts[0].wait()
+    starts[1].wait()
     rows_ref[...] = raw_ref[...].T
     for b in range(cells_z // brick_len):
         at = pl.multiple_of(order_ref[b] * brick_len, brick_len)
         placed_ref[b * brick_len : (b + 1) * brick_len, :] = rows_ref[pl.ds(at, brick_len), :]
-    core = (core_ref[0] & 1)
+    core = lax.axis_index("gc")
     half = cells_z // 2
     third_ref[:, :half] = placed_ref[pl.ds(core, half, stride=2), :].T
     third_ref[:, half:] = placed_ref[pl.ds(1 - core, half, stride=2), :].T
@@ -100,7 +101,7 @@
             cut = slice(j * LANES, (j + 1) * LANES)
             block = field_ref[s, :, cut] * taper[:, cut]
             out_ref[pl.ds(j * LANES * species + s, LANES, stride=species), :] = block.T
-    for load in starts[1:]:
+    for load in starts[2:]:
         load.wait()
 
 
@@ -119,7 +120,7 @@
 
 
 def second_kernel(
-    core_ref, gram_ref, start_ref, data_ref, merged_ref, kept_ref, sent_ref, rows_ref, *, species, rows_x, parts
+    gram_ref, start_ref, data_ref, merged_ref, kept_ref, sent_ref, rows_ref, *, species, rows_x, parts
 ):
     gram = gram_ref[...]
     current = start_ref[...]
@@ -145,10 +146,11 @@
         product = mm3([x[cut] for x in flipped], [x[:, i * LANES :] for x in merged], NN)
         blocks += [product[:, j * LANES : (j + 1) * LANES] for j in range(parts - i)]
     count = len(blocks) // 2
+    first = lax.axis_index("gc") == 0
     for i in range(count):
         rows = slice(i * LANES, (i + 1) * LANES)
-        kept_ref[rows, :] = jnp.where((core_ref[0] & 1) == 0, blocks[i], blocks[count + i])
-        sent_ref[rows, :] = jnp.where((core_ref[0] & 1) == 0, blocks[count + i], blocks[i])
+        kept_ref[rows, :] = jnp.where(first, blocks[i], blocks[count + i])
+        sent_ref[rows, :] = jnp.where(first, blocks[count + i], blocks[i])
 
 
 def symmetric_of(core, own_ref, other_ref, parts):
@@ -166,8 +168,8 @@
     return jnp.concatenate([jnp.concatenate(line, axis=1) for line in lines], axis=0)
 
 
-def third_kernel(core_ref, own_ref, other_ref, start_ref, merged_ref, out_ref, rows_ref, *, parts):
-    gram = halves(symmetric_of((core_ref[0] & 1), own_ref, other_ref, parts))
+def third_kernel(own_ref, other_ref, start_ref, merged_ref, out_ref, rows_ref, *, parts):
+    gram = halves(symmetric_of(lax.axis_index("gc"), own_ref, other_ref, parts))
     current = start_ref[...]
     for repeat in range(ITERS):
         current = orthonormal_rows(mm3(halves(current), gram, NN))
@@ -226,30 +228,28 @@
     spread(out_ref, mm3(halves(inner), data, NT))
 
 
-def core_kernel(place_ref, parts_ref, high_ref, low_ref, out_ref, rows_ref):
+def core_kernel(parts_ref, high_ref, low_ref, out_ref, rows_ref):
     current = halves(orthonormal_rows(total_of(parts_ref)))
-    block = (place_ref[0] >> 1 & 1) * 2 + (place_ref[0] & 1)
+    block = lax.axis_index("gw") * 2 + lax.axis_index("gc")
     cut = pl.ds(pl.multiple_of(block * LANES, LANES), LANES)
     rows_ref[...] = mm3(current, (high_ref[:, cut], low_ref[:, cut]), NN).T
-    at = place_ref[0] >> 2
+    at = lax.axis_index("gu") * 16 + lax.axis_index("gv") * 4 + lax.axis_index("gh") * 2
     for e in range(out_ref.shape[1]):
         for b in range(out_ref.shape[0]):
             out_ref[b, e, :] = rows_ref[at + e * (LANES // 4) + b, :]
 
 
-def call(kernel, out_shape, *args, scratch=(), scalars=0, in_hbm=0):
+def call(kernel, out_shape, *args, scratch=(), in_hbm=0):
     vmem = pl.BlockSpec(memory_space=pltpu.VMEM)
-    smem = pl.BlockSpec(memory_space=pltpu.SMEM)
     hbm = pl.BlockSpec(memory_space=pltpu.HBM)
-    lead = scalars + in_hbm
     return pl.pallas_call(
         kernel,
         out_shape=out_shape,
-        in_specs=[smem] * scalars + [hbm] * in_hbm + [vmem] * (len(args) - lead),
+        in_specs=[hbm] * in_hbm + [vmem] * (len(args) - in_hbm),
         out_specs=jax.tree.map(lambda _: vmem, out_shape),
         compiler_params=pltpu.CompilerParams(vmem_limit_bytes=None if in_hbm else VMEM_BYTES),
         scratch_shapes=[pltpu.VMEM(s, jnp.float32) if isinstance(s, tuple) else s for s in scratch],
-    )(*args[:lead], *[pltpu.with_memory_space_constraint(a, pltpu.VMEM) for a in args[lead:]])
+    )(*args[:in_hbm], *[pltpu.with_memory_space_constraint(a, pltpu.VMEM) for a in args[in_hbm:]])
 
 
 def vm(*shape, dtype=jnp.float32):
@@ -274,16 +274,12 @@
     devices = lax.axis_size(ORDER)
     chips = lax.axis_size(CHIPS)
     parts_y = full_y // LANES
-    gx = lax.axis_index(("gu", "gv", "gk"))
-    row = (gx >> 2) * 8 + (gx >> 1 & 1) * 4 + lax.axis_index("gh") * 2
-    core = (row * 4 + lax.axis_index("gw") * 2 + lax.axis_index("gc")).astype(jnp.int32).reshape(1)
     exchange = [(0, 1), (1, 0)]
 
     sent, start_first, start_second, start_third = call(
         functools.partial(send_field_kernel, brick_len=brick_len),
         (vm(cells_z * species, cells_y), vm(rank_one, rows_x), vm(rank_two, full_y), vm(rank_three, cells_z)),
         brick_order,
-        core,
         field.reshape(species, cells_y, cells_z),
         start_first.T,
         start_second.T,
@@ -293,11 +289,11 @@
             (rank_three, cells_z),
             (cells_z, rank_three),
             (cells_z, rank_three),
+            pltpu.SMEM(brick_order.shape, jnp.int32),
             pltpu.SemaphoreType.DMA((species,)),
-            pltpu.SemaphoreType.DMA((3,)),
+            pltpu.SemaphoreType.DMA((4,)),
         ],
-        scalars=2,
-        in_hbm=4,
+        in_hbm=5,
     )
     data = swap(sent.reshape(devices, species, cells_y), ORDER).reshape(devices * species, cells_y)
 
@@ -311,12 +307,10 @@
     merged, kept, sent = call(
         functools.partial(second_kernel, species=species, rows_x=rows_x, parts=parts_y),
         (vm(merged_rows, full_y),) + (vm(parts_y * (parts_y + 1) // 4 * LANES, LANES),) * 2,
-        core,
         gram,
         start_first,
         data,
         scratch=[(rank_one, rows_x)],
-        scalars=1,
     )
     gram = kept + lax.ppermute(sent, "gc", exchange)
     gram = jnp.sum(swap(gram.reshape(lax.axis_size(BLOCK), -1, LANES), BLOCK), axis=0)
@@ -327,13 +321,11 @@
     sent = call(
         functools.partial(third_kernel, parts=parts_y),
         vm(lax.axis_size("gh"), lax.axis_size("gl"), lax.axis_size(("gu", "gv")), lax.axis_size("gk"), 2, 8, LANES),
-        core,
         own,
         other,
         start_second,
         merged,
         scratch=[(rank_two, merged_rows)],
-        scalars=1,
     )
     own = swap(sent.reshape(chips, 4, LANES), CHIPS).reshape(chips * 4, LANES)
     other = lax.ppermute(own, "gc", exchange)
@@ -352,12 +344,10 @@
     return call(
         core_kernel,
         jax.ShapeDtypeStruct((2, 4, rank_three), jnp.float32),
-        core,
         swap(pieces, NEAR),
         high,
         low,
         scratch=[(merged_rows, rank_three)],
-        scalars=1,
     )
 
 

time: 211 us -> 210 us (level)
  no operation moved by 1% of the time
where the time goes in v9:
time: 210 us; the launch traced here: 208 us
  blocking collectives  180 us (86%)
  Pallas kernels  13 us (6%)
  starting transfers between devices  10.7 us (5%)
  waiting for transfers between devices  3.98 us (2%)
    all_to_all x10, blocking collectives, swap(): return lax.all_to_all(pieces, axes, split_axis=0, concat_axis=0, tiled=True)  180 us
    pallas_call x7, Pallas kernels, call(): pl.pallas_call(kernel, out_shape=out_shape, in_specs=[hbm] * in_hbm + [vm...  13 us
    ppermute x2, starting transfers between devices, shards(): other = lax.ppermute(own, 'gc', exchange)  8.35 us
  transfers between devices with their start and end apart: 3, of which 3 were waited for; matrix products, arithmetic and copies ran while one was open for 0% of the time, Pallas kernels for 0%

profile of v9, /device:TPU:1, one launch (start us, length us, event | category | flops | bytes accessed | tf_op | source)
XLA Modules:
  0.0 207.8 jit_solution(4518655808648764174)
XLA Ops:
  0.0 1.8 shard_map.55
  1.8 54.3 %all_to_all.50 = f32[512,4,128]{2,1,0:T(4,128)S(1)} all-to-all(f32[512,4,128]{2,1,0:T(4,128)S(1)} %bitcast.19), channel_id=1, replica_groups=mesh['gu'=2,'gv'=4,'gk'=2,'gh'=2,'gl'=2,'gw'=2,'gp'=2,'gc'=2] {'gh','gl'..., dimensions={0} | all-to-all | bytes 2097152 | tf_op jit(solution)/shard_map/all_to_all | solution.py:260
  56.1 0.6 shard_map.56
  56.7 9.9 %all_to_all.51 = f32[16,8,128]{2,1,0:T(8,128)S(1)} all-to-all(f32[16,8,128]{2,1,0:T(8,128)S(1)} %bitcast.21), channel_id=1, replica_groups=mesh['gu'=2,'gv'=4,'gk'=2,'gh'=2,'gl'=2,'gw'=2,'gp'=2,'gc'=2] {'gl','gw'..., dimensions={0} | all-to-all | bytes 131072 | tf_op jit(solution)/shard_map/all_to_all | solution.py:260
  66.6 16.9 %all_to_all.52 = f32[32,8,128]{2,1,0:T(8,128)S(1)} all-to-all(f32[32,8,128]{2,1,0:T(8,128)S(1)} %broadcast_in_dim.12), channel_id=1, replica_groups=mesh['gu'=2,'gv'=4,'gk'=2,'gh'=2,'gl'=2,'gw'=2,'gp'=2,'gc'=2] {'gh','gu'..., dimensions={0} | all-to-all | bytes 262144 | tf_op jit(solution)/shard_map/all_to_all | solution.py:260
  83.5 10.5 %all_to_all.53 = f32[16,8,128]{2,1,0:T(8,128)S(1)} all-to-all(f32[16,8,128]{2,1,0:T(8,128)S(1)} %broadcast_in_dim.13), channel_id=1, replica_groups=mesh['gu'=2,'gv'=4,'gk'=2,'gh'=2,'gl'=2,'gw'=2,'gp'=2,'gc'=2] {'gl','gw'..., dimensions={0} | all-to-all | bytes 131072 | tf_op jit(solution)/shard_map/all_to_all | solution.py:260
  94.0 3.1 %shard_map.57 = (f32[128,512]{1,0:T(8,128)S(1)}, f32[640,128]{1,0:T(8,128)S(1)}, f32[640,128]{1,0:T(8,128)S(1)}) custom-call(f32[128,128]{1,0:T(8,128)S(1)} %bitcast.20, f32[32,128]{1,0:T(8,128)S(1)} %get-tuple-element.17.start_ref, f32[2048,128]{1,0:T(8,128)S(1)} %bitcast.13), custom_call_target="tpu_custom_call" | custom-call | tf_op jit(solution)/shard_map/pallas_call | solution.py:245
  97.0 2.3 %collective-permute-start = (f32[640,128]{1,0:T(8,128)S(1)}, f32[640,128]{1,0:T(8,128)S(1)}, u32[]{:S(2)}, u32[]{:S(2)}) collective-permute-start(f32[640,128]{1,0:T(8,128)S(1)} %get-tuple-element.19), channel_id=1, source_target_pairs={{0,1},{1,0},{2,3},{3,2},{4,5},{5,4},{6,7},{7,6},{8,9},{9,8},{10,11... | collective-permute-start | bytes 983048 | tf_op jit(solution)/shard_map/ppermute | solution.py:315
  99.4 1.2 collective-permute-done
  100.7 11.1 %all_to_all.54 = f32[16,40,128]{2,1,0:T(8,128)S(1)} all-to-all(f32[16,40,128]{2,1,0:T(8,128)S(1)} %bitcast.22), channel_id=1, replica_groups=mesh['gu'=2,'gv'=4,'gk'=2,'gh'=2,'gl'=2,'gw'=2,'gp'=2,'gc'=2] {'gk','gl'..., dimensions={0} | all-to-all | bytes 655360 | tf_op jit(solution)/shard_map/all_to_all | solution.py:260
  111.9 17.6 %all_to_all.55 = f32[16,40,128]{2,1,0:T(8,128)S(1)} all-to-all(f32[16,40,128]{2,1,0:T(8,128)S(1)} %broadcast_in_dim.14), channel_id=1, replica_groups=mesh['gu'=2,'gv'=4,'gk'=2,'gh'=2,'gl'=2,'gw'=2,'gp'=2,'gc'=2] {'gu','gh'..., dimensions={0} | all-to-all | bytes 655360 | tf_op jit(solution)/shard_map/all_to_all | solution.py:260
  129.5 10.8 %all_to_all.56 = f32[16,40,128]{2,1,0:T(8,128)S(1)} all-to-all(f32[16,40,128]{2,1,0:T(8,128)S(1)} %broadcast_in_dim.15), channel_id=1, replica_groups=mesh['gu'=2,'gv'=4,'gk'=2,'gh'=2,'gl'=2,'gw'=2,'gp'=2,'gc'=2] {'gk','gl'..., dimensions={0} | all-to-all | bytes 655360 | tf_op jit(solution)/shard_map/all_to_all | solution.py:260
  140.4 4.4 %collective-permute-start.1 = (f32[640,128]{1,0:T(8,128)S(1)}, f32[640,128]{1,0:T(8,128)S(1)}, u32[]{:S(2)}, u32[]{:S(2)}) collective-permute-start(f32[640,128]{1,0:T(8,128)S(1)} %bitcast.17), channel_id=1, source_target_pairs={{0,1},{1,0},{2,3},{3,2},{4,5},{5,4},{6,7},{7,6},{8,9},{9,8},{10,11... | collective-permute-start | bytes 983048 | tf_op jit(solution)/shard_map/ppermute | solution.py:319
  144.8 1.2 collective-permute-done.1.other_ref
  146.0 3.3 %shard_map.58 = f32[2,2,8,2,2,8,128]{6,5,4,3,2,1,0:T(8,128)S(1)} custom-call(f32[640,128]{1,0:T(8,128)S(1)} %bitcast.18, f32[640,128]{1,0:T(8,128)S(1)} %collective-permute-done.1.other_ref, f32[32,512]{1,0:T(8,128)S(1)} %get-tuple-element.20.start_ref, f32[128,512]{1,0:T(8,128)S(1)} %get-tuple-element.21.merged_ref), custom_call_target="tpu_custom_call" | custom-call | tf_op jit(solution)/shard_map/pallas_call | solution.py:245
  149.3 27.9 %all_to_all.57 = f32[256,4,128]{2,1,0:T(4,128)S(1)} all-to-all(f32[256,4,128]{2,1,0:T(4,128)S(1)} %bitcast.14), channel_id=1, replica_groups=mesh['gu'=2,'gv'=4,'gk'=2,'gh'=2,'gl'=2,'gw'=2,'gp'=2,'gc'=2] {'gh','gl'..., dimensions={0} | all-to-all | bytes 1048576 | tf_op jit(solution)/shard_map/all_to_all | solution.py:260
  177.2 4.0 %collective-permute-start.2 = (f32[1024,128]{1,0:T(8,128)S(1)}, f32[1024,128]{1,0:T(8,128)S(1)}, u32[]{:S(2)}, u32[]{:S(2)}) collective-permute-start(f32[1024,128]{1,0:T(8,128)S(1)} %bitcast.15), channel_id=1, source_target_pairs={{0,1},{1,0},{2,3},{3,2},{4,5},{5,4},{6,7},{7,6},{8,9},{9,8},{10,11... | collective-permute-start | bytes 1572872 | tf_op jit(solution)/shard_map/ppermute | solution.py:331
  181.2 1.5 collective-permute-done.2.other_ref
  182.7 0.7 shard_map.59
  183.4 11.4 %all_to_all.58.parts_ref = f32[8,32,512]{2,1,0:T(8,128)S(1)} all-to-all(f32[8,32,512]{2,1,0:T(8,128)S(1)} %get-tuple-element.22), channel_id=1, replica_groups=mesh['gu'=2,'gv'=4,'gk'=2,'gh'=2,'gl'=2,'gw'=2,'gp'=2,'gc'=2] {'gl','gk'..., dimensions={0} | all-to-all | bytes 1048576 | tf_op jit(solution)/shard_map/all_to_all | solution.py:260
  194.8 1.6 shard_map.60
  196.5 9.4 %all_to_all.59.parts_ref = f32[8,32,512]{2,1,0:T(8,128)S(1)} all-to-all(f32[8,32,512]{2,1,0:T(8,128)S(1)} %shard_map.60), channel_id=1, replica_groups=mesh['gu'=2,'gv'=4,'gk'=2,'gh'=2,'gl'=2,'gw'=2,'gp'=2,'gc'=2] {'gl','gk'..., dimensions={0} | all-to-all | bytes 1048576 | tf_op jit(solution)/shard_map/all_to_all | solution.py:260
  205.9 1.9 shard_map.61
  (9 shorter events, 0.2 us)
Async XLA Ops:
  97.0 3.6 %collective-permute-start = (f32[640,128]{1,0:T(8,128)S(1)}, f32[640,128]{1,0:T(8,128)S(1)}, u32[]{:S(2)}, u32[]{:S(2)}) collective-permute-start(f32[640,128]{1,0:T(8,128)S(1)} %get-tuple-element.19), channel_id=1, source_target_pairs={{0,1},{1,0},{2,3},{3,2},{4,5},{5,4},{6,7},{7,6},{8,9},{9,8},{10,11... | collective-permute-start | bytes 983048 | tf_op jit(solution)/shard_map/ppermute | solution.py:315
  140.4 5.6 %collective-permute-start.1 = (f32[640,128]{1,0:T(8,128)S(1)}, f32[640,128]{1,0:T(8,128)S(1)}, u32[]{:S(2)}, u32[]{:S(2)}) collective-permute-start(f32[640,128]{1,0:T(8,128)S(1)} %bitcast.17), channel_id=1, source_target_pairs={{0,1},{1,0},{2,3},{3,2},{4,5},{5,4},{6,7},{7,6},{8,9},{9,8},{10,11... | collective-permute-start | bytes 983048 | tf_op jit(solution)/shard_map/ppermute | solution.py:319
  177.2 5.5 %collective-permute-start.2 = (f32[1024,128]{1,0:T(8,128)S(1)}, f32[1024,128]{1,0:T(8,128)S(1)}, u32[]{:S(2)}, u32[]{:S(2)}) collective-permute-start(f32[1024,128]{1,0:T(8,128)S(1)} %bitcast.15), channel_id=1, source_target_pairs={{0,1},{1,0},{2,3},{3,2},{4,5},{5,4},{6,7},{7,6},{8,9},{9,8},{10,11... | collective-permute-start | bytes 1572872 | tf_op jit(solution)/shard_map/ppermute | solution.py:331

commit v10 on v9

--- a/solution.py
+++ b/solution.py
@@ -15,8 +15,7 @@
 CHIPS = ("gh", "gl", "gu", "gv", "gk", "gw", "gp")
 ORDER = CHIPS + ("gc",)
 NEAR = ("gl", "gk", "gp")
-CLOSE = ("gl", "gw", "gp", "gc")
-FAR = ("gh", "gu", "gv", "gk")
+CLOSE = ("gk", "gl", "gw", "gp", "gc")
 BLOCK = ("gk", "gl", "gw", "gp")
 BEYOND = ("gu", "gh", "gv")
 
@@ -301,7 +300,7 @@
         functools.partial(gram_first_kernel, species=species, rows_x=rows_x, parts=parts_y), vm(rows_x, rows_x), data
     )
     gram = jnp.sum(swap(gram.reshape(lax.axis_size(CLOSE), -1, rows_x), CLOSE), axis=0)
-    gram = jnp.sum(swap(copies(gram, FAR), FAR), axis=0)
+    gram = jnp.sum(swap(copies(gram, BEYOND), BEYOND), axis=0)
     gram = swap(copies(gram, CLOSE), CLOSE).reshape(rows_x, rows_x)
 
     merged, kept, sent = call(

time: 210 us -> 211 us (level)
  no operation moved by 1% of the time
where the time goes in v10:
time: 211 us; the launch traced here: 209 us
  blocking collectives  182 us (86%)
  Pallas kernels  13 us (6%)
  starting transfers between devices  9.8 us (5%)
  waiting for transfers between devices  3.98 us (2%)
    all_to_all x10, blocking collectives, swap(): return lax.all_to_all(pieces, axes, split_axis=0, concat_axis=0, tiled=True)  182 us
    pallas_call x7, Pallas kernels, call(): pl.pallas_call(kernel, out_shape=out_shape, in_specs=[hbm] * in_hbm + [vm...  13 us
    ppermute x2, starting transfers between devices, shards(): other = lax.ppermute(own, 'gc', exchange)  7.5 us
  transfers between devices with their start and end apart: 3, of which 3 were waited for; matrix products, arithmetic and copies ran while one was open for 0% of the time, Pallas kernels for 0%

profile of v10, /device:TPU:1, one launch (start us, length us, event | category | flops | bytes accessed | tf_op | source)
XLA Modules:
  0.0 209.0 jit_solution(8721348626024445177)
XLA Ops:
  0.0 1.8 shard_map.55
  1.8 54.3 %all_to_all.50 = f32[512,4,128]{2,1,0:T(4,128)S(1)} all-to-all(f32[512,4,128]{2,1,0:T(4,128)S(1)} %bitcast.19), channel_id=1, replica_groups=mesh['gu'=2,'gv'=4,'gk'=2,'gh'=2,'gl'=2,'gw'=2,'gp'=2,'gc'=2] {'gh','gl'..., dimensions={0} | all-to-all | bytes 2097152 | tf_op jit(solution)/shard_map/all_to_all | solution.py:259
  56.1 0.6 shard_map.56
  56.7 11.4 %all_to_all.51 = f32[32,4,128]{2,1,0:T(4,128)S(1)} all-to-all(f32[32,4,128]{2,1,0:T(4,128)S(1)} %bitcast.21), channel_id=1, replica_groups=mesh['gu'=2,'gv'=4,'gk'=2,'gh'=2,'gl'=2,'gw'=2,'gp'=2,'gc'=2] {'gk','gl'..., dimensions={0} | all-to-all | bytes 131072 | tf_op jit(solution)/shard_map/all_to_all | solution.py:259
  68.1 15.9 %all_to_all.52 = f32[16,4,128]{2,1,0:T(4,128)S(1)} all-to-all(f32[16,4,128]{2,1,0:T(4,128)S(1)} %broadcast_in_dim.12), channel_id=1, replica_groups=mesh['gu'=2,'gv'=4,'gk'=2,'gh'=2,'gl'=2,'gw'=2,'gp'=2,'gc'=2] {'gu','gh'..., dimensions={0} | all-to-all | bytes 65536 | tf_op jit(solution)/shard_map/all_to_all | solution.py:259
  84.0 11.3 %all_to_all.53 = f32[32,4,128]{2,1,0:T(4,128)S(1)} all-to-all(f32[32,4,128]{2,1,0:T(4,128)S(1)} %broadcast_in_dim.13), channel_id=1, replica_groups=mesh['gu'=2,'gv'=4,'gk'=2,'gh'=2,'gl'=2,'gw'=2,'gp'=2,'gc'=2] {'gk','gl'..., dimensions={0} | all-to-all | bytes 131072 | tf_op jit(solution)/shard_map/all_to_all | solution.py:259
  95.4 3.1 %shard_map.57 = (f32[128,512]{1,0:T(8,128)S(1)}, f32[640,128]{1,0:T(8,128)S(1)}, f32[640,128]{1,0:T(8,128)S(1)}) custom-call(f32[128,128]{1,0:T(8,128)S(1)} %bitcast.20, f32[32,128]{1,0:T(8,128)S(1)} %get-tuple-element.17.start_ref, f32[2048,128]{1,0:T(8,128)S(1)} %bitcast.13), custom_call_target="tpu_custom_call" | custom-call | tf_op jit(solution)/shard_map/pallas_call | solution.py:244
  98.5 2.3 %collective-permute-start = (f32[640,128]{1,0:T(8,128)S(1)}, f32[640,128]{1,0:T(8,128)S(1)}, u32[]{:S(2)}, u32[]{:S(2)}) collective-permute-start(f32[640,128]{1,0:T(8,128)S(1)} %get-tuple-element.19), channel_id=1, source_target_pairs={{0,1},{1,0},{2,3},{3,2},{4,5},{5,4},{6,7},{7,6},{8,9},{9,8},{10,11... | collective-permute-start | bytes 983048 | tf_op jit(solution)/shard_map/ppermute | solution.py:314
  100.8 1.2 collective-permute-done
  102.1 11.1 %all_to_all.54 = f32[16,40,128]{2,1,0:T(8,128)S(1)} all-to-all(f32[16,40,128]{2,1,0:T(8,128)S(1)} %bitcast.22), channel_id=1, replica_groups=mesh['gu'=2,'gv'=4,'gk'=2,'gh'=2,'gl'=2,'gw'=2,'gp'=2,'gc'=2] {'gk','gl'..., dimensions={0} | all-to-all | bytes 655360 | tf_op jit(solution)/shard_map/all_to_all | solution.py:259
  113.3 17.7 %all_to_all.55 = f32[16,40,128]{2,1,0:T(8,128)S(1)} all-to-all(f32[16,40,128]{2,1,0:T(8,128)S(1)} %broadcast_in_dim.14), channel_id=1, replica_groups=mesh['gu'=2,'gv'=4,'gk'=2,'gh'=2,'gl'=2,'gw'=2,'gp'=2,'gc'=2] {'gu','gh'..., dimensions={0} | all-to-all | bytes 655360 | tf_op jit(solution)/shard_map/all_to_all | solution.py:259
  131.0 11.7 %all_to_all.56 = f32[16,40,128]{2,1,0:T(8,128)S(1)} all-to-all(f32[16,40,128]{2,1,0:T(8,128)S(1)} %broadcast_in_dim.15), channel_id=1, replica_groups=mesh['gu'=2,'gv'=4,'gk'=2,'gh'=2,'gl'=2,'gw'=2,'gp'=2,'gc'=2] {'gk','gl'..., dimensions={0} | all-to-all | bytes 655360 | tf_op jit(solution)/shard_map/all_to_all | solution.py:259
  142.7 3.9 %collective-permute-start.1 = (f32[640,128]{1,0:T(8,128)S(1)}, f32[640,128]{1,0:T(8,128)S(1)}, u32[]{:S(2)}, u32[]{:S(2)}) collective-permute-start(f32[640,128]{1,0:T(8,128)S(1)} %bitcast.17), channel_id=1, source_target_pairs={{0,1},{1,0},{2,3},{3,2},{4,5},{5,4},{6,7},{7,6},{8,9},{9,8},{10,11... | collective-permute-start | bytes 983048 | tf_op jit(solution)/shard_map/ppermute | solution.py:318
  146.6 1.2 collective-permute-done.1.other_ref
  147.8 3.3 %shard_map.58 = f32[2,2,8,2,2,8,128]{6,5,4,3,2,1,0:T(8,128)S(1)} custom-call(f32[640,128]{1,0:T(8,128)S(1)} %bitcast.18, f32[640,128]{1,0:T(8,128)S(1)} %collective-permute-done.1.other_ref, f32[32,512]{1,0:T(8,128)S(1)} %get-tuple-element.20.start_ref, f32[128,512]{1,0:T(8,128)S(1)} %get-tuple-element.21.merged_ref), custom_call_target="tpu_custom_call" | custom-call | tf_op jit(solution)/shard_map/pallas_call | solution.py:244
  151.1 27.7 %all_to_all.57 = f32[256,4,128]{2,1,0:T(4,128)S(1)} all-to-all(f32[256,4,128]{2,1,0:T(4,128)S(1)} %bitcast.14), channel_id=1, replica_groups=mesh['gu'=2,'gv'=4,'gk'=2,'gh'=2,'gl'=2,'gw'=2,'gp'=2,'gc'=2] {'gh','gl'..., dimensions={0} | all-to-all | bytes 1048576 | tf_op jit(solution)/shard_map/all_to_all | solution.py:259
  178.8 3.6 %collective-permute-start.2 = (f32[1024,128]{1,0:T(8,128)S(1)}, f32[1024,128]{1,0:T(8,128)S(1)}, u32[]{:S(2)}, u32[]{:S(2)}) collective-permute-start(f32[1024,128]{1,0:T(8,128)S(1)} %bitcast.15), channel_id=1, source_target_pairs={{0,1},{1,0},{2,3},{3,2},{4,5},{5,4},{6,7},{7,6},{8,9},{9,8},{10,11... | collective-permute-start | bytes 1572872 | tf_op jit(solution)/shard_map/ppermute | solution.py:330
  182.4 1.5 collective-permute-done.2.other_ref
  184.0 0.7 shard_map.59
  184.7 11.4 %all_to_all.58.parts_ref = f32[8,32,512]{2,1,0:T(8,128)S(1)} all-to-all(f32[8,32,512]{2,1,0:T(8,128)S(1)} %get-tuple-element.22), channel_id=1, replica_groups=mesh['gu'=2,'gv'=4,'gk'=2,'gh'=2,'gl'=2,'gw'=2,'gp'=2,'gc'=2] {'gl','gk'..., dimensions={0} | all-to-all | bytes 1048576 | tf_op jit(solution)/shard_map/all_to_all | solution.py:259
  196.1 1.6 shard_map.60
  197.7 9.4 %all_to_all.59.parts_ref = f32[8,32,512]{2,1,0:T(8,128)S(1)} all-to-all(f32[8,32,512]{2,1,0:T(8,128)S(1)} %shard_map.60), channel_id=1, replica_groups=mesh['gu'=2,'gv'=4,'gk'=2,'gh'=2,'gl'=2,'gw'=2,'gp'=2,'gc'=2] {'gl','gk'..., dimensions={0} | all-to-all | bytes 1048576 | tf_op jit(solution)/shard_map/all_to_all | solution.py:259
  207.2 1.9 shard_map.61
  (9 shorter events, 0.2 us)
Async XLA Ops:
  98.5 3.5 %collective-permute-start = (f32[640,128]{1,0:T(8,128)S(1)}, f32[640,128]{1,0:T(8,128)S(1)}, u32[]{:S(2)}, u32[]{:S(2)}) collective-permute-start(f32[640,128]{1,0:T(8,128)S(1)} %get-tuple-element.19), channel_id=1, source_target_pairs={{0,1},{1,0},{2,3},{3,2},{4,5},{5,4},{6,7},{7,6},{8,9},{9,8},{10,11... | collective-permute-start | bytes 983048 | tf_op jit(solution)/shard_map/ppermute | solution.py:314
  142.7 5.2 %collective-permute-start.1 = (f32[640,128]{1,0:T(8,128)S(1)}, f32[640,128]{1,0:T(8,128)S(1)}, u32[]{:S(2)}, u32[]{:S(2)}) collective-permute-start(f32[640,128]{1,0:T(8,128)S(1)} %bitcast.17), channel_id=1, source_target_pairs={{0,1},{1,0},{2,3},{3,2},{4,5},{5,4},{6,7},{7,6},{8,9},{9,8},{10,11... | collective-permute-start | bytes 983048 | tf_op jit(solution)/shard_map/ppermute | solution.py:318
  178.8 5.1 %collective-permute-start.2 = (f32[1024,128]{1,0:T(8,128)S(1)}, f32[1024,128]{1,0:T(8,128)S(1)}, u32[]{:S(2)}, u32[]{:S(2)}) collective-permute-start(f32[1024,128]{1,0:T(8,128)S(1)} %bitcast.15), channel_id=1, source_target_pairs={{0,1},{1,0},{2,3},{3,2},{4,5},{5,4},{6,7},{7,6},{8,9},{9,8},{10,11... | collective-permute-start | bytes 1572872 | tf_op jit(solution)/shard_map/ppermute | solution.py:330

commit v11 on v9

--- a/solution.py
+++ b/solution.py
@@ -14,11 +14,11 @@
 FINE = ("gu", "gv", "gk", "gh", "gl", "gw", "gp", "gc")
 CHIPS = ("gh", "gl", "gu", "gv", "gk", "gw", "gp")
 ORDER = CHIPS + ("gc",)
-NEAR = ("gl", "gk", "gp")
-CLOSE = ("gl", "gw", "gp", "gc")
-FAR = ("gh", "gu", "gv", "gk")
-BLOCK = ("gk", "gl", "gw", "gp")
-BEYOND = ("gu", "gh", "gv")
+NEAR = ("gk", "gp", "gl")
+CLOSE = ("gw", "gl", "gp", "gc")
+FAR = ("gv", "gu", "gk", "gh")
+BLOCK = ("gw", "gk", "gp", "gl")
+BEYOND = ("gv", "gu", "gh")
 
 highest = lax.Precision.HIGHEST
 NN = ((1,), (0,))
@@ -173,7 +173,7 @@
     current = start_ref[...]
     for repeat in range(ITERS):
         current = orthonormal_rows(mm3(halves(current), gram, NN))
-    rows_ref[...] = mm(current, merged_ref[...], NT)
+    rows_ref[...] = mm3(halves(current), halves(merged_ref[...]), NT)
     quarter = LANES // 4
     groups = [rows_ref[pl.ds(e, rows_ref.shape[0] // 4, stride=4), :] for e in range(4)]
     group_id = lax.broadcasted_iota(jnp.int32, groups[0].shape, 1) // quarter

time: 210 us -> 210 us (level)
  no operation moved by 1% of the time
where the time goes in v11:
time: 210 us; the launch traced here: 208 us
  blocking collectives  179 us (85%)
  Pallas kernels  12.7 us (6%)
  starting transfers between devices  11.9 us (6%)
  waiting for transfers between devices  3.98 us (2%)
    all_to_all x10, blocking collectives, swap(): return lax.all_to_all(pieces, axes, split_axis=0, concat_axis=0, tiled=True)  179 us
    pallas_call x7, Pallas kernels, call(): pl.pallas_call(kernel, out_shape=out_shape, in_specs=[hbm] * in_hbm + [vm...  12.7 us
    ppermute x2, starting transfers between devices, shards(): other = lax.ppermute(own, 'gc', exchange)  9.59 us
  transfers between devices with their start and end apart: 3, of which 3 were waited for; matrix products, arithmetic and copies ran while one was open for 0% of the time, Pallas kernels for 0%

profile of v11, /device:TPU:1, one launch (start us, length us, event | category | flops | bytes accessed | tf_op | source)
XLA Modules:
  0.0 208.3 jit_solution(3059371833608359502)
XLA Ops:
  0.0 1.8 shard_map.55
  1.8 54.3 %all_to_all.50 = f32[512,4,128]{2,1,0:T(4,128)S(1)} all-to-all(f32[512,4,128]{2,1,0:T(4,128)S(1)} %bitcast.19), channel_id=1, replica_groups=mesh['gu'=2,'gv'=4,'gk'=2,'gh'=2,'gl'=2,'gw'=2,'gp'=2,'gc'=2] {'gh','gl'..., dimensions={0} | all-to-all | bytes 2097152 | tf_op jit(solution)/shard_map/all_to_all | solution.py:260
  56.1 0.6 shard_map.56
  56.7 9.9 %all_to_all.51 = f32[16,8,128]{2,1,0:T(8,128)S(1)} all-to-all(f32[16,8,128]{2,1,0:T(8,128)S(1)} %bitcast.21), channel_id=1, replica_groups=mesh['gu'=2,'gv'=4,'gk'=2,'gh'=2,'gl'=2,'gw'=2,'gp'=2,'gc'=2] {'gw','gl'..., dimensions={0} | all-to-all | bytes 131072 | tf_op jit(solution)/shard_map/all_to_all | solution.py:260
  66.6 17.5 %all_to_all.52 = f32[32,8,128]{2,1,0:T(8,128)S(1)} all-to-all(f32[32,8,128]{2,1,0:T(8,128)S(1)} %broadcast_in_dim.12), channel_id=1, replica_groups=mesh['gu'=2,'gv'=4,'gk'=2,'gh'=2,'gl'=2,'gw'=2,'gp'=2,'gc'=2] {'gv','gu'..., dimensions={0} | all-to-all | bytes 262144 | tf_op jit(solution)/shard_map/all_to_all | solution.py:260
  84.1 10.1 %all_to_all.53 = f32[16,8,128]{2,1,0:T(8,128)S(1)} all-to-all(f32[16,8,128]{2,1,0:T(8,128)S(1)} %broadcast_in_dim.13), channel_id=1, replica_groups=mesh['gu'=2,'gv'=4,'gk'=2,'gh'=2,'gl'=2,'gw'=2,'gp'=2,'gc'=2] {'gw','gl'..., dimensions={0} | all-to-all | bytes 131072 | tf_op jit(solution)/shard_map/all_to_all | solution.py:260
  94.2 3.1 %shard_map.57 = (f32[128,512]{1,0:T(8,128)S(1)}, f32[640,128]{1,0:T(8,128)S(1)}, f32[640,128]{1,0:T(8,128)S(1)}) custom-call(f32[128,128]{1,0:T(8,128)S(1)} %bitcast.20, f32[32,128]{1,0:T(8,128)S(1)} %get-tuple-element.17.start_ref, f32[2048,128]{1,0:T(8,128)S(1)} %bitcast.13), custom_call_target="tpu_custom_call" | custom-call | tf_op jit(solution)/shard_map/pallas_call | solution.py:245
  97.3 2.3 %collective-permute-start = (f32[640,128]{1,0:T(8,128)S(1)}, f32[640,128]{1,0:T(8,128)S(1)}, u32[]{:S(2)}, u32[]{:S(2)}) collective-permute-start(f32[640,128]{1,0:T(8,128)S(1)} %get-tuple-element.19), channel_id=1, source_target_pairs={{0,1},{1,0},{2,3},{3,2},{4,5},{5,4},{6,7},{7,6},{8,9},{9,8},{10,11... | collective-permute-start | bytes 983048 | tf_op jit(solution)/shard_map/ppermute | solution.py:315
  99.6 1.2 collective-permute-done
  100.9 9.4 %all_to_all.54 = f32[16,40,128]{2,1,0:T(8,128)S(1)} all-to-all(f32[16,40,128]{2,1,0:T(8,128)S(1)} %bitcast.22), channel_id=1, replica_groups=mesh['gu'=2,'gv'=4,'gk'=2,'gh'=2,'gl'=2,'gw'=2,'gp'=2,'gc'=2] {'gw','gk'..., dimensions={0} | all-to-all | bytes 655360 | tf_op jit(solution)/shard_map/all_to_all | solution.py:260
  110.3 16.5 %all_to_all.55 = f32[16,40,128]{2,1,0:T(8,128)S(1)} all-to-all(f32[16,40,128]{2,1,0:T(8,128)S(1)} %broadcast_in_dim.14), channel_id=1, replica_groups=mesh['gu'=2,'gv'=4,'gk'=2,'gh'=2,'gl'=2,'gw'=2,'gp'=2,'gc'=2] {'gv','gu'..., dimensions={0} | all-to-all | bytes 655360 | tf_op jit(solution)/shard_map/all_to_all | solution.py:260
  126.9 10.7 %all_to_all.56 = f32[16,40,128]{2,1,0:T(8,128)S(1)} all-to-all(f32[16,40,128]{2,1,0:T(8,128)S(1)} %broadcast_in_dim.15), channel_id=1, replica_groups=mesh['gu'=2,'gv'=4,'gk'=2,'gh'=2,'gl'=2,'gw'=2,'gp'=2,'gc'=2] {'gw','gk'..., dimensions={0} | all-to-all | bytes 655360 | tf_op jit(solution)/shard_map/all_to_all | solution.py:260
  137.7 5.6 %collective-permute-start.1 = (f32[640,128]{1,0:T(8,128)S(1)}, f32[640,128]{1,0:T(8,128)S(1)}, u32[]{:S(2)}, u32[]{:S(2)}) collective-permute-start(f32[640,128]{1,0:T(8,128)S(1)} %bitcast.17), channel_id=1, source_target_pairs={{0,1},{1,0},{2,3},{3,2},{4,5},{5,4},{6,7},{7,6},{8,9},{9,8},{10,11... | collective-permute-start | bytes 983048 | tf_op jit(solution)/shard_map/ppermute | solution.py:319
  143.3 1.2 collective-permute-done.1.other_ref
  144.5 3.0 %shard_map.58 = f32[2,2,8,2,2,8,128]{6,5,4,3,2,1,0:T(8,128)S(1)} custom-call(f32[640,128]{1,0:T(8,128)S(1)} %bitcast.18, f32[640,128]{1,0:T(8,128)S(1)} %collective-permute-done.1.other_ref, f32[32,512]{1,0:T(8,128)S(1)} %get-tuple-element.20.start_ref, f32[128,512]{1,0:T(8,128)S(1)} %get-tuple-element.21.merged_ref), custom_call_target="tpu_custom_call" | custom-call | tf_op jit(solution)/shard_map/pallas_call | solution.py:245
  147.5 28.5 %all_to_all.57 = f32[256,4,128]{2,1,0:T(4,128)S(1)} all-to-all(f32[256,4,128]{2,1,0:T(4,128)S(1)} %bitcast.14), channel_id=1, replica_groups=mesh['gu'=2,'gv'=4,'gk'=2,'gh'=2,'gl'=2,'gw'=2,'gp'=2,'gc'=2] {'gh','gl'..., dimensions={0} | all-to-all | bytes 1048576 | tf_op jit(solution)/shard_map/all_to_all | solution.py:260
  176.0 4.0 %collective-permute-start.2 = (f32[1024,128]{1,0:T(8,128)S(1)}, f32[1024,128]{1,0:T(8,128)S(1)}, u32[]{:S(2)}, u32[]{:S(2)}) collective-permute-start(f32[1024,128]{1,0:T(8,128)S(1)} %bitcast.15), channel_id=1, source_target_pairs={{0,1},{1,0},{2,3},{3,2},{4,5},{5,4},{6,7},{7,6},{8,9},{9,8},{10,11... | collective-permute-start | bytes 1572872 | tf_op jit(solution)/shard_map/ppermute | solution.py:331
  180.0 1.5 collective-permute-done.2.other_ref
  181.5 0.7 shard_map.59
  182.2 12.0 %all_to_all.58.parts_ref = f32[8,32,512]{2,1,0:T(8,128)S(1)} all-to-all(f32[8,32,512]{2,1,0:T(8,128)S(1)} %get-tuple-element.22), channel_id=1, replica_groups=mesh['gu'=2,'gv'=4,'gk'=2,'gh'=2,'gl'=2,'gw'=2,'gp'=2,'gc'=2] {'gk','gp'..., dimensions={0} | all-to-all | bytes 1048576 | tf_op jit(solution)/shard_map/all_to_all | solution.py:260
  194.2 1.6 shard_map.60
  195.8 10.6 %all_to_all.59.parts_ref = f32[8,32,512]{2,1,0:T(8,128)S(1)} all-to-all(f32[8,32,512]{2,1,0:T(8,128)S(1)} %shard_map.60), channel_id=1, replica_groups=mesh['gu'=2,'gv'=4,'gk'=2,'gh'=2,'gl'=2,'gw'=2,'gp'=2,'gc'=2] {'gk','gp'..., dimensions={0} | all-to-all | bytes 1048576 | tf_op jit(solution)/shard_map/all_to_all | solution.py:260
  206.4 1.9 shard_map.61
  (9 shorter events, 0.2 us)
Async XLA Ops:
  97.3 3.6 %collective-permute-start = (f32[640,128]{1,0:T(8,128)S(1)}, f32[640,128]{1,0:T(8,128)S(1)}, u32[]{:S(2)}, u32[]{:S(2)}) collective-permute-start(f32[640,128]{1,0:T(8,128)S(1)} %get-tuple-element.19), channel_id=1, source_target_pairs={{0,1},{1,0},{2,3},{3,2},{4,5},{5,4},{6,7},{7,6},{8,9},{9,8},{10,11... | collective-permute-start | bytes 983048 | tf_op jit(solution)/shard_map/ppermute | solution.py:315
  137.7 6.8 %collective-permute-start.1 = (f32[640,128]{1,0:T(8,128)S(1)}, f32[640,128]{1,0:T(8,128)S(1)}, u32[]{:S(2)}, u32[]{:S(2)}) collective-permute-start(f32[640,128]{1,0:T(8,128)S(1)} %bitcast.17), channel_id=1, source_target_pairs={{0,1},{1,0},{2,3},{3,2},{4,5},{5,4},{6,7},{7,6},{8,9},{9,8},{10,11... | collective-permute-start | bytes 983048 | tf_op jit(solution)/shard_map/ppermute | solution.py:319
  176.0 5.5 %collective-permute-start.2 = (f32[1024,128]{1,0:T(8,128)S(1)}, f32[1024,128]{1,0:T(8,128)S(1)}, u32[]{:S(2)}, u32[]{:S(2)}) collective-permute-start(f32[1024,128]{1,0:T(8,128)S(1)} %bitcast.15), channel_id=1, source_target_pairs={{0,1},{1,0},{2,3},{3,2},{4,5},{5,4},{6,7},{7,6},{8,9},{9,8},{10,11... | collective-permute-start | bytes 1572872 | tf_op jit(solution)/shard_map/ppermute | solution.py:331

commit v12 on v11

--- a/solution.py
+++ b/solution.py
@@ -14,9 +14,9 @@
 FINE = ("gu", "gv", "gk", "gh", "gl", "gw", "gp", "gc")
 CHIPS = ("gh", "gl", "gu", "gv", "gk", "gw", "gp")
 ORDER = CHIPS + ("gc",)
-NEAR = ("gk", "gp", "gl")
+NEAR = ("gl", "gk", "gp")
 CLOSE = ("gw", "gl", "gp", "gc")
-FAR = ("gv", "gu", "gk", "gh")
+FAR = ("gh", "gu", "gv", "gk")
 BLOCK = ("gw", "gk", "gp", "gl")
 BEYOND = ("gv", "gu", "gh")
 

time: 210 us -> 208 us (level)
  blocking collectives: 179 us -> 176 us
    all_to_all x10, blocking collectives: 179 us -> 176 us  [swap(): return lax.all_to_all(pieces, axes, split_axis=0, concat_axis=0, tiled=True)]
where the time goes in v12:
time: 208 us; the launch traced here: 206 us
  blocking collectives  176 us (85%)
  starting transfers between devices  12.9 us (6%)
  Pallas kernels  12.7 us (6%)
  waiting for transfers between devices  3.98 us (2%)
    all_to_all x10, blocking collectives, swap(): return lax.all_to_all(pieces, axes, split_axis=0, concat_axis=0, tiled=True)  176 us
    pallas_call x7, Pallas kernels, call(): pl.pallas_call(kernel, out_shape=out_shape, in_specs=[hbm] * in_hbm + [vm...  12.7 us
    ppermute x2, starting transfers between devices, shards(): other = lax.ppermute(own, 'gc', exchange)  10.5 us
  transfers between devices with their start and end apart: 3, of which 3 were waited for; matrix products, arithmetic and copies ran while one was open for 0% of the time, Pallas kernels for 0%

profile of v12, /device:TPU:1, one launch (start us, length us, event | category | flops | bytes accessed | tf_op | source)
XLA Modules:
  0.0 206.2 jit_solution(5954706079797438087)
XLA Ops:
  0.0 1.8 shard_map.55
  1.8 54.3 %all_to_all.50 = f32[512,4,128]{2,1,0:T(4,128)S(1)} all-to-all(f32[512,4,128]{2,1,0:T(4,128)S(1)} %bitcast.19), channel_id=1, replica_groups=mesh['gu'=2,'gv'=4,'gk'=2,'gh'=2,'gl'=2,'gw'=2,'gp'=2,'gc'=2] {'gh','gl'..., dimensions={0} | all-to-all | bytes 2097152 | tf_op jit(solution)/shard_map/all_to_all | solution.py:260
  56.1 0.6 shard_map.56
  56.7 9.9 %all_to_all.51 = f32[16,8,128]{2,1,0:T(8,128)S(1)} all-to-all(f32[16,8,128]{2,1,0:T(8,128)S(1)} %bitcast.21), channel_id=1, replica_groups=mesh['gu'=2,'gv'=4,'gk'=2,'gh'=2,'gl'=2,'gw'=2,'gp'=2,'gc'=2] {'gw','gl'..., dimensions={0} | all-to-all | bytes 131072 | tf_op jit(solution)/shard_map/all_to_all | solution.py:260
  66.6 16.9 %all_to_all.52 = f32[32,8,128]{2,1,0:T(8,128)S(1)} all-to-all(f32[32,8,128]{2,1,0:T(8,128)S(1)} %broadcast_in_dim.12), channel_id=1, replica_groups=mesh['gu'=2,'gv'=4,'gk'=2,'gh'=2,'gl'=2,'gw'=2,'gp'=2,'gc'=2] {'gh','gu'..., dimensions={0} | all-to-all | bytes 262144 | tf_op jit(solution)/shard_map/all_to_all | solution.py:260
  83.5 10.6 %all_to_all.53 = f32[16,8,128]{2,1,0:T(8,128)S(1)} all-to-all(f32[16,8,128]{2,1,0:T(8,128)S(1)} %broadcast_in_dim.13), channel_id=1, replica_groups=mesh['gu'=2,'gv'=4,'gk'=2,'gh'=2,'gl'=2,'gw'=2,'gp'=2,'gc'=2] {'gw','gl'..., dimensions={0} | all-to-all | bytes 131072 | tf_op jit(solution)/shard_map/all_to_all | solution.py:260
  94.0 3.1 %shard_map.57 = (f32[128,512]{1,0:T(8,128)S(1)}, f32[640,128]{1,0:T(8,128)S(1)}, f32[640,128]{1,0:T(8,128)S(1)}) custom-call(f32[128,128]{1,0:T(8,128)S(1)} %bitcast.20, f32[32,128]{1,0:T(8,128)S(1)} %get-tuple-element.17.start_ref, f32[2048,128]{1,0:T(8,128)S(1)} %bitcast.13), custom_call_target="tpu_custom_call" | custom-call | tf_op jit(solution)/shard_map/pallas_call | solution.py:245
  97.1 2.3 %collective-permute-start = (f32[640,128]{1,0:T(8,128)S(1)}, f32[640,128]{1,0:T(8,128)S(1)}, u32[]{:S(2)}, u32[]{:S(2)}) collective-permute-start(f32[640,128]{1,0:T(8,128)S(1)} %get-tuple-element.19), channel_id=1, source_target_pairs={{0,1},{1,0},{2,3},{3,2},{4,5},{5,4},{6,7},{7,6},{8,9},{9,8},{10,11... | collective-permute-start | bytes 983048 | tf_op jit(solution)/shard_map/ppermute | solution.py:315
  99.5 1.2 collective-permute-done
  100.8 9.5 %all_to_all.54 = f32[16,40,128]{2,1,0:T(8,128)S(1)} all-to-all(f32[16,40,128]{2,1,0:T(8,128)S(1)} %bitcast.22), channel_id=1, replica_groups=mesh['gu'=2,'gv'=4,'gk'=2,'gh'=2,'gl'=2,'gw'=2,'gp'=2,'gc'=2] {'gw','gk'..., dimensions={0} | all-to-all | bytes 655360 | tf_op jit(solution)/shard_map/all_to_all | solution.py:260
  110.3 16.6 %all_to_all.55 = f32[16,40,128]{2,1,0:T(8,128)S(1)} all-to-all(f32[16,40,128]{2,1,0:T(8,128)S(1)} %broadcast_in_dim.14), channel_id=1, replica_groups=mesh['gu'=2,'gv'=4,'gk'=2,'gh'=2,'gl'=2,'gw'=2,'gp'=2,'gc'=2] {'gv','gu'..., dimensions={0} | all-to-all | bytes 655360 | tf_op jit(solution)/shard_map/all_to_all | solution.py:260
  127.0 9.8 %all_to_all.56 = f32[16,40,128]{2,1,0:T(8,128)S(1)} all-to-all(f32[16,40,128]{2,1,0:T(8,128)S(1)} %broadcast_in_dim.15), channel_id=1, replica_groups=mesh['gu'=2,'gv'=4,'gk'=2,'gh'=2,'gl'=2,'gw'=2,'gp'=2,'gc'=2] {'gw','gk'..., dimensions={0} | all-to-all | bytes 655360 | tf_op jit(solution)/shard_map/all_to_all | solution.py:260
  136.8 6.5 %collective-permute-start.1 = (f32[640,128]{1,0:T(8,128)S(1)}, f32[640,128]{1,0:T(8,128)S(1)}, u32[]{:S(2)}, u32[]{:S(2)}) collective-permute-start(f32[640,128]{1,0:T(8,128)S(1)} %bitcast.17), channel_id=1, source_target_pairs={{0,1},{1,0},{2,3},{3,2},{4,5},{5,4},{6,7},{7,6},{8,9},{9,8},{10,11... | collective-permute-start | bytes 983048 | tf_op jit(solution)/shard_map/ppermute | solution.py:319
  143.3 1.2 collective-permute-done.1.other_ref
  144.5 3.0 %shard_map.58 = f32[2,2,8,2,2,8,128]{6,5,4,3,2,1,0:T(8,128)S(1)} custom-call(f32[640,128]{1,0:T(8,128)S(1)} %bitcast.18, f32[640,128]{1,0:T(8,128)S(1)} %collective-permute-done.1.other_ref, f32[32,512]{1,0:T(8,128)S(1)} %get-tuple-element.20.start_ref, f32[128,512]{1,0:T(8,128)S(1)} %get-tuple-element.21.merged_ref), custom_call_target="tpu_custom_call" | custom-call | tf_op jit(solution)/shard_map/pallas_call | solution.py:245
  147.5 28.0 %all_to_all.57 = f32[256,4,128]{2,1,0:T(4,128)S(1)} all-to-all(f32[256,4,128]{2,1,0:T(4,128)S(1)} %bitcast.14), channel_id=1, replica_groups=mesh['gu'=2,'gv'=4,'gk'=2,'gh'=2,'gl'=2,'gw'=2,'gp'=2,'gc'=2] {'gh','gl'..., dimensions={0} | all-to-all | bytes 1048576 | tf_op jit(solution)/shard_map/all_to_all | solution.py:260
  175.6 4.0 %collective-permute-start.2 = (f32[1024,128]{1,0:T(8,128)S(1)}, f32[1024,128]{1,0:T(8,128)S(1)}, u32[]{:S(2)}, u32[]{:S(2)}) collective-permute-start(f32[1024,128]{1,0:T(8,128)S(1)} %bitcast.15), channel_id=1, source_target_pairs={{0,1},{1,0},{2,3},{3,2},{4,5},{5,4},{6,7},{7,6},{8,9},{9,8},{10,11... | collective-permute-start | bytes 1572872 | tf_op jit(solution)/shard_map/ppermute | solution.py:331
  179.6 1.5 collective-permute-done.2.other_ref
  181.1 0.7 shard_map.59
  181.8 11.4 %all_to_all.58.parts_ref = f32[8,32,512]{2,1,0:T(8,128)S(1)} all-to-all(f32[8,32,512]{2,1,0:T(8,128)S(1)} %get-tuple-element.22), channel_id=1, replica_groups=mesh['gu'=2,'gv'=4,'gk'=2,'gh'=2,'gl'=2,'gw'=2,'gp'=2,'gc'=2] {'gl','gk'..., dimensions={0} | all-to-all | bytes 1048576 | tf_op jit(solution)/shard_map/all_to_all | solution.py:260
  193.2 1.6 shard_map.60
  194.8 9.4 %all_to_all.59.parts_ref = f32[8,32,512]{2,1,0:T(8,128)S(1)} all-to-all(f32[8,32,512]{2,1,0:T(8,128)S(1)} %shard_map.60), channel_id=1, replica_groups=mesh['gu'=2,'gv'=4,'gk'=2,'gh'=2,'gl'=2,'gw'=2,'gp'=2,'gc'=2] {'gl','gk'..., dimensions={0} | all-to-all | bytes 1048576 | tf_op jit(solution)/shard_map/all_to_all | solution.py:260
  204.3 1.9 shard_map.61
  (9 shorter events, 0.2 us)
Async XLA Ops:
  97.1 3.6 %collective-permute-start = (f32[640,128]{1,0:T(8,128)S(1)}, f32[640,128]{1,0:T(8,128)S(1)}, u32[]{:S(2)}, u32[]{:S(2)}) collective-permute-start(f32[640,128]{1,0:T(8,128)S(1)} %get-tuple-element.19), channel_id=1, source_target_pairs={{0,1},{1,0},{2,3},{3,2},{4,5},{5,4},{6,7},{7,6},{8,9},{9,8},{10,11... | collective-permute-start | bytes 983048 | tf_op jit(solution)/shard_map/ppermute | solution.py:315
  136.8 7.7 %collective-permute-start.1 = (f32[640,128]{1,0:T(8,128)S(1)}, f32[640,128]{1,0:T(8,128)S(1)}, u32[]{:S(2)}, u32[]{:S(2)}) collective-permute-start(f32[640,128]{1,0:T(8,128)S(1)} %bitcast.17), channel_id=1, source_target_pairs={{0,1},{1,0},{2,3},{3,2},{4,5},{5,4},{6,7},{7,6},{8,9},{9,8},{10,11... | collective-permute-start | bytes 983048 | tf_op jit(solution)/shard_map/ppermute | solution.py:319
  175.6 5.6 %collective-permute-start.2 = (f32[1024,128]{1,0:T(8,128)S(1)}, f32[1024,128]{1,0:T(8,128)S(1)}, u32[]{:S(2)}, u32[]{:S(2)}) collective-permute-start(f32[1024,128]{1,0:T(8,128)S(1)} %bitcast.15), channel_id=1, source_target_pairs={{0,1},{1,0},{2,3},{3,2},{4,5},{5,4},{6,7},{7,6},{8,9},{9,8},{10,11... | collective-permute-start | bytes 1572872 | tf_op jit(solution)/shard_map/ppermute | solution.py:331

commit v13 on v12

--- a/solution.py
+++ b/solution.py
@@ -69,14 +69,13 @@
 
 
 def send_field_kernel(
-    order_hbm, field_hbm, first_hbm, second_hbm, third_hbm, out_ref, first_ref, second_ref, third_ref, field_ref,
-    raw_ref, rows_ref, placed_ref, order_ref, sems, start_sems, *, brick_len
+    order_hbm, field_hbm, first_hbm, second_hbm, out_ref, first_ref, second_ref, field_ref, order_ref, sems, start_sems, *, brick_len
 ):
     species, cells_y, cells_z = field_hbm.shape
     loads = [pltpu.make_async_copy(field_hbm.at[s], field_ref.at[s], sems.at[s]) for s in range(species)]
-    pairs = (order_hbm, order_ref), (third_hbm, raw_ref), (second_hbm, second_ref), (first_hbm, first_ref)
+    pairs = (order_hbm, order_ref), (second_hbm, second_ref), (first_hbm, first_ref)
     starts = [pltpu.make_async_copy(source, target, start_sems.at[i]) for i, (source, target) in enumerate(pairs)]
-    for load in starts[:2] + loads + starts[2:]:
+    for load in starts[:1] + loads + starts[1:]:
         load.start()
     starts[0].wait()
     lane = lax.broadcasted_iota(jnp.int32, (1, cells_z), 1)
@@ -86,23 +85,34 @@
         place = jnp.where(brick == b, order_ref[b] * brick_len, place)
     grid_z = (place + lane % brick_len).astype(jnp.float32)
     taper = 0.5 + 1.5 * grid_z / (cells_z - 1)
-    starts[1].wait()
-    rows_ref[...] = raw_ref[...].T
-    for b in range(cells_z // brick_len):
-        at = pl.multiple_of(order_ref[b] * brick_len, brick_len)
-        placed_ref[b * brick_len : (b + 1) * brick_len, :] = rows_ref[pl.ds(at, brick_len), :]
-    core = lax.axis_index("gc")
-    half = cells_z // 2
-    third_ref[:, :half] = placed_ref[pl.ds(core, half, stride=2), :].T
-    third_ref[:, half:] = placed_ref[pl.ds(1 - core, half, stride=2), :].T
     for s in range(species):
         loads[s].wait()
         for j in range(cells_z // LANES):
             cut = slice(j * LANES, (j + 1) * LANES)
             block = field_ref[s, :, cut] * taper[:, cut]
             out_ref[pl.ds(j * LANES * species + s, LANES, stride=species), :] = block.T
-    for load in starts[2:]:
+    for load in starts[1:]:
         load.wait()
+
+
+def place_third_kernel(order_hbm, third_hbm, third_ref, raw_ref, rows_ref, placed_ref, order_ref, sems, *, brick_len):
+    loads = [
+        pltpu.make_async_copy(source, target, sems.at[i])
+        for i, (source, target) in enumerate(((order_hbm, order_ref), (third_hbm, raw_ref)))
+    ]
+    for load in loads:
+        load.start()
+    for load in loads:
+        load.wait()
+    size = rows_ref.shape[0]
+    rows_ref[...] = raw_ref[...].T
+    for b in range(size // brick_len):
+        at = pl.multiple_of(order_ref[b] * brick_len, brick_len)
+        placed_ref[b * brick_len : (b + 1) * brick_len, :] = rows_ref[pl.ds(at, brick_len), :]
+    core = lax.axis_index("gc")
+    half = size // 2
+    third_ref[:, :half] = placed_ref[pl.ds(core, half, stride=2), :].T
+    third_ref[:, half:] = placed_ref[pl.ds(1 - core, half, stride=2), :].T
 
 
 def fibre(ref, s, species, rows_x, parts):
@@ -239,7 +249,7 @@
             out_ref[b, e, :] = rows_ref[at + e * (LANES // 4) + b, :]
 
 
-def call(kernel, out_shape, *args, scratch=(), in_hbm=0):
+def call(kernel, out_shape, *args, scratch=(), in_hbm=0, limit=None):
     vmem = pl.BlockSpec(memory_space=pltpu.VMEM)
     hbm = pl.BlockSpec(memory_space=pltpu.HBM)
     return pl.pallas_call(
@@ -247,7 +257,7 @@
         out_shape=out_shape,
         in_specs=[hbm] * in_hbm + [vmem] * (len(args) - in_hbm),
         out_specs=jax.tree.map(lambda _: vmem, out_shape),
-        compiler_params=pltpu.CompilerParams(vmem_limit_bytes=None if in_hbm else VMEM_BYTES),
+        compiler_params=pltpu.CompilerParams(vmem_limit_bytes=limit if in_hbm else VMEM_BYTES),
         scratch_shapes=[pltpu.VMEM(s, jnp.float32) if isinstance(s, tuple) else s for s in scratch],
     )(*args[:in_hbm], *[pltpu.with_memory_space_constraint(a, pltpu.VMEM) for a in args[in_hbm:]])
 
@@ -276,24 +286,20 @@
     parts_y = full_y // LANES
     exchange = [(0, 1), (1, 0)]
 
-    sent, start_first, start_second, start_third = call(
+    sent, start_first, start_second = call(
         functools.partial(send_field_kernel, brick_len=brick_len),
-        (vm(cells_z * species, cells_y), vm(rank_one, rows_x), vm(rank_two, full_y), vm(rank_three, cells_z)),
+        (vm(cells_z * species, cells_y), vm(rank_one, rows_x), vm(rank_two, full_y)),
         brick_order,
         field.reshape(species, cells_y, cells_z),
         start_first.T,
         start_second.T,
-        start_third.T,
         scratch=[
             (species, cells_y, cells_z),
-            (rank_three, cells_z),
-            (cells_z, rank_three),
-            (cells_z, rank_three),
             pltpu.SMEM(brick_order.shape, jnp.int32),
             pltpu.SemaphoreType.DMA((species,)),
-            pltpu.SemaphoreType.DMA((4,)),
+            pltpu.SemaphoreType.DMA((3,)),
         ],
-        in_hbm=5,
+        in_hbm=4,
     )
     data = swap(sent.reshape(devices, species, cells_y), ORDER).reshape(devices * species, cells_y)
 
@@ -312,7 +318,25 @@
         data,
         scratch=[(rank_one, rows_x)],
     )
-    gram = kept + lax.ppermute(sent, "gc", exchange)
+    swapped = lax.ppermute(sent, "gc", exchange)
+    raw_third, kept = lax.optimization_barrier((start_third.T, kept))
+    start_third = call(
+        functools.partial(place_third_kernel, brick_len=brick_len),
+        vm(rank_three, cells_z),
+        brick_order,
+        raw_third,
+        scratch=[
+            (rank_three, cells_z),
+            (cells_z, rank_three),
+            (cells_z, rank_three),
+            pltpu.SMEM(brick_order.shape, jnp.int32),
+            pltpu.SemaphoreType.DMA((2,)),
+        ],
+        in_hbm=2,
+        limit=VMEM_BYTES,
+    )
+    kept, start_third = lax.optimization_barrier((kept, start_third))
+    gram = kept + swapped
     gram = jnp.sum(swap(gram.reshape(lax.axis_size(BLOCK), -1, LANES), BLOCK), axis=0)
     gram = jnp.sum(swap(copies(gram, BEYOND), BEYOND), axis=0)
     own = swap(copies(gram, BLOCK), BLOCK).reshape(-1, LANES)

time: 208 us -> 209 us (level)
    pallas_call x7 -> x8, Pallas kernels: 12.7 us -> 13.2 us  [call(): pl.pallas_call(kernel, out_shape=out_shape, in_specs=[hbm] * in_hbm + [vm...]
  transfers between devices with their start and end apart: 3 -> 3, of which waited for: 3 -> 2; matrix products, arithmetic and copies ran while one was open for 0% -> 0% of each run, Pallas kernels for 0% -> 0%
where the time goes in v13:
time: 209 us; the launch traced here: 207 us
  blocking collectives  178 us (85%)
  Pallas kernels  13.2 us (6%)
  starting transfers between devices  11.6 us (6%)
  waiting for transfers between devices  2.75 us (1%)
    all_to_all x10, blocking collectives, swap(): return lax.all_to_all(pieces, axes, split_axis=0, concat_axis=0, tiled=True)  178 us
    pallas_call x8, Pallas kernels, call(): pl.pallas_call(kernel, out_shape=out_shape, in_specs=[hbm] * in_hbm + [vm...  13.2 us
    ppermute x2, starting transfers between devices, shards(): other = lax.ppermute(own, 'gc', exchange)  9.23 us
  transfers between devices with their start and end apart: 3, of which 2 were waited for; matrix products, arithmetic and copies ran while one was open for 0% of the time, Pallas kernels for 0%

profile of v13, /device:TPU:1, one launch (start us, length us, event | category | flops | bytes accessed | tf_op | source)
XLA Modules:
  0.0 206.5 jit_solution(11585737161288177176)
XLA Ops:
  0.0 1.6 shard_map.55
  1.6 54.3 %all_to_all.50 = f32[512,4,128]{2,1,0:T(4,128)S(1)} all-to-all(f32[512,4,128]{2,1,0:T(4,128)S(1)} %bitcast.19), channel_id=1, replica_groups=mesh['gu'=2,'gv'=4,'gk'=2,'gh'=2,'gl'=2,'gw'=2,'gp'=2,'gc'=2] {'gh','gl'..., dimensions={0} | all-to-all | bytes 2097152 | tf_op jit(solution)/shard_map/all_to_all | solution.py:270
  55.9 0.6 shard_map.56
  56.4 9.9 %all_to_all.51 = f32[16,8,128]{2,1,0:T(8,128)S(1)} all-to-all(f32[16,8,128]{2,1,0:T(8,128)S(1)} %bitcast.21), channel_id=1, replica_groups=mesh['gu'=2,'gv'=4,'gk'=2,'gh'=2,'gl'=2,'gw'=2,'gp'=2,'gc'=2] {'gw','gl'..., dimensions={0} | all-to-all | bytes 131072 | tf_op jit(solution)/shard_map/all_to_all | solution.py:270
  66.3 16.9 %all_to_all.52 = f32[32,8,128]{2,1,0:T(8,128)S(1)} all-to-all(f32[32,8,128]{2,1,0:T(8,128)S(1)} %broadcast_in_dim.12), channel_id=1, replica_groups=mesh['gu'=2,'gv'=4,'gk'=2,'gh'=2,'gl'=2,'gw'=2,'gp'=2,'gc'=2] {'gh','gu'..., dimensions={0} | all-to-all | bytes 262144 | tf_op jit(solution)/shard_map/all_to_all | solution.py:270
  83.2 10.6 %all_to_all.53 = f32[16,8,128]{2,1,0:T(8,128)S(1)} all-to-all(f32[16,8,128]{2,1,0:T(8,128)S(1)} %broadcast_in_dim.13), channel_id=1, replica_groups=mesh['gu'=2,'gv'=4,'gk'=2,'gh'=2,'gl'=2,'gw'=2,'gp'=2,'gc'=2] {'gw','gl'..., dimensions={0} | all-to-all | bytes 131072 | tf_op jit(solution)/shard_map/all_to_all | solution.py:270
  93.8 0.0 copy-start
  93.8 3.1 %shard_map.57 = (f32[128,512]{1,0:T(8,128)S(1)}, f32[640,128]{1,0:T(8,128)S(1)}, f32[640,128]{1,0:T(8,128)S(1)}) custom-call(f32[128,128]{1,0:T(8,128)S(1)} %bitcast.20, f32[32,128]{1,0:T(8,128)S(1)} %get-tuple-element.19.start_ref, f32[2048,128]{1,0:T(8,128)S(1)} %bitcast.13), custom_call_target="tpu_custom_call" | custom-call | tf_op jit(solution)/shard_map/pallas_call | solution.py:255
  96.9 2.3 %collective-permute-start = (f32[640,128]{1,0:T(8,128)S(1)}, f32[640,128]{1,0:T(8,128)S(1)}, u32[]{:S(2)}, u32[]{:S(2)}) collective-permute-start(f32[640,128]{1,0:T(8,128)S(1)} %get-tuple-element.25), channel_id=1, source_target_pairs={{0,1},{1,0},{2,3},{3,2},{4,5},{5,4},{6,7},{7,6},{8,9},{9,8},{10,11... | collective-permute-start | bytes 983048 | tf_op jit(solution)/shard_map/ppermute | solution.py:321
  99.2 0.0 copy-start.1
  99.2 0.0 copy-done
  99.3 0.6 copy-done.1
  99.9 0.8 shard_map.58.start_ref
  100.7 0.0 collective-permute-done
  100.8 9.6 %all_to_all.54 = f32[16,40,128]{2,1,0:T(8,128)S(1)} all-to-all(f32[16,40,128]{2,1,0:T(8,128)S(1)} %bitcast.23), channel_id=1, replica_groups=mesh['gu'=2,'gv'=4,'gk'=2,'gh'=2,'gl'=2,'gw'=2,'gp'=2,'gc'=2] {'gw','gk'..., dimensions={0} | all-to-all | bytes 655360 | tf_op jit(solution)/shard_map/all_to_all | solution.py:270
  110.5 16.6 %all_to_all.55 = f32[16,40,128]{2,1,0:T(8,128)S(1)} all-to-all(f32[16,40,128]{2,1,0:T(8,128)S(1)} %broadcast_in_dim.14), channel_id=1, replica_groups=mesh['gu'=2,'gv'=4,'gk'=2,'gh'=2,'gl'=2,'gw'=2,'gp'=2,'gc'=2] {'gv','gu'..., dimensions={0} | all-to-all | bytes 655360 | tf_op jit(solution)/shard_map/all_to_all | solution.py:270
  127.1 11.1 %all_to_all.56 = f32[16,40,128]{2,1,0:T(8,128)S(1)} all-to-all(f32[16,40,128]{2,1,0:T(8,128)S(1)} %broadcast_in_dim.15), channel_id=1, replica_groups=mesh['gu'=2,'gv'=4,'gk'=2,'gh'=2,'gl'=2,'gw'=2,'gp'=2,'gc'=2] {'gw','gk'..., dimensions={0} | all-to-all | bytes 655360 | tf_op jit(solution)/shard_map/all_to_all | solution.py:270
  138.3 5.2 %collective-permute-start.1 = (f32[640,128]{1,0:T(8,128)S(1)}, f32[640,128]{1,0:T(8,128)S(1)}, u32[]{:S(2)}, u32[]{:S(2)}) collective-permute-start(f32[640,128]{1,0:T(8,128)S(1)} %bitcast.17), channel_id=1, source_target_pairs={{0,1},{1,0},{2,3},{3,2},{4,5},{5,4},{6,7},{7,6},{8,9},{9,8},{10,11... | collective-permute-start | bytes 983048 | tf_op jit(solution)/shard_map/ppermute | solution.py:343
  143.5 1.2 collective-permute-done.1.other_ref
  144.7 3.0 %shard_map.59 = f32[2,2,8,2,2,8,128]{6,5,4,3,2,1,0:T(8,128)S(1)} custom-call(f32[640,128]{1,0:T(8,128)S(1)} %bitcast.18, f32[640,128]{1,0:T(8,128)S(1)} %collective-permute-done.1.other_ref, f32[32,512]{1,0:T(8,128)S(1)} %get-tuple-element.26.start_ref, f32[128,512]{1,0:T(8,128)S(1)} %get-tuple-element.27.merged_ref), custom_call_target="tpu_custom_call" | custom-call | tf_op jit(solution)/shard_map/pallas_call | solution.py:255
  147.7 28.2 %all_to_all.57 = f32[256,4,128]{2,1,0:T(4,128)S(1)} all-to-all(f32[256,4,128]{2,1,0:T(4,128)S(1)} %bitcast.14), channel_id=1, replica_groups=mesh['gu'=2,'gv'=4,'gk'=2,'gh'=2,'gl'=2,'gw'=2,'gp'=2,'gc'=2] {'gh','gl'..., dimensions={0} | all-to-all | bytes 1048576 | tf_op jit(solution)/shard_map/all_to_all | solution.py:270
  175.9 4.0 %collective-permute-start.2 = (f32[1024,128]{1,0:T(8,128)S(1)}, f32[1024,128]{1,0:T(8,128)S(1)}, u32[]{:S(2)}, u32[]{:S(2)}) collective-permute-start(f32[1024,128]{1,0:T(8,128)S(1)} %bitcast.15), channel_id=1, source_target_pairs={{0,1},{1,0},{2,3},{3,2},{4,5},{5,4},{6,7},{7,6},{8,9},{9,8},{10,11... | collective-permute-start | bytes 1572872 | tf_op jit(solution)/shard_map/ppermute | solution.py:355
  180.0 1.5 collective-permute-done.2.other_ref
  181.5 0.7 shard_map.60
  182.2 11.4 %all_to_all.58.parts_ref = f32[8,32,512]{2,1,0:T(8,128)S(1)} all-to-all(f32[8,32,512]{2,1,0:T(8,128)S(1)} %get-tuple-element.28), channel_id=1, replica_groups=mesh['gu'=2,'gv'=4,'gk'=2,'gh'=2,'gl'=2,'gw'=2,'gp'=2,'gc'=2] {'gl','gk'..., dimensions={0} | all-to-all | bytes 1048576 | tf_op jit(solution)/shard_map/all_to_all | solution.py:270
  193.5 1.6 shard_map.61
  195.2 9.4 %all_to_all.59.parts_ref = f32[8,32,512]{2,1,0:T(8,128)S(1)} all-to-all(f32[8,32,512]{2,1,0:T(8,128)S(1)} %shard_map.61), channel_id=1, replica_groups=mesh['gu'=2,'gv'=4,'gk'=2,'gh'=2,'gl'=2,'gw'=2,'gp'=2,'gc'=2] {'gl','gk'..., dimensions={0} | all-to-all | bytes 1048576 | tf_op jit(solution)/shard_map/all_to_all | solution.py:270
  204.6 1.9 shard_map.62
  (9 shorter events, 0.2 us)
Async XLA Ops:
  93.8 5.4 %copy-start = (f32[512,32]{0,1:T(8,128)S(1)}, f32[512,32]{0,1:T(8,128)}, u32[]{:S(2)}) copy-start(f32[512,32]{0,1:T(8,128)} %param.9) | copy-start | bytes 196612
  96.9 3.8 %collective-permute-start = (f32[640,128]{1,0:T(8,128)S(1)}, f32[640,128]{1,0:T(8,128)S(1)}, u32[]{:S(2)}, u32[]{:S(2)}) collective-permute-start(f32[640,128]{1,0:T(8,128)S(1)} %get-tuple-element.25), channel_id=1, source_target_pairs={{0,1},{1,0},{2,3},{3,2},{4,5},{5,4},{6,7},{7,6},{8,9},{9,8},{10,11... | collective-permute-start | bytes 983048 | tf_op jit(solution)/shard_map/ppermute | solution.py:321
  99.2 0.7 copy-start.1
  138.3 6.4 %collective-permute-start.1 = (f32[640,128]{1,0:T(8,128)S(1)}, f32[640,128]{1,0:T(8,128)S(1)}, u32[]{:S(2)}, u32[]{:S(2)}) collective-permute-start(f32[640,128]{1,0:T(8,128)S(1)} %bitcast.17), channel_id=1, source_target_pairs={{0,1},{1,0},{2,3},{3,2},{4,5},{5,4},{6,7},{7,6},{8,9},{9,8},{10,11... | collective-permute-start | bytes 983048 | tf_op jit(solution)/shard_map/ppermute | solution.py:343
  175.9 5.6 %collective-permute-start.2 = (f32[1024,128]{1,0:T(8,128)S(1)}, f32[1024,128]{1,0:T(8,128)S(1)}, u32[]{:S(2)}, u32[]{:S(2)}) collective-permute-start(f32[1024,128]{1,0:T(8,128)S(1)} %bitcast.15), channel_id=1, source_target_pairs={{0,1},{1,0},{2,3},{3,2},{4,5},{5,4},{6,7},{7,6},{8,9},{9,8},{10,11... | collective-permute-start | bytes 1572872 | tf_op jit(solution)/shard_map/ppermute | solution.py:355

commit v14 on v13

--- a/solution.py
+++ b/solution.py
@@ -130,7 +130,7 @@
 
 
 def second_kernel(
-    gram_ref, start_ref, data_ref, merged_ref, kept_ref, sent_ref, rows_ref, *, species, rows_x, parts
+    gram_ref, start_ref, data_ref, high_ref, low_ref, kept_ref, sent_ref, rows_ref, merged_ref, *, species, rows_x, parts
 ):
     gram = gram_ref[...]
     current = start_ref[...]
@@ -150,6 +150,7 @@
     merged = merged_ref[...]
     flipped = halves(merged.T)
     merged = halves(merged)
+    high_ref[...], low_ref[...] = merged
     blocks = []
     for i in range(parts):
         cut = slice(i * LANES, (i + 1) * LANES)
@@ -178,12 +179,12 @@
     return jnp.concatenate([jnp.concatenate(line, axis=1) for line in lines], axis=0)
 
 
-def third_kernel(own_ref, other_ref, start_ref, merged_ref, out_ref, rows_ref, *, parts):
+def third_kernel(own_ref, other_ref, start_ref, high_ref, low_ref, out_ref, rows_ref, *, parts):
     gram = halves(symmetric_of(lax.axis_index("gc"), own_ref, other_ref, parts))
     current = start_ref[...]
     for repeat in range(ITERS):
         current = orthonormal_rows(mm3(halves(current), gram, NN))
-    rows_ref[...] = mm3(halves(current), halves(merged_ref[...]), NT)
+    rows_ref[...] = mm3(halves(current), (high_ref[...], low_ref[...]), NT)
     quarter = LANES // 4
     groups = [rows_ref[pl.ds(e, rows_ref.shape[0] // 4, stride=4), :] for e in range(4)]
     group_id = lax.broadcasted_iota(jnp.int32, groups[0].shape, 1) // quarter
@@ -201,15 +202,13 @@
                         out_ref[i, h, j, k, w] = piece
 
 
-def columns_of(own_ref, other_ref, parts):
-    size = own_ref.shape[0] // parts
-    return jnp.concatenate(
-        [
-            jnp.concatenate([ref[pl.ds(q, size, stride=parts), :] for q in range(parts)], axis=1)
-            for ref in (own_ref, other_ref)
-        ],
-        axis=0,
-    )
+def columns_of(ref, parts):
+    size = ref.shape[0] // parts
+    return jnp.concatenate([ref[pl.ds(q, size, stride=parts), :] for q in range(parts)], axis=1)
+
+
+def own_third_kernel(own_ref, high_ref, low_ref, *, parts):
+    high_ref[...], low_ref[...] = halves(columns_of(own_ref, parts))
 
 
 def spread(out_ref, wide):
@@ -217,8 +216,9 @@
         out_ref[i] = wide
 
 
-def start_third_kernel(start_ref, own_ref, other_ref, out_ref, high_ref, low_ref, *, parts):
-    data = halves(columns_of(own_ref, other_ref, parts))
+def start_third_kernel(start_ref, own_high_ref, own_low_ref, other_ref, out_ref, high_ref, low_ref, *, parts):
+    high, low = halves(columns_of(other_ref, parts))
+    data = jnp.concatenate([own_high_ref[...], high], axis=0), jnp.concatenate([own_low_ref[...], low], axis=0)
     high_ref[...], low_ref[...] = data
     inner = mm3(halves(start_ref[...]), data, NN)
     spread(out_ref, mm3(halves(inner), data, NT))
@@ -310,13 +310,13 @@
     gram = jnp.sum(swap(copies(gram, FAR), FAR), axis=0)
     gram = swap(copies(gram, CLOSE), CLOSE).reshape(rows_x, rows_x)
 
-    merged, kept, sent = call(
+    high, low, kept, sent = call(
         functools.partial(second_kernel, species=species, rows_x=rows_x, parts=parts_y),
-        (vm(merged_rows, full_y),) + (vm(parts_y * (parts_y + 1) // 4 * LANES, LANES),) * 2,
+        (vm(merged_rows, full_y, dtype=jnp.bfloat16),) * 2 + (vm(parts_y * (parts_y + 1) // 4 * LANES, LANES),) * 2,
         gram,
         start_first,
         data,
-        scratch=[(rank_one, rows_x)],
+        scratch=[(rank_one, rows_x), (merged_rows, full_y)],
     )
     swapped = lax.ppermute(sent, "gc", exchange)
     raw_third, kept = lax.optimization_barrier((start_third.T, kept))
@@ -348,11 +348,14 @@
         own,
         other,
         start_second,
-        merged,
+        high,
+        low,
         scratch=[(rank_two, merged_rows)],
     )
     own = swap(sent.reshape(chips, 4, LANES), CHIPS).reshape(chips * 4, LANES)
     other = lax.ppermute(own, "gc", exchange)
+    own_cut = vm(cells_z // 2, 4 * LANES, dtype=jnp.bfloat16)
+    own_high, own_low = call(functools.partial(own_third_kernel, parts=4), (own_cut, own_cut), own)
 
     spread_shape = vm(lax.axis_size(NEAR), rank_three, cells_z)
     cut = vm(cells_z, 4 * LANES, dtype=jnp.bfloat16)
@@ -360,7 +363,8 @@
         functools.partial(start_third_kernel, parts=4),
         (spread_shape, cut, cut),
         start_third,
-        own,
+        own_high,
+        own_low,
         other,
     )
     for repeat in range(ITERS - 1):

time: 209 us -> 209 us (level)
    pallas_call x8 -> x9, Pallas kernels: 13.2 us -> 13.4 us  [call(): pl.pallas_call(kernel, out_shape=out_shape, in_specs=[hbm] * in_hbm + [vm...]
where the time goes in v14:
time: 209 us; the launch traced here: 207 us
  blocking collectives  178 us (85%)
  Pallas kernels  13.4 us (6%)
  starting transfers between devices  11.6 us (6%)
  waiting for transfers between devices  2.65 us (1%)
    all_to_all x10, blocking collectives, swap(): return lax.all_to_all(pieces, axes, split_axis=0, concat_axis=0, tiled=True)  178 us
    pallas_call x9, Pallas kernels, call(): pl.pallas_call(kernel, out_shape=out_shape, in_specs=[hbm] * in_hbm + [vm...  13.4 us
    ppermute x2, starting transfers between devices, shards(): other = lax.ppermute(own, 'gc', exchange)  9.22 us
  transfers between devices with their start and end apart: 3, of which 2 were waited for; matrix products, arithmetic and copies ran while one was open for 0% of the time, Pallas kernels for 0%

profile of v14, /device:TPU:1, one launch (start us, length us, event | category | flops | bytes accessed | tf_op | source)
XLA Modules:
  0.0 206.6 jit_solution(14930349326542331307)
XLA Ops:
  0.0 1.6 shard_map.55
  1.6 54.3 %all_to_all.50 = f32[512,4,128]{2,1,0:T(4,128)S(1)} all-to-all(f32[512,4,128]{2,1,0:T(4,128)S(1)} %bitcast.19), channel_id=1, replica_groups=mesh['gu'=2,'gv'=4,'gk'=2,'gh'=2,'gl'=2,'gw'=2,'gp'=2,'gc'=2] {'gh','gl'..., dimensions={0} | all-to-all | bytes 2097152 | tf_op jit(solution)/shard_map/all_to_all | solution.py:270
  55.9 0.6 shard_map.56
  56.4 9.9 %all_to_all.51 = f32[16,8,128]{2,1,0:T(8,128)S(1)} all-to-all(f32[16,8,128]{2,1,0:T(8,128)S(1)} %bitcast.21), channel_id=1, replica_groups=mesh['gu'=2,'gv'=4,'gk'=2,'gh'=2,'gl'=2,'gw'=2,'gp'=2,'gc'=2] {'gw','gl'..., dimensions={0} | all-to-all | bytes 131072 | tf_op jit(solution)/shard_map/all_to_all | solution.py:270
  66.3 16.9 %all_to_all.52 = f32[32,8,128]{2,1,0:T(8,128)S(1)} all-to-all(f32[32,8,128]{2,1,0:T(8,128)S(1)} %broadcast_in_dim.12), channel_id=1, replica_groups=mesh['gu'=2,'gv'=4,'gk'=2,'gh'=2,'gl'=2,'gw'=2,'gp'=2,'gc'=2] {'gh','gu'..., dimensions={0} | all-to-all | bytes 262144 | tf_op jit(solution)/shard_map/all_to_all | solution.py:270
  83.2 10.6 %all_to_all.53 = f32[16,8,128]{2,1,0:T(8,128)S(1)} all-to-all(f32[16,8,128]{2,1,0:T(8,128)S(1)} %broadcast_in_dim.13), channel_id=1, replica_groups=mesh['gu'=2,'gv'=4,'gk'=2,'gh'=2,'gl'=2,'gw'=2,'gp'=2,'gc'=2] {'gw','gl'..., dimensions={0} | all-to-all | bytes 131072 | tf_op jit(solution)/shard_map/all_to_all | solution.py:270
  93.8 0.0 copy-start
  93.8 3.1 %shard_map.57 = (bf16[128,512]{1,0:T(8,128)(2,1)S(1)}, bf16[128,512]{1,0:T(8,128)(2,1)S(1)}, f32[640,128]{1,0:T(8,128)S(1)}, f32[640,128]{1,0:T(8,128)S(1)}) custom-call(f32[128,128]{1,0:T(8,128)S(1)} %bitcast.20, f32[32,128]{1,0:T(8,128)S(1)} %get-tuple-element.22.start_ref, f32[2048,128]{1,0:T(8,128)S(1)} %bitcast.13), custom_call_target="tpu_custom_call" | custom-call | tf_op jit(solution)/shard_map/pallas_call | solution.py:255
  96.9 2.3 %collective-permute-start = (f32[640,128]{1,0:T(8,128)S(1)}, f32[640,128]{1,0:T(8,128)S(1)}, u32[]{:S(2)}, u32[]{:S(2)}) collective-permute-start(f32[640,128]{1,0:T(8,128)S(1)} %get-tuple-element.28), channel_id=1, source_target_pairs={{0,1},{1,0},{2,3},{3,2},{4,5},{5,4},{6,7},{7,6},{8,9},{9,8},{10,11... | collective-permute-start | bytes 983048 | tf_op jit(solution)/shard_map/ppermute | solution.py:321
  99.2 0.0 copy-start.1
  99.3 0.0 copy-done
  99.3 0.6 copy-done.1
  99.9 0.8 shard_map.58.start_ref
  100.7 0.0 collective-permute-done
  100.8 9.6 %all_to_all.54 = f32[16,40,128]{2,1,0:T(8,128)S(1)} all-to-all(f32[16,40,128]{2,1,0:T(8,128)S(1)} %bitcast.23), channel_id=1, replica_groups=mesh['gu'=2,'gv'=4,'gk'=2,'gh'=2,'gl'=2,'gw'=2,'gp'=2,'gc'=2] {'gw','gk'..., dimensions={0} | all-to-all | bytes 655360 | tf_op jit(solution)/shard_map/all_to_all | solution.py:270
  110.5 16.6 %all_to_all.55 = f32[16,40,128]{2,1,0:T(8,128)S(1)} all-to-all(f32[16,40,128]{2,1,0:T(8,128)S(1)} %broadcast_in_dim.14), channel_id=1, replica_groups=mesh['gu'=2,'gv'=4,'gk'=2,'gh'=2,'gl'=2,'gw'=2,'gp'=2,'gc'=2] {'gv','gu'..., dimensions={0} | all-to-all | bytes 655360 | tf_op jit(solution)/shard_map/all_to_all | solution.py:270
  127.1 11.1 %all_to_all.56 = f32[16,40,128]{2,1,0:T(8,128)S(1)} all-to-all(f32[16,40,128]{2,1,0:T(8,128)S(1)} %broadcast_in_dim.15), channel_id=1, replica_groups=mesh['gu'=2,'gv'=4,'gk'=2,'gh'=2,'gl'=2,'gw'=2,'gp'=2,'gc'=2] {'gw','gk'..., dimensions={0} | all-to-all | bytes 655360 | tf_op jit(solution)/shard_map/all_to_all | solution.py:270
  138.3 5.2 %collective-permute-start.1 = (f32[640,128]{1,0:T(8,128)S(1)}, f32[640,128]{1,0:T(8,128)S(1)}, u32[]{:S(2)}, u32[]{:S(2)}) collective-permute-start(f32[640,128]{1,0:T(8,128)S(1)} %bitcast.17), channel_id=1, source_target_pairs={{0,1},{1,0},{2,3},{3,2},{4,5},{5,4},{6,7},{7,6},{8,9},{9,8},{10,11... | collective-permute-start | bytes 983048 | tf_op jit(solution)/shard_map/ppermute | solution.py:343
  143.5 1.2 collective-permute-done.1.other_ref
  144.7 3.0 %shard_map.59 = f32[2,2,8,2,2,8,128]{6,5,4,3,2,1,0:T(8,128)S(1)} custom-call(f32[640,128]{1,0:T(8,128)S(1)} %bitcast.18, f32[640,128]{1,0:T(8,128)S(1)} %collective-permute-done.1.other_ref, f32[32,512]{1,0:T(8,128)S(1)} %get-tuple-element.29.start_ref, bf16[128,512]{1,0:T(8,128)(2,1)S(1)} %get-tuple-element.30.high_ref, ...), custom_call_target="tpu_custom_call" | custom-call | tf_op jit(solution)/shard_map/pallas_call | solution.py:255
  147.7 28.2 %all_to_all.57 = f32[256,4,128]{2,1,0:T(4,128)S(1)} all-to-all(f32[256,4,128]{2,1,0:T(4,128)S(1)} %bitcast.14), channel_id=1, replica_groups=mesh['gu'=2,'gv'=4,'gk'=2,'gh'=2,'gl'=2,'gw'=2,'gp'=2,'gc'=2] {'gh','gl'..., dimensions={0} | all-to-all | bytes 1048576 | tf_op jit(solution)/shard_map/all_to_all | solution.py:270
  175.9 4.0 %collective-permute-start.2 = (f32[1024,128]{1,0:T(8,128)S(1)}, f32[1024,128]{1,0:T(8,128)S(1)}, u32[]{:S(2)}, u32[]{:S(2)}) collective-permute-start(f32[1024,128]{1,0:T(8,128)S(1)} %bitcast.15), channel_id=1, source_target_pairs={{0,1},{1,0},{2,3},{3,2},{4,5},{5,4},{6,7},{7,6},{8,9},{9,8},{10,11... | collective-permute-start | bytes 1572872 | tf_op jit(solution)/shard_map/ppermute | solution.py:356
  180.0 0.1 shard_map.60
  180.1 1.4 collective-permute-done.2.other_ref
  181.5 0.7 shard_map.61
  182.2 11.4 %all_to_all.58.parts_ref = f32[8,32,512]{2,1,0:T(8,128)S(1)} all-to-all(f32[8,32,512]{2,1,0:T(8,128)S(1)} %get-tuple-element.34), channel_id=1, replica_groups=mesh['gu'=2,'gv'=4,'gk'=2,'gh'=2,'gl'=2,'gw'=2,'gp'=2,'gc'=2] {'gl','gk'..., dimensions={0} | all-to-all | bytes 1048576 | tf_op jit(solution)/shard_map/all_to_all | solution.py:270
  193.6 1.6 shard_map.62
  195.2 9.4 %all_to_all.59.parts_ref = f32[8,32,512]{2,1,0:T(8,128)S(1)} all-to-all(f32[8,32,512]{2,1,0:T(8,128)S(1)} %shard_map.62), channel_id=1, replica_groups=mesh['gu'=2,'gv'=4,'gk'=2,'gh'=2,'gl'=2,'gw'=2,'gp'=2,'gc'=2] {'gl','gk'..., dimensions={0} | all-to-all | bytes 1048576 | tf_op jit(solution)/shard_map/all_to_all | solution.py:270
  204.7 1.9 shard_map.63
  (9 shorter events, 0.2 us)
Async XLA Ops:
  93.8 5.4 %copy-start = (f32[512,32]{0,1:T(8,128)S(1)}, f32[512,32]{0,1:T(8,128)}, u32[]{:S(2)}) copy-start(f32[512,32]{0,1:T(8,128)} %param.9) | copy-start | bytes 196612
  96.9 3.8 %collective-permute-start = (f32[640,128]{1,0:T(8,128)S(1)}, f32[640,128]{1,0:T(8,128)S(1)}, u32[]{:S(2)}, u32[]{:S(2)}) collective-permute-start(f32[640,128]{1,0:T(8,128)S(1)} %get-tuple-element.28), channel_id=1, source_target_pairs={{0,1},{1,0},{2,3},{3,2},{4,5},{5,4},{6,7},{7,6},{8,9},{9,8},{10,11... | collective-permute-start | bytes 983048 | tf_op jit(solution)/shard_map/ppermute | solution.py:321
  99.2 0.7 copy-start.1
  138.3 6.4 %collective-permute-start.1 = (f32[640,128]{1,0:T(8,128)S(1)}, f32[640,128]{1,0:T(8,128)S(1)}, u32[]{:S(2)}, u32[]{:S(2)}) collective-permute-start(f32[640,128]{1,0:T(8,128)S(1)} %bitcast.17), channel_id=1, source_target_pairs={{0,1},{1,0},{2,3},{3,2},{4,5},{5,4},{6,7},{7,6},{8,9},{9,8},{10,11... | collective-permute-start | bytes 983048 | tf_op jit(solution)/shard_map/ppermute | solution.py:343
  175.9 5.6 %collective-permute-start.2 = (f32[1024,128]{1,0:T(8,128)S(1)}, f32[1024,128]{1,0:T(8,128)S(1)}, u32[]{:S(2)}, u32[]{:S(2)}) collective-permute-start(f32[1024,128]{1,0:T(8,128)S(1)} %bitcast.15), channel_id=1, source_target_pairs={{0,1},{1,0},{2,3},{3,2},{4,5},{5,4},{6,7},{7,6},{8,9},{9,8},{10,11... | collective-permute-start | bytes 1572872 | tf_op jit(solution)/shard_map/ppermute | solution.py:356

commit v15 on v13

--- a/solution.py
+++ b/solution.py
@@ -15,10 +15,10 @@
 CHIPS = ("gh", "gl", "gu", "gv", "gk", "gw", "gp")
 ORDER = CHIPS + ("gc",)
 NEAR = ("gl", "gk", "gp")
-CLOSE = ("gw", "gl", "gp", "gc")
+CLOSE = ("gl", "gw", "gp", "gc")
 FAR = ("gh", "gu", "gv", "gk")
 BLOCK = ("gw", "gk", "gp", "gl")
-BEYOND = ("gv", "gu", "gh")
+BEYOND = ("gu", "gh", "gv")
 
 highest = lax.Precision.HIGHEST
 NN = ((1,), (0,))

time: 209 us -> 210 us (level)
  no operation moved by 1% of the time
where the time goes in v15:
time: 210 us; the launch traced here: 207 us
  blocking collectives  179 us (85%)
  Pallas kernels  13.2 us (6%)
  starting transfers between devices  11 us (5%)
  waiting for transfers between devices  2.75 us (1%)
    all_to_all x10, blocking collectives, swap(): return lax.all_to_all(pieces, axes, split_axis=0, concat_axis=0, tiled=True)  179 us
    pallas_call x8, Pallas kernels, call(): pl.pallas_call(kernel, out_shape=out_shape, in_specs=[hbm] * in_hbm + [vm...  13.2 us
    ppermute x2, starting transfers between devices, shards(): other = lax.ppermute(own, 'gc', exchange)  8.61 us
  transfers between devices with their start and end apart: 3, of which 2 were waited for; matrix products, arithmetic and copies ran while one was open for 0% of the time, Pallas kernels for 0%

profile of v15, /device:TPU:1, one launch (start us, length us, event | category | flops | bytes accessed | tf_op | source)
XLA Modules:
  0.0 207.2 jit_solution(12514884299762103369)
XLA Ops:
  0.0 1.6 shard_map.55
  1.6 54.3 %all_to_all.50 = f32[512,4,128]{2,1,0:T(4,128)S(1)} all-to-all(f32[512,4,128]{2,1,0:T(4,128)S(1)} %bitcast.19), channel_id=1, replica_groups=mesh['gu'=2,'gv'=4,'gk'=2,'gh'=2,'gl'=2,'gw'=2,'gp'=2,'gc'=2] {'gh','gl'..., dimensions={0} | all-to-all | bytes 2097152 | tf_op jit(solution)/shard_map/all_to_all | solution.py:270
  55.9 0.6 shard_map.56
  56.4 9.9 %all_to_all.51 = f32[16,8,128]{2,1,0:T(8,128)S(1)} all-to-all(f32[16,8,128]{2,1,0:T(8,128)S(1)} %bitcast.21), channel_id=1, replica_groups=mesh['gu'=2,'gv'=4,'gk'=2,'gh'=2,'gl'=2,'gw'=2,'gp'=2,'gc'=2] {'gl','gw'..., dimensions={0} | all-to-all | bytes 131072 | tf_op jit(solution)/shard_map/all_to_all | solution.py:270
  66.3 16.9 %all_to_all.52 = f32[32,8,128]{2,1,0:T(8,128)S(1)} all-to-all(f32[32,8,128]{2,1,0:T(8,128)S(1)} %broadcast_in_dim.12), channel_id=1, replica_groups=mesh['gu'=2,'gv'=4,'gk'=2,'gh'=2,'gl'=2,'gw'=2,'gp'=2,'gc'=2] {'gh','gu'..., dimensions={0} | all-to-all | bytes 262144 | tf_op jit(solution)/shard_map/all_to_all | solution.py:270
  83.2 10.5 %all_to_all.53 = f32[16,8,128]{2,1,0:T(8,128)S(1)} all-to-all(f32[16,8,128]{2,1,0:T(8,128)S(1)} %broadcast_in_dim.13), channel_id=1, replica_groups=mesh['gu'=2,'gv'=4,'gk'=2,'gh'=2,'gl'=2,'gw'=2,'gp'=2,'gc'=2] {'gl','gw'..., dimensions={0} | all-to-all | bytes 131072 | tf_op jit(solution)/shard_map/all_to_all | solution.py:270
  93.7 0.0 copy-start
  93.7 3.1 %shard_map.57 = (f32[128,512]{1,0:T(8,128)S(1)}, f32[640,128]{1,0:T(8,128)S(1)}, f32[640,128]{1,0:T(8,128)S(1)}) custom-call(f32[128,128]{1,0:T(8,128)S(1)} %bitcast.20, f32[32,128]{1,0:T(8,128)S(1)} %get-tuple-element.19.start_ref, f32[2048,128]{1,0:T(8,128)S(1)} %bitcast.13), custom_call_target="tpu_custom_call" | custom-call | tf_op jit(solution)/shard_map/pallas_call | solution.py:255
  96.8 2.3 %collective-permute-start = (f32[640,128]{1,0:T(8,128)S(1)}, f32[640,128]{1,0:T(8,128)S(1)}, u32[]{:S(2)}, u32[]{:S(2)}) collective-permute-start(f32[640,128]{1,0:T(8,128)S(1)} %get-tuple-element.25), channel_id=1, source_target_pairs={{0,1},{1,0},{2,3},{3,2},{4,5},{5,4},{6,7},{7,6},{8,9},{9,8},{10,11... | collective-permute-start | bytes 983048 | tf_op jit(solution)/shard_map/ppermute | solution.py:321
  99.2 0.0 copy-start.1
  99.2 0.0 copy-done
  99.2 0.6 copy-done.1
  99.8 0.8 shard_map.58.start_ref
  100.6 0.0 collective-permute-done
  100.7 9.6 %all_to_all.54 = f32[16,40,128]{2,1,0:T(8,128)S(1)} all-to-all(f32[16,40,128]{2,1,0:T(8,128)S(1)} %bitcast.23), channel_id=1, replica_groups=mesh['gu'=2,'gv'=4,'gk'=2,'gh'=2,'gl'=2,'gw'=2,'gp'=2,'gc'=2] {'gw','gk'..., dimensions={0} | all-to-all | bytes 655360 | tf_op jit(solution)/shard_map/all_to_all | solution.py:270
  110.4 15.0 %all_to_all.55 = f32[16,40,128]{2,1,0:T(8,128)S(1)} all-to-all(f32[16,40,128]{2,1,0:T(8,128)S(1)} %broadcast_in_dim.14), channel_id=1, replica_groups=mesh['gu'=2,'gv'=4,'gk'=2,'gh'=2,'gl'=2,'gw'=2,'gp'=2,'gc'=2] {'gu','gh'..., dimensions={0} | all-to-all | bytes 655360 | tf_op jit(solution)/shard_map/all_to_all | solution.py:270
  125.4 13.0 %all_to_all.56 = f32[16,40,128]{2,1,0:T(8,128)S(1)} all-to-all(f32[16,40,128]{2,1,0:T(8,128)S(1)} %broadcast_in_dim.15), channel_id=1, replica_groups=mesh['gu'=2,'gv'=4,'gk'=2,'gh'=2,'gl'=2,'gw'=2,'gp'=2,'gc'=2] {'gw','gk'..., dimensions={0} | all-to-all | bytes 655360 | tf_op jit(solution)/shard_map/all_to_all | solution.py:270
  138.4 4.6 %collective-permute-start.1 = (f32[640,128]{1,0:T(8,128)S(1)}, f32[640,128]{1,0:T(8,128)S(1)}, u32[]{:S(2)}, u32[]{:S(2)}) collective-permute-start(f32[640,128]{1,0:T(8,128)S(1)} %bitcast.17), channel_id=1, source_target_pairs={{0,1},{1,0},{2,3},{3,2},{4,5},{5,4},{6,7},{7,6},{8,9},{9,8},{10,11... | collective-permute-start | bytes 983048 | tf_op jit(solution)/shard_map/ppermute | solution.py:343
  143.0 1.2 collective-permute-done.1.other_ref
  144.3 3.0 %shard_map.59 = f32[2,2,8,2,2,8,128]{6,5,4,3,2,1,0:T(8,128)S(1)} custom-call(f32[640,128]{1,0:T(8,128)S(1)} %bitcast.18, f32[640,128]{1,0:T(8,128)S(1)} %collective-permute-done.1.other_ref, f32[32,512]{1,0:T(8,128)S(1)} %get-tuple-element.26.start_ref, f32[128,512]{1,0:T(8,128)S(1)} %get-tuple-element.27.merged_ref), custom_call_target="tpu_custom_call" | custom-call | tf_op jit(solution)/shard_map/pallas_call | solution.py:255
  147.3 29.4 %all_to_all.57 = f32[256,4,128]{2,1,0:T(4,128)S(1)} all-to-all(f32[256,4,128]{2,1,0:T(4,128)S(1)} %bitcast.14), channel_id=1, replica_groups=mesh['gu'=2,'gv'=4,'gk'=2,'gh'=2,'gl'=2,'gw'=2,'gp'=2,'gc'=2] {'gh','gl'..., dimensions={0} | all-to-all | bytes 1048576 | tf_op jit(solution)/shard_map/all_to_all | solution.py:270
  176.6 4.0 %collective-permute-start.2 = (f32[1024,128]{1,0:T(8,128)S(1)}, f32[1024,128]{1,0:T(8,128)S(1)}, u32[]{:S(2)}, u32[]{:S(2)}) collective-permute-start(f32[1024,128]{1,0:T(8,128)S(1)} %bitcast.15), channel_id=1, source_target_pairs={{0,1},{1,0},{2,3},{3,2},{4,5},{5,4},{6,7},{7,6},{8,9},{9,8},{10,11... | collective-permute-start | bytes 1572872 | tf_op jit(solution)/shard_map/ppermute | solution.py:355
  180.7 1.5 collective-permute-done.2.other_ref
  182.2 0.7 shard_map.60
  182.9 11.4 %all_to_all.58.parts_ref = f32[8,32,512]{2,1,0:T(8,128)S(1)} all-to-all(f32[8,32,512]{2,1,0:T(8,128)S(1)} %get-tuple-element.28), channel_id=1, replica_groups=mesh['gu'=2,'gv'=4,'gk'=2,'gh'=2,'gl'=2,'gw'=2,'gp'=2,'gc'=2] {'gl','gk'..., dimensions={0} | all-to-all | bytes 1048576 | tf_op jit(solution)/shard_map/all_to_all | solution.py:270
  194.2 1.6 shard_map.61
  195.9 9.4 %all_to_all.59.parts_ref = f32[8,32,512]{2,1,0:T(8,128)S(1)} all-to-all(f32[8,32,512]{2,1,0:T(8,128)S(1)} %shard_map.61), channel_id=1, replica_groups=mesh['gu'=2,'gv'=4,'gk'=2,'gh'=2,'gl'=2,'gw'=2,'gp'=2,'gc'=2] {'gl','gk'..., dimensions={0} | all-to-all | bytes 1048576 | tf_op jit(solution)/shard_map/all_to_all | solution.py:270
  205.3 1.9 shard_map.62
  (9 shorter events, 0.2 us)
Async XLA Ops:
  93.7 5.4 %copy-start = (f32[512,32]{0,1:T(8,128)S(1)}, f32[512,32]{0,1:T(8,128)}, u32[]{:S(2)}) copy-start(f32[512,32]{0,1:T(8,128)} %param.9) | copy-start | bytes 196612
  96.8 3.8 %collective-permute-start = (f32[640,128]{1,0:T(8,128)S(1)}, f32[640,128]{1,0:T(8,128)S(1)}, u32[]{:S(2)}, u32[]{:S(2)}) collective-permute-start(f32[640,128]{1,0:T(8,128)S(1)} %get-tuple-element.25), channel_id=1, source_target_pairs={{0,1},{1,0},{2,3},{3,2},{4,5},{5,4},{6,7},{7,6},{8,9},{9,8},{10,11... | collective-permute-start | bytes 983048 | tf_op jit(solution)/shard_map/ppermute | solution.py:321
  99.2 0.7 copy-start.1
  138.4 5.8 %collective-permute-start.1 = (f32[640,128]{1,0:T(8,128)S(1)}, f32[640,128]{1,0:T(8,128)S(1)}, u32[]{:S(2)}, u32[]{:S(2)}) collective-permute-start(f32[640,128]{1,0:T(8,128)S(1)} %bitcast.17), channel_id=1, source_target_pairs={{0,1},{1,0},{2,3},{3,2},{4,5},{5,4},{6,7},{7,6},{8,9},{9,8},{10,11... | collective-permute-start | bytes 983048 | tf_op jit(solution)/shard_map/ppermute | solution.py:343
  176.6 5.6 %collective-permute-start.2 = (f32[1024,128]{1,0:T(8,128)S(1)}, f32[1024,128]{1,0:T(8,128)S(1)}, u32[]{:S(2)}, u32[]{:S(2)}) collective-permute-start(f32[1024,128]{1,0:T(8,128)S(1)} %bitcast.15), channel_id=1, source_target_pairs={{0,1},{1,0},{2,3},{3,2},{4,5},{5,4},{6,7},{7,6},{8,9},{9,8},{10,11... | collective-permute-start | bytes 1572872 | tf_op jit(solution)/shard_map/ppermute | solution.py:355
